TPU v7x, 256 devices: a whole 4x4x8 slice. The times are simulated.
256 devices in a mesh: ctx: 8 (over x_hi, y), db: 32 (over z, x_lo, core).
Axes of the slice: x: 4 (x_hi: 2, x_lo: 2; x = x_hi * 2 + x_lo), y: 4, z: 8, core: 2. Of those that a mesh axis runs over, the one named last changes fastest.
Arguments:
- q_self: bfloat16 [8192, 4096], P('ctx', 'db'), may hold values from -144 to 144
- k_self: bfloat16 [8192, 4096], P('ctx', 'db'), may hold values from -6 to 6
- v_self: bfloat16 [8192, 4096], P('ctx', 'db'), may hold values from -8 to 8
- db_states: bfloat16 [512, 128, 896], P('db'), may hold values from -16 to 16
- nb_shard: int32 [128, 2], P('ctx'), may hold values from 0 to 31, all different within a row; in each aligned block of 16 rows (0 to 15, 16 to 31, ...) at most 2 rows name the same one
- nb_row: int32 [128, 2], P('ctx'), may hold values from 0 to 15
- wk_x: bfloat16 [896, 4096], P(None, 'db'), may hold values from -2 to 2
- wv_x: bfloat16 [896, 4096], P(None, 'db'), may hold values from -0.1875 to 0.1875
- wq_x: bfloat16 [4096, 4096], P(None, 'db'), may hold values from -2 to 2
Outputs:
- self_out: bfloat16 [8192, 4096], P('ctx', 'db')
- cross_out: bfloat16 [8192, 4096], P('ctx', 'db')
Inputs may be any that keep to these rules, and one draw needn't show every extreme that they name: `nb_shard`: among the groups of one sequence block (16 consecutive groups) no shard is named more than 2 times, a bound that some block reaches; the 2 neighbours of a group lie on different shards.
All inputs are finite; a program needn't handle non-finite values.
Results may differ from a plain program's by a relative error of at most 0.013.
The roundings to bfloat16 on the way count: a program that leaves them out, or rounds other values in their place, can miss the bound.
Values may be sent and summed in bfloat16 or wider, within the bound.
No kernel may reach another device: no remote copies, remote signals or barrier semaphores. Data moves between devices by JAX's collectives and lax.ppermute only.
A program may use at most 128 MiB of HBM per device.

v0:
```python
import math

import jax
import jax.numpy as jnp
from jax import lax
from jax.sharding import PartitionSpec as P

HD = 128


def shifted(value, axis, steps):
    count = lax.axis_size(axis)
    initial, last = (max(0, -steps), min(count, count - steps))
    return lax.ppermute(value, axis, [(source, source + steps) for source in range(initial, last)])


def local(q_self, k_self, v_self, db_states, nb_shard, nb_row, wk_x, wv_x, wq_x):
    tok_rows = q_self.shape[0]
    head_dim = HD
    head_count = q_self.shape[1] // head_dim
    scaling = 1.0 / math.sqrt(head_dim)
    cycle_size = lax.axis_size("ctx")
    db_size = lax.axis_size("db")
    ctx_index = lax.axis_index("ctx")
    db_index = lax.axis_index("db")
    query_heads = q_self.reshape(tok_rows, head_count, head_dim)
    query_pos = ctx_index * tok_rows + jnp.arange(tok_rows)
    initial = (
        jnp.full((head_count, tok_rows, 1), -1e30, jnp.float32),
        jnp.zeros((head_count, tok_rows, 1), jnp.float32),
        jnp.zeros((head_count, tok_rows, head_dim), jnp.float32),
    )
    state_now = initial
    stacked = jnp.stack([k_self, v_self])
    for turn_index in range(cycle_size):
        source = ctx_index - turn_index
        key_block = stacked[0]
        attend_row_max, attend_denominator, attend_numerator = state_now
        row_count = key_block.shape[0]
        key_heads = key_block.reshape(row_count, head_count, head_dim)
        value_heads = stacked[1].reshape(row_count, head_count, head_dim)
        attend_scores = (
            jnp.einsum("qhd,khd->hqk", query_heads, key_heads, preferred_element_type=jnp.float32)
            * scaling
        )
        key_pos = source * tok_rows + jnp.arange(row_count)
        allowed = ((query_pos[:, None] >= key_pos[None, :]) & (key_pos[None, :] >= 0))[None]
        max_next = jnp.maximum(
            attend_row_max, jnp.max(jnp.where(allowed, attend_scores, -1e30), axis=2, keepdims=True)
        )
        attend_weights = jnp.where(allowed, jnp.exp(attend_scores - max_next), 0.0)
        factor = jnp.exp(attend_row_max - max_next)
        attend_denominator = attend_denominator * factor + jnp.sum(
            attend_weights, axis=2, keepdims=True
        )
        attend_numerator = attend_numerator * factor + jnp.einsum(
            "hqk,khd->hqd",
            attend_weights.astype(jnp.bfloat16),
            value_heads,
            preferred_element_type=jnp.float32,
        )
        state_now = (max_next, attend_denominator, attend_numerator)
        if turn_index + 1 < cycle_size:
            stacked = shifted(stacked, "ctx", 1)
    row_max, denominator, numerator = state_now
    self_out = (
        (numerator / denominator)
        .transpose(1, 0, 2)
        .reshape(tok_rows, head_count * head_dim)
        .astype(jnp.bfloat16)
    )
    cross_query = jnp.dot(
        lax.all_gather(self_out, "db", axis=1, tiled=True), wq_x, preferred_element_type=jnp.float32
    ).astype(jnp.bfloat16)
    group_count = nb_shard.shape[0]
    per_group = nb_shard.shape[1]
    requests = group_count * per_group
    capacity = 2 * ((requests + db_size - 1) // db_size)
    shard_flat = nb_shard.reshape(requests)
    row_flat = nb_row.reshape(requests)
    same_shard = shard_flat[:, None] == shard_flat[None, :]
    earlier = jnp.arange(requests)[None, :] < jnp.arange(requests)[:, None]
    rank_within = jnp.sum((same_shard & earlier).astype(jnp.int32), axis=1)
    picked = (shard_flat[None, :] == db_index) & (
        rank_within[None, :] == jnp.arange(capacity)[:, None]
    )
    slot_rows = jnp.sum(jnp.where(picked, row_flat[None, :], 0), axis=1)
    slot_states = jnp.take(db_states, slot_rows, axis=0)
    state_len = db_states.shape[1]
    state_width = db_states.shape[2]
    slot_of = shard_flat * capacity + rank_within
    gathered = lax.all_gather(slot_states, "db", axis=0, tiled=True)
    requested = jnp.take(gathered, slot_of, axis=0)
    flat_states = requested.reshape(requests * state_len, state_width)
    nb_keys = (
        jnp.dot(flat_states, wk_x, preferred_element_type=jnp.float32)
        .astype(jnp.bfloat16)
        .reshape(requests, state_len, head_count, head_dim)
    )
    nb_values = (
        jnp.dot(flat_states, wv_x, preferred_element_type=jnp.float32)
        .astype(jnp.bfloat16)
        .reshape(requests, state_len, head_count, head_dim)
    )
    chosen = jnp.concatenate([nb_keys, nb_values], axis=3).reshape(
        group_count, per_group * state_len, head_count, 2 * head_dim
    )
    group_keys = chosen[..., :head_dim]
    group_values = chosen[..., head_dim:]
    group_len = tok_rows // group_count
    group_query = cross_query.reshape(group_count, group_len, head_count, head_dim)
    scores = (
        jnp.einsum("cqhd,ckhd->chqk", group_query, group_keys, preferred_element_type=jnp.float32)
        * scaling
    )
    cross_max = jnp.max(scores, axis=3, keepdims=True)
    weights = jnp.exp(scores - cross_max)
    cross_total = jnp.sum(weights, axis=3, keepdims=True)
    weighted = jnp.einsum(
        "chqk,ckhd->chqd",
        weights.astype(jnp.bfloat16),
        group_values,
        preferred_element_type=jnp.float32,
    )
    cross_out = (
        (weighted / cross_total)
        .transpose(0, 2, 1, 3)
        .reshape(tok_rows, head_count * head_dim)
        .astype(jnp.bfloat16)
    )
    return (self_out, cross_out)


def solution(mesh):
    return jax.shard_map(
        local,
        mesh=mesh,
        in_specs=(
            P("ctx", "db"),
            P("ctx", "db"),
            P("ctx", "db"),
            P("db", None, None),
            P("ctx", None),
            P("ctx", None),
            P(None, "db"),
            P(None, "db"),
            P(None, "db"),
        ),
        out_specs=(P("ctx", "db"), P("ctx", "db")),
        check_vma=False,
    )
```

profile of v0, /device:TPU:31, one launch (start us, length us, event | category | flops | bytes accessed | tf_op | source)
XLA Modules:
  0.0 366.4 jit_solution(519869210603963765)
XLA Ops:
  7.2 1.2 pad_maximum_fusion
  8.4 1.3 collective-permute-start
  9.7 13.4 %collective-permute-done = bf16[2,1024,128]{2,1,0:T(8,128)(2,1)S(1)} collective-permute-done((bf16[2,1024,128]{2,1,0:T(8,128)(2,1)S(1)}, bf16[2,1024,128]{2,1,0:T(8,128)(2,1)S(1)}, u32[]{:S(2)}, u32[]{:S(2)}) %collective-permute-start) | collective-permute-done | bytes 524320 | tf_op jit(solution)/shard_map/ppermute | solution.py:14
  23.1 1.3 collective-permute-start.1
  24.5 12.4 %collective-permute-done.1 = bf16[2,1024,128]{2,1,0:T(8,128)(2,1)S(1)} collective-permute-done((bf16[2,1024,128]{2,1,0:T(8,128)(2,1)S(1)}, bf16[2,1024,128]{2,1,0:T(8,128)(2,1)S(1)}, u32[]{:S(2)}, u32[]{:S(2)}) %collective-permute-start.1) | collective-permute-done | bytes 524320 | tf_op jit(solution)/shard_map/ppermute | solution.py:14
  36.9 1.3 collective-permute-start.2
  38.2 1.7 fusion.140
  39.9 9.8 %collective-permute-done.2 = bf16[2,1024,128]{2,1,0:T(8,128)(2,1)S(1)} collective-permute-done((bf16[2,1024,128]{2,1,0:T(8,128)(2,1)S(1)}, bf16[2,1024,128]{2,1,0:T(8,128)(2,1)S(1)}, u32[]{:S(2)}, u32[]{:S(2)}) %collective-permute-start.2) | collective-permute-done | bytes 524320 | tf_op jit(solution)/shard_map/ppermute | solution.py:14
  49.7 1.3 collective-permute-start.3
  51.0 0.7 fusion.115
  51.7 11.6 %collective-permute-done.3 = bf16[2,1024,128]{2,1,0:T(8,128)(2,1)S(1)} collective-permute-done((bf16[2,1024,128]{2,1,0:T(8,128)(2,1)S(1)}, bf16[2,1024,128]{2,1,0:T(8,128)(2,1)S(1)}, u32[]{:S(2)}, u32[]{:S(2)}) %collective-permute-start.3) | collective-permute-done | bytes 524320 | tf_op jit(solution)/shard_map/ppermute | solution.py:14
  63.3 1.3 collective-permute-start.4
  64.6 3.4 fusion.15
  68.0 9.9 %collective-permute-done.4 = bf16[2,1024,128]{2,1,0:T(8,128)(2,1)S(1)} collective-permute-done((bf16[2,1024,128]{2,1,0:T(8,128)(2,1)S(1)}, bf16[2,1024,128]{2,1,0:T(8,128)(2,1)S(1)}, u32[]{:S(2)}, u32[]{:S(2)}) %collective-permute-start.4) | collective-permute-done | bytes 524320 | tf_op jit(solution)/shard_map/ppermute | solution.py:14
  77.9 1.3 collective-permute-start.5
  79.2 0.7 fusion.112
  80.0 11.7 %collective-permute-done.5 = bf16[2,1024,128]{2,1,0:T(8,128)(2,1)S(1)} collective-permute-done((bf16[2,1024,128]{2,1,0:T(8,128)(2,1)S(1)}, bf16[2,1024,128]{2,1,0:T(8,128)(2,1)S(1)}, u32[]{:S(2)}, u32[]{:S(2)}) %collective-permute-start.5) | collective-permute-done | bytes 524320 | tf_op jit(solution)/shard_map/ppermute | solution.py:14
  91.6 1.5 collective-permute-start.6
  93.1 0.7 fusion.111
  93.8 0.7 fusion.110
  94.5 9.8 %collective-permute-done.6 = bf16[2,1024,128]{2,1,0:T(8,128)(2,1)S(1)} collective-permute-done((bf16[2,1024,128]{2,1,0:T(8,128)(2,1)S(1)}, bf16[2,1024,128]{2,1,0:T(8,128)(2,1)S(1)}, u32[]{:S(2)}, u32[]{:S(2)}) %collective-permute-start.6) | collective-permute-done | bytes 524320 | tf_op jit(solution)/shard_map/ppermute | solution.py:14
  104.3 0.7 fusion.109
  105.0 7.2 %fusion.21 = (f32[1024]{0:T(1024)S(1)}, f32[1024]{0:T(1024)S(1)}, f32[1024]{0:T(1024)S(1)}, f32[1024]{0:T(1024)S(1)}, f32[1024]{0:T(1024)S(1)}, /*index=5*/f32[1024]{0:T(1024)S(1)}, f32[1024,1024]{1,0:T(8,128)S(1)}) fusion(f32[1024,1024]{0,1:T(8,128)S(1)} %fusion.140, f32[1024]{0:T(1024)S(1)} %broadcast_maximum_fusion, s32[1024]{0:T(1024)S(1)} %get-tuple-element.41, ...), kind=kOutput, calls=%fused_computation.50 | convolution fusion | flops 300935168 | bytes 25753600 | tf_op jit(solution)/shard_map/qhd,khd->hqk/dot_general | solution.py:43
  112.3 4.8 %fusion.31 = (f32[1024]{0:T(1024)S(1)}, f32[1024]{0:T(1024)S(1)}, f32[1024]{0:T(1024)S(1)}) fusion(f32[1024,1024]{1,0:T(8,128)S(1)} %fusion.111, f32[1024]{0:T(1024)S(1)} %get-tuple-element.28, s32[1024]{0:T(1024)S(1)} %get-tuple-element.41, s32[1024]{0:T(1024)S(1)} %get-tuple-element.46, pred[1024]{0:T(1024)(128)(4,1)S(1)} %get-tuple-element.50, ...), kind=kLoop, calls=%fused_computation.60 | loop fusion | flops 18871296 | bytes 12626944 | tf_op jit(solution)/shard_map/reduce_sum | solution.py:53
  117.0 7.1 %fusion.23 = (f32[1024]{0:T(1024)S(1)}, f32[1024]{0:T(1024)S(1)}, f32[1024]{0:T(1024)S(1)}, f32[1024]{0:T(1024)S(1)}) fusion(f32[1024,1024]{1,0:T(8,128)S(1)} %fusion.115, f32[1024]{0:T(1024)S(1)} %get-tuple-element.32, s32[1024]{0:T(1024)S(1)} %get-tuple-element.41, s32[1024]{0:T(1024)S(1)} %iota_add_fusion.6, pred[1024]{0:T(1024)(128)(4,1)S(1)} %get-tuple-element.43, ...), kind=kLoop, calls=%fused_computation.52 | loop fusion | flops 25161728 | bytes 16834560 | tf_op jit(solution)/shard_map/reduce_sum | solution.py:53
  124.2 1.8 fusion.77
  126.0 1.8 fusion.95
  127.8 1.8 fusion.92
  129.5 1.8 fusion.89
  131.3 1.8 fusion.86
  133.1 1.8 fusion.83
  134.9 1.8 fusion.80
  136.7 2.6 fusion.102
  139.5 0.1 reshape.785
  139.8 0.2 convert_reduce_fusion
  140.0 0.1 fusion.117
  140.2 2.7 gather_fusion
  142.8 0.9 broadcast_select_fusion
  144.0 106.1 %all-gather.3.cloned.1.call-done = bf16[1024,4096]{1,0:T(8,128)(2,1)} async-done(((bf16[1024,128]{1,0:T(8,128)(2,1)}), bf16[1024,4096]{1,0:T(8,128)(2,1)}) %all-gather.3.cloned.1.call-update) | async-done | bytes 8388624 | tf_op jit(solution)/shard_map/all_gather | solution.py:73
  250.2 5.7 %convolution_convert_fusion.2 = bf16[1024,128]{1,0:T(8,128)(2,1)S(1)} fusion(bf16[1024,4096]{1,0:T(8,128)(2,1)} %all-gather.3.cloned.1.call-done, bf16[4096,128]{1,0:T(8,128)(2,1)S(1)} %copy-done), kind=kOutput, calls=%fused_computation.92 | convolution fusion | flops 1073872896 | bytes 9699328 | tf_op jit(solution)/shard_map/dot_general | solution.py:72
  255.9 83.0 %all-gather.5.cloned.1.call-done = bf16[64,128,896]{2,1,0:T(8,128)(2,1)} async-done(((bf16[2,128,896]{2,1,0:T(8,128)(2,1)}), bf16[64,128,896]{2,1,0:T(8,128)(2,1)}) %all-gather.5.cloned.1.call-update) | async-done | bytes 14680080 | tf_op jit(solution)/shard_map/all_gather | solution.py:92
  338.9 9.5 %gather_fusion.1 = bf16[32,128,896]{2,1,0:T(8,128)(2,1)} fusion(bf16[64,128,896]{2,1,0:T(8,128)(2,1)} %all-gather.5.cloned.1.call-done, s32[1024]{0:T(1024)S(1)} %pad_clamp_fusion), kind=kCustom, calls=%fused_computation.1 | custom fusion | bytes 14680192 | tf_op jit(solution)/shard_map/jit(_take)/gather | solution.py:93
  348.4 4.3 %bitcast_select_fusion = bf16[4096,896]{1,0:T(8,128)(2,1)S(1)} fusion(bf16[32,128,896]{2,1,0:T(8,128)(2,1)} %gather_fusion.1, pred[4096]{0:T(1024)(128)(4,1)S(1)} %broadcast_bitcast_fusion), kind=kLoop, calls=%fused_computation.2 | loop fusion | flops 3670016 | bytes 14684160 | tf_op jit(solution)/shard_map/jit(_take)/select_n | solution.py:93
  352.7 2.1 convolution_convert_fusion.1
  354.9 2.1 convolution_convert_fusion
  357.0 0.6 fusion.139
  357.6 0.4 fusion.105
  358.0 1.1 fusion.98
  (43 shorter events, 0.8 us)
Async XLA Ops:
  7.2 243.0 %copy-start = (bf16[4096,128]{1,0:T(8,128)(2,1)S(1)}, bf16[4096,128]{1,0:T(8,128)(2,1)}, u32[]{:S(2)}) copy-start(bf16[4096,128]{1,0:T(8,128)(2,1)} %param.17) | copy-start | bytes 3145732
  7.2 43.8 %copy-start.1 = (bf16[1024,128]{1,0:T(8,128)(2,1)S(1)}, bf16[1024,128]{1,0:T(8,128)(2,1)}, u32[]{:S(2)}) copy-start(bf16[1024,128]{1,0:T(8,128)(2,1)} %param.9) | copy-start | bytes 786436
  7.2 243.0 %all-gather.3.cloned.1.call-start = ((), (), s32[]{:S(2)}) async-start(), calls=%async_computation | async-start | bytes 8650752 | tf_op jit(solution)/shard_map/all_gather | solution.py:73
  8.4 14.7 %collective-permute-start = (bf16[2,1024,128]{2,1,0:T(8,128)(2,1)S(1)}, bf16[2,1024,128]{2,1,0:T(8,128)(2,1)S(1)}, u32[]{:S(2)}, u32[]{:S(2)}) collective-permute-start(bf16[2,1024,128]{2,1,0:T(8,128)(2,1)S(1)} %pad_maximum_fusion), channel_id=1, source_target_pairs={{0,32},{32,64},{64,96},{96,128},{128,160},{160,192},{192,224},{1,3... | collective-permute-start | bytes 1572872 | tf_op jit(solution)/shard_map/ppermute | solution.py:14
  23.1 13.8 %collective-permute-start.1 = (bf16[2,1024,128]{2,1,0:T(8,128)(2,1)S(1)}, bf16[2,1024,128]{2,1,0:T(8,128)(2,1)S(1)}, u32[]{:S(2)}, u32[]{:S(2)}) collective-permute-start(bf16[2,1024,128]{2,1,0:T(8,128)(2,1)S(1)} %collective-permute-done), channel_id=1, source_target_pairs={{0,32},{32,64},{64,96},{96,128},{128,160},{160,192},{192,224},{1,3... | collective-permute-start | bytes 1572872 | tf_op jit(solution)/shard_map/ppermute | solution.py:14
  36.9 12.8 %collective-permute-start.2 = (bf16[2,1024,128]{2,1,0:T(8,128)(2,1)S(1)}, bf16[2,1024,128]{2,1,0:T(8,128)(2,1)S(1)}, u32[]{:S(2)}, u32[]{:S(2)}) collective-permute-start(bf16[2,1024,128]{2,1,0:T(8,128)(2,1)S(1)} %collective-permute-done.1), channel_id=1, source_target_pairs={{0,32},{32,64},{64,96},{96,128},{128,160},{160,192},{192,224},{1,3... | collective-permute-start | bytes 1572872 | tf_op jit(solution)/shard_map/ppermute | solution.py:14
  49.7 13.6 %collective-permute-start.3 = (bf16[2,1024,128]{2,1,0:T(8,128)(2,1)S(1)}, bf16[2,1024,128]{2,1,0:T(8,128)(2,1)S(1)}, u32[]{:S(2)}, u32[]{:S(2)}) collective-permute-start(bf16[2,1024,128]{2,1,0:T(8,128)(2,1)S(1)} %collective-permute-done.2), channel_id=1, source_target_pairs={{0,32},{32,64},{64,96},{96,128},{128,160},{160,192},{192,224},{1,3... | collective-permute-start | bytes 1572872 | tf_op jit(solution)/shard_map/ppermute | solution.py:14
  63.3 14.6 %collective-permute-start.4 = (bf16[2,1024,128]{2,1,0:T(8,128)(2,1)S(1)}, bf16[2,1024,128]{2,1,0:T(8,128)(2,1)S(1)}, u32[]{:S(2)}, u32[]{:S(2)}) collective-permute-start(bf16[2,1024,128]{2,1,0:T(8,128)(2,1)S(1)} %collective-permute-done.3), channel_id=1, source_target_pairs={{0,32},{32,64},{64,96},{96,128},{128,160},{160,192},{192,224},{1,3... | collective-permute-start | bytes 1572872 | tf_op jit(solution)/shard_map/ppermute | solution.py:14
  77.9 13.7 %collective-permute-start.5 = (bf16[2,1024,128]{2,1,0:T(8,128)(2,1)S(1)}, bf16[2,1024,128]{2,1,0:T(8,128)(2,1)S(1)}, u32[]{:S(2)}, u32[]{:S(2)}) collective-permute-start(bf16[2,1024,128]{2,1,0:T(8,128)(2,1)S(1)} %collective-permute-done.4), channel_id=1, source_target_pairs={{0,32},{32,64},{64,96},{96,128},{128,160},{160,192},{192,224},{1,3... | collective-permute-start | bytes 1572872 | tf_op jit(solution)/shard_map/ppermute | solution.py:14
  91.6 12.7 %collective-permute-start.6 = (bf16[2,1024,128]{2,1,0:T(8,128)(2,1)S(1)}, bf16[2,1024,128]{2,1,0:T(8,128)(2,1)S(1)}, u32[]{:S(2)}, u32[]{:S(2)}) collective-permute-start(bf16[2,1024,128]{2,1,0:T(8,128)(2,1)S(1)} %collective-permute-done.5), channel_id=1, source_target_pairs={{0,32},{32,64},{64,96},{96,128},{128,160},{160,192},{192,224},{1,3... | collective-permute-start | bytes 1572872 | tf_op jit(solution)/shard_map/ppermute | solution.py:14
  117.0 7.2 %copy-start.2 = (bf16[1024,128]{1,0:T(8,128)(2,1)S(1)}, bf16[1024,128]{1,0:T(8,128)(2,1)}, u32[]{:S(2)}) copy-start(bf16[1024,128]{1,0:T(8,128)(2,1)} %param.11) | copy-start | bytes 786436
  136.7 2.8 copy-start.5
  136.7 2.9 copy-start.6
  139.4 199.5 %all-gather.5.cloned.1.call-start = ((), (), s32[]{:S(2)}) async-start(), calls=%async_computation.1 | async-start | bytes 15138816 | tf_op jit(solution)/shard_map/all_gather | solution.py:92
  348.4 4.3 %copy-start.3 = (bf16[896,128]{1,0:T(8,128)(2,1)S(1)}, bf16[896,128]{1,0:T(8,128)(2,1)}, u32[]{:S(2)}) copy-start(bf16[896,128]{1,0:T(8,128)(2,1)} %param.15) | copy-start | bytes 688132
  352.7 2.2 copy-start.4
Sparse Core Ops, SparseCore 0:
  139.5 110.5 all-gather.2
  252.0 86.8 all-gather.4
where the time goes:
time: 373 us; the launch traced here: 366 us
  waiting for transfers between devices  268 us (72%)
  matrix products  42.6 us (11%)
  other arithmetic  19.1 us (5%)
  between operations  14.9 us (4%)
  local copies, waits for them, and re-layouts  12.8 us (3%)
  starting transfers between devices  9.23 us (2%)
    all_gather x1, waiting for transfers between devices, local(): lax.all_gather(self_out, 'db', axis=1, tiled=True)  106 us
    all_gather x1, waiting for transfers between devices, local(): gathered = lax.all_gather(slot_states, 'db', axis=0, tiled=True)  83 us
    ppermute x7, waiting for transfers between devices, shifted(): lax.ppermute(value, axis, [(source, source + steps) for source in range(i...  78.5 us
    dot_general x8, matrix products, local(): jnp.einsum('qhd,khd->hqk', query_heads, key_heads, preferred_element_type...  15.9 us
    dot_general x8, matrix products, local(): jnp.einsum('hqk,khd->hqd', attend_weights.astype(jnp.bfloat16), value_hea...  15.1 us
    reduce_sum x2, other arithmetic, local(): jnp.sum(attend_weights, axis=2, keepdims=True)  11.9 us
    gather x1, local copies, waits for them, and re-layouts, local(): requested = jnp.take(gathered, slot_of, axis=0)  9.5 us
    ppermute x7, starting transfers between devices, shifted(): lax.ppermute(value, axis, [(source, source + steps) for source in range(i...  9.15 us
  transfers between devices with their start and end apart: 9, of which 9 were waited for; matrix products, arithmetic and copies ran while one was open for 5% of the time, Pallas kernels for 0%

commit v1 on v0

--- a/solution.py
+++ b/solution.py
@@ -85,12 +85,12 @@
         rank_within[None, :] == jnp.arange(capacity)[:, None]
     )
     slot_rows = jnp.sum(jnp.where(picked, row_flat[None, :], 0), axis=1)
-    slot_states = jnp.take(db_states, slot_rows, axis=0)
+    slot_states = jnp.concatenate([lax.dynamic_slice_in_dim(db_states, slot_rows[i], 1, 0) for i in range(capacity)], axis=0)
     state_len = db_states.shape[1]
     state_width = db_states.shape[2]
     slot_of = shard_flat * capacity + rank_within
     gathered = lax.all_gather(slot_states, "db", axis=0, tiled=True)
-    requested = jnp.take(gathered, slot_of, axis=0)
+    requested = jnp.concatenate([lax.dynamic_slice_in_dim(gathered, slot_of[i], 1, 0) for i in range(requests)], axis=0)
     flat_states = requested.reshape(requests * state_len, state_width)
     nb_keys = (
         jnp.dot(flat_states, wk_x, preferred_element_type=jnp.float32)

time: 373 us -> 392 us (1.051)
  the two profiles are of different devices: /device:TPU:31 before, /device:TPU:1 now
where the time goes in v1:
time: 392 us; the launch traced here: 385 us
  waiting for transfers between devices  175 us (45%)
  between operations  79.3 us (20%)
  matrix products  42.6 us (11%)
  starting transfers between devices  38 us (10%)
  local copies, waits for them, and re-layouts  34.7 us (9%)
  other arithmetic  14.7 us (4%)
    all_gather x1, waiting for transfers between devices, local(): gathered = lax.all_gather(slot_states, 'db', axis=0, tiled=True)  82.8 us
    ppermute x7, waiting for transfers between devices, shifted(): lax.ppermute(value, axis, [(source, source + steps) for source in range(i...  47.3 us
    all_gather x1, waiting for transfers between devices, local(): lax.all_gather(self_out, 'db', axis=1, tiled=True)  45.3 us
    ppermute x7, starting transfers between devices, shifted(): lax.ppermute(value, axis, [(source, source + steps) for source in range(i...  37.9 us
    unnamed x47, local copies, waits for them, and re-layouts  30.3 us
    dot_general x8, matrix products, local(): jnp.einsum('qhd,khd->hqk', query_heads, key_heads, preferred_element_type...  15.8 us
    dot_general x8, matrix products, local(): jnp.einsum('hqk,khd->hqd', attend_weights.astype(jnp.bfloat16), value_hea...  15.1 us
    reduce_sum x2, other arithmetic, local(): jnp.sum(attend_weights, axis=2, keepdims=True)  11.9 us
  transfers between devices with their start and end apart: 9, of which 9 were waited for; matrix products, arithmetic and copies ran while one was open for 5% of the time, Pallas kernels for 0%

profile of v1, /device:TPU:1, one launch (start us, length us, event | category | flops | bytes accessed | tf_op | source)
XLA Modules:
  0.0 384.8 jit_solution(90592906332742439)
XLA Ops:
  7.2 1.2 pad_maximum_fusion
  8.4 4.1 %collective-permute-start = (bf16[2,1024,128]{2,1,0:T(8,128)(2,1)S(1)}, bf16[2,1024,128]{2,1,0:T(8,128)(2,1)S(1)}, u32[]{:S(2)}, u32[]{:S(2)}) collective-permute-start(bf16[2,1024,128]{2,1,0:T(8,128)(2,1)S(1)} %pad_maximum_fusion), channel_id=1, source_target_pairs={{0,32},{32,64},{64,96},{96,128},{128,160},{160,192},{192,224},{1,3... | collective-permute-start | bytes 1572872 | tf_op jit(solution)/shard_map/ppermute | solution.py:14
  12.5 10.5 %collective-permute-done = bf16[2,1024,128]{2,1,0:T(8,128)(2,1)S(1)} collective-permute-done((bf16[2,1024,128]{2,1,0:T(8,128)(2,1)S(1)}, bf16[2,1024,128]{2,1,0:T(8,128)(2,1)S(1)}, u32[]{:S(2)}, u32[]{:S(2)}) %collective-permute-start) | collective-permute-done | bytes 524320 | tf_op jit(solution)/shard_map/ppermute | solution.py:14
  23.0 4.1 %collective-permute-start.1 = (bf16[2,1024,128]{2,1,0:T(8,128)(2,1)S(1)}, bf16[2,1024,128]{2,1,0:T(8,128)(2,1)S(1)}, u32[]{:S(2)}, u32[]{:S(2)}) collective-permute-start(bf16[2,1024,128]{2,1,0:T(8,128)(2,1)S(1)} %collective-permute-done), channel_id=1, source_target_pairs={{0,32},{32,64},{64,96},{96,128},{128,160},{160,192},{192,224},{1,3... | collective-permute-start | bytes 1572872 | tf_op jit(solution)/shard_map/ppermute | solution.py:14
  27.2 9.6 %collective-permute-done.1 = bf16[2,1024,128]{2,1,0:T(8,128)(2,1)S(1)} collective-permute-done((bf16[2,1024,128]{2,1,0:T(8,128)(2,1)S(1)}, bf16[2,1024,128]{2,1,0:T(8,128)(2,1)S(1)}, u32[]{:S(2)}, u32[]{:S(2)}) %collective-permute-start.1) | collective-permute-done | bytes 524320 | tf_op jit(solution)/shard_map/ppermute | solution.py:14
  36.8 4.1 %collective-permute-start.2 = (bf16[2,1024,128]{2,1,0:T(8,128)(2,1)S(1)}, bf16[2,1024,128]{2,1,0:T(8,128)(2,1)S(1)}, u32[]{:S(2)}, u32[]{:S(2)}) collective-permute-start(bf16[2,1024,128]{2,1,0:T(8,128)(2,1)S(1)} %collective-permute-done.1), channel_id=1, source_target_pairs={{0,32},{32,64},{64,96},{96,128},{128,160},{160,192},{192,224},{1,3... | collective-permute-start | bytes 1572872 | tf_op jit(solution)/shard_map/ppermute | solution.py:14
  41.0 1.7 fusion.141
  42.7 6.9 %collective-permute-done.2 = bf16[2,1024,128]{2,1,0:T(8,128)(2,1)S(1)} collective-permute-done((bf16[2,1024,128]{2,1,0:T(8,128)(2,1)S(1)}, bf16[2,1024,128]{2,1,0:T(8,128)(2,1)S(1)}, u32[]{:S(2)}, u32[]{:S(2)}) %collective-permute-start.2) | collective-permute-done | bytes 524320 | tf_op jit(solution)/shard_map/ppermute | solution.py:14
  49.6 4.1 %collective-permute-start.3 = (bf16[2,1024,128]{2,1,0:T(8,128)(2,1)S(1)}, bf16[2,1024,128]{2,1,0:T(8,128)(2,1)S(1)}, u32[]{:S(2)}, u32[]{:S(2)}) collective-permute-start(bf16[2,1024,128]{2,1,0:T(8,128)(2,1)S(1)} %collective-permute-done.2), channel_id=1, source_target_pairs={{0,32},{32,64},{64,96},{96,128},{128,160},{160,192},{192,224},{1,3... | collective-permute-start | bytes 1572872 | tf_op jit(solution)/shard_map/ppermute | solution.py:14
  54.5 7.0 %collective-permute-done.3 = bf16[2,1024,128]{2,1,0:T(8,128)(2,1)S(1)} collective-permute-done((bf16[2,1024,128]{2,1,0:T(8,128)(2,1)S(1)}, bf16[2,1024,128]{2,1,0:T(8,128)(2,1)S(1)}, u32[]{:S(2)}, u32[]{:S(2)}) %collective-permute-start.3) | collective-permute-done | bytes 524320 | tf_op jit(solution)/shard_map/ppermute | solution.py:14
  61.5 5.8 %collective-permute-start.4 = (bf16[2,1024,128]{2,1,0:T(8,128)(2,1)S(1)}, bf16[2,1024,128]{2,1,0:T(8,128)(2,1)S(1)}, u32[]{:S(2)}, u32[]{:S(2)}) collective-permute-start(bf16[2,1024,128]{2,1,0:T(8,128)(2,1)S(1)} %collective-permute-done.3), channel_id=1, source_target_pairs={{0,32},{32,64},{64,96},{96,128},{128,160},{160,192},{192,224},{1,3... | collective-permute-start | bytes 1572872 | tf_op jit(solution)/shard_map/ppermute | solution.py:14
  67.4 3.4 fusion.15
  70.7 3.5 collective-permute-done.4
  74.2 7.7 %collective-permute-start.5 = (bf16[2,1024,128]{2,1,0:T(8,128)(2,1)S(1)}, bf16[2,1024,128]{2,1,0:T(8,128)(2,1)S(1)}, u32[]{:S(2)}, u32[]{:S(2)}) collective-permute-start(bf16[2,1024,128]{2,1,0:T(8,128)(2,1)S(1)} %collective-permute-done.4), channel_id=1, source_target_pairs={{0,32},{32,64},{64,96},{96,128},{128,160},{160,192},{192,224},{1,3... | collective-permute-start | bytes 1572872 | tf_op jit(solution)/shard_map/ppermute | solution.py:14
  82.7 5.3 %collective-permute-done.5 = bf16[2,1024,128]{2,1,0:T(8,128)(2,1)S(1)} collective-permute-done((bf16[2,1024,128]{2,1,0:T(8,128)(2,1)S(1)}, bf16[2,1024,128]{2,1,0:T(8,128)(2,1)S(1)}, u32[]{:S(2)}, u32[]{:S(2)}) %collective-permute-start.5) | collective-permute-done | bytes 524320 | tf_op jit(solution)/shard_map/ppermute | solution.py:14
  88.1 7.9 %collective-permute-start.6 = (bf16[2,1024,128]{2,1,0:T(8,128)(2,1)S(1)}, bf16[2,1024,128]{2,1,0:T(8,128)(2,1)S(1)}, u32[]{:S(2)}, u32[]{:S(2)}) collective-permute-start(bf16[2,1024,128]{2,1,0:T(8,128)(2,1)S(1)} %collective-permute-done.5), channel_id=1, source_target_pairs={{0,32},{32,64},{64,96},{96,128},{128,160},{160,192},{192,224},{1,3... | collective-permute-start | bytes 1572872 | tf_op jit(solution)/shard_map/ppermute | solution.py:14
  97.4 4.5 %collective-permute-done.6 = bf16[2,1024,128]{2,1,0:T(8,128)(2,1)S(1)} collective-permute-done((bf16[2,1024,128]{2,1,0:T(8,128)(2,1)S(1)}, bf16[2,1024,128]{2,1,0:T(8,128)(2,1)S(1)}, u32[]{:S(2)}, u32[]{:S(2)}) %collective-permute-start.6) | collective-permute-done | bytes 524320 | tf_op jit(solution)/shard_map/ppermute | solution.py:14
  102.6 7.2 %fusion.21 = (f32[1024]{0:T(1024)S(1)}, f32[1024]{0:T(1024)S(1)}, f32[1024]{0:T(1024)S(1)}, f32[1024]{0:T(1024)S(1)}, f32[1024]{0:T(1024)S(1)}, /*index=5*/f32[1024]{0:T(1024)S(1)}, f32[1024,1024]{1,0:T(8,128)S(1)}) fusion(f32[1024,1024]{0,1:T(8,128)S(1)} %fusion.141, f32[1024]{0:T(1024)S(1)} %broadcast_maximum_fusion, s32[1024]{0:T(1024)S(1)} %get-tuple-element.83, ...), kind=kOutput, calls=%fused_computation.47 | convolution fusion | flops 300935168 | bytes 25753600 | tf_op jit(solution)/shard_map/qhd,khd->hqk/dot_general | solution.py:43
  109.8 4.8 %fusion.31 = (f32[1024]{0:T(1024)S(1)}, f32[1024]{0:T(1024)S(1)}, f32[1024]{0:T(1024)S(1)}) fusion(f32[1024,1024]{1,0:T(8,128)S(1)} %fusion.111, f32[1024]{0:T(1024)S(1)} %get-tuple-element.28, s32[1024]{0:T(1024)S(1)} %get-tuple-element.83, s32[1024]{0:T(1024)S(1)} %get-tuple-element.86, pred[1024]{0:T(1024)(128)(4,1)S(1)} %get-tuple-element.76, ...), kind=kLoop, calls=%fused_computation.57 | loop fusion | flops 18871296 | bytes 12626944 | tf_op jit(solution)/shard_map/reduce_sum | solution.py:53
  114.6 7.1 %fusion.23 = (f32[1024]{0:T(1024)S(1)}, f32[1024]{0:T(1024)S(1)}, f32[1024]{0:T(1024)S(1)}, f32[1024]{0:T(1024)S(1)}) fusion(f32[1024,1024]{1,0:T(8,128)S(1)} %fusion.115, f32[1024]{0:T(1024)S(1)} %get-tuple-element.32, s32[1024]{0:T(1024)S(1)} %get-tuple-element.83, s32[1024]{0:T(1024)S(1)} %iota_add_fusion.6, pred[1024]{0:T(1024)(128)(4,1)S(1)} %get-tuple-element.81, ...), kind=kLoop, calls=%fused_computation.49 | loop fusion | flops 25161728 | bytes 16834560 | tf_op jit(solution)/shard_map/reduce_sum | solution.py:53
  121.8 1.8 fusion.77
  123.6 1.8 fusion.95
  125.4 1.8 fusion.92
  127.2 1.8 fusion.89
  129.0 1.8 fusion.86
  130.7 1.8 fusion.83
  132.5 1.8 fusion.80
  134.3 2.6 fusion.102
  142.4 1.1 constant_dynamic-slice_fusion.1
  206.2 45.3 %all-gather.3.cloned.1.call-done = bf16[1024,4096]{1,0:T(8,128)(2,1)} async-done(((bf16[1024,128]{1,0:T(8,128)(2,1)}), bf16[1024,4096]{1,0:T(8,128)(2,1)}) %all-gather.3.cloned.1.call-update) | async-done | bytes 8388624 | tf_op jit(solution)/shard_map/all_gather | solution.py:73
  251.5 5.7 %convolution_convert_fusion.2 = bf16[1024,128]{1,0:T(8,128)(2,1)S(1)} fusion(bf16[1024,4096]{1,0:T(8,128)(2,1)} %all-gather.3.cloned.1.call-done, bf16[4096,128]{1,0:T(8,128)(2,1)S(1)} %copy-done), kind=kOutput, calls=%fused_computation.89 | convolution fusion | flops 1073872896 | bytes 9699328 | tf_op jit(solution)/shard_map/dot_general | solution.py:72
  257.2 82.8 %all-gather.5.cloned.1.call-done = bf16[64,128,896]{2,1,0:T(8,128)(2,1)} async-done(((bf16[2,128,896]{2,1,0:T(8,128)(2,1)}), bf16[64,128,896]{2,1,0:T(8,128)(2,1)}) %all-gather.5.cloned.1.call-update) | async-done | bytes 14680080 | tf_op jit(solution)/shard_map/all_gather | solution.py:92
  340.9 1.0 dynamic-slice_dynamic-update-slice_fusion.30
  341.9 1.0 dynamic-slice_dynamic-update-slice_fusion.29
  342.9 1.0 dynamic-slice_dynamic-update-slice_fusion.28
  343.8 1.0 dynamic-slice_dynamic-update-slice_fusion.27
  344.8 1.0 dynamic-slice_dynamic-update-slice_fusion.26
  349.7 1.0 dynamic-slice_dynamic-update-slice_fusion.21
  351.6 1.0 dynamic-slice_dynamic-update-slice_fusion.19
  353.6 1.0 dynamic-slice_dynamic-update-slice_fusion.17
  354.6 1.0 dynamic-slice_dynamic-update-slice_fusion.16
  357.5 1.0 dynamic-slice_dynamic-update-slice_fusion.13
  359.5 1.0 dynamic-slice_dynamic-update-slice_fusion.11
  364.3 1.0 dynamic-slice_dynamic-update-slice_fusion.6
  366.3 1.0 dynamic-slice_dynamic-update-slice_fusion.4
  371.1 2.1 convolution_convert_fusion
  373.3 2.1 convolution_convert_fusion.1
  376.4 1.1 fusion.98
  (68 shorter events, 26.8 us)
Async XLA Ops:
  7.2 244.3 %copy-start = (bf16[4096,128]{1,0:T(8,128)(2,1)S(1)}, bf16[4096,128]{1,0:T(8,128)(2,1)}, u32[]{:S(2)}) copy-start(bf16[4096,128]{1,0:T(8,128)(2,1)} %param.17) | copy-start | bytes 3145732
  7.2 46.6 %copy-start.1 = (bf16[1024,128]{1,0:T(8,128)(2,1)S(1)}, bf16[1024,128]{1,0:T(8,128)(2,1)}, u32[]{:S(2)}) copy-start(bf16[1024,128]{1,0:T(8,128)(2,1)} %param.9) | copy-start | bytes 786436
  7.2 244.3 %all-gather.3.cloned.1.call-start = ((), (), s32[]{:S(2)}) async-start(), calls=%async_computation | async-start | bytes 8650752 | tf_op jit(solution)/shard_map/all_gather | solution.py:73
  8.4 14.6 %collective-permute-start = (bf16[2,1024,128]{2,1,0:T(8,128)(2,1)S(1)}, bf16[2,1024,128]{2,1,0:T(8,128)(2,1)S(1)}, u32[]{:S(2)}, u32[]{:S(2)}) collective-permute-start(bf16[2,1024,128]{2,1,0:T(8,128)(2,1)S(1)} %pad_maximum_fusion), channel_id=1, source_target_pairs={{0,32},{32,64},{64,96},{96,128},{128,160},{160,192},{192,224},{1,3... | collective-permute-start | bytes 1572872 | tf_op jit(solution)/shard_map/ppermute | solution.py:14
  23.0 13.8 %collective-permute-start.1 = (bf16[2,1024,128]{2,1,0:T(8,128)(2,1)S(1)}, bf16[2,1024,128]{2,1,0:T(8,128)(2,1)S(1)}, u32[]{:S(2)}, u32[]{:S(2)}) collective-permute-start(bf16[2,1024,128]{2,1,0:T(8,128)(2,1)S(1)} %collective-permute-done), channel_id=1, source_target_pairs={{0,32},{32,64},{64,96},{96,128},{128,160},{160,192},{192,224},{1,3... | collective-permute-start | bytes 1572872 | tf_op jit(solution)/shard_map/ppermute | solution.py:14
  36.8 12.8 %collective-permute-start.2 = (bf16[2,1024,128]{2,1,0:T(8,128)(2,1)S(1)}, bf16[2,1024,128]{2,1,0:T(8,128)(2,1)S(1)}, u32[]{:S(2)}, u32[]{:S(2)}) collective-permute-start(bf16[2,1024,128]{2,1,0:T(8,128)(2,1)S(1)} %collective-permute-done.1), channel_id=1, source_target_pairs={{0,32},{32,64},{64,96},{96,128},{128,160},{160,192},{192,224},{1,3... | collective-permute-start | bytes 1572872 | tf_op jit(solution)/shard_map/ppermute | solution.py:14
  49.6 11.9 %collective-permute-start.3 = (bf16[2,1024,128]{2,1,0:T(8,128)(2,1)S(1)}, bf16[2,1024,128]{2,1,0:T(8,128)(2,1)S(1)}, u32[]{:S(2)}, u32[]{:S(2)}) collective-permute-start(bf16[2,1024,128]{2,1,0:T(8,128)(2,1)S(1)} %collective-permute-done.2), channel_id=1, source_target_pairs={{0,32},{32,64},{64,96},{96,128},{128,160},{160,192},{192,224},{1,3... | collective-permute-start | bytes 1572872 | tf_op jit(solution)/shard_map/ppermute | solution.py:14
  61.5 12.7 %collective-permute-start.4 = (bf16[2,1024,128]{2,1,0:T(8,128)(2,1)S(1)}, bf16[2,1024,128]{2,1,0:T(8,128)(2,1)S(1)}, u32[]{:S(2)}, u32[]{:S(2)}) collective-permute-start(bf16[2,1024,128]{2,1,0:T(8,128)(2,1)S(1)} %collective-permute-done.3), channel_id=1, source_target_pairs={{0,32},{32,64},{64,96},{96,128},{128,160},{160,192},{192,224},{1,3... | collective-permute-start | bytes 1572872 | tf_op jit(solution)/shard_map/ppermute | solution.py:14
  74.2 13.8 %collective-permute-start.5 = (bf16[2,1024,128]{2,1,0:T(8,128)(2,1)S(1)}, bf16[2,1024,128]{2,1,0:T(8,128)(2,1)S(1)}, u32[]{:S(2)}, u32[]{:S(2)}) collective-permute-start(bf16[2,1024,128]{2,1,0:T(8,128)(2,1)S(1)} %collective-permute-done.4), channel_id=1, source_target_pairs={{0,32},{32,64},{64,96},{96,128},{128,160},{160,192},{192,224},{1,3... | collective-permute-start | bytes 1572872 | tf_op jit(solution)/shard_map/ppermute | solution.py:14
  88.1 13.8 %collective-permute-start.6 = (bf16[2,1024,128]{2,1,0:T(8,128)(2,1)S(1)}, bf16[2,1024,128]{2,1,0:T(8,128)(2,1)S(1)}, u32[]{:S(2)}, u32[]{:S(2)}) collective-permute-start(bf16[2,1024,128]{2,1,0:T(8,128)(2,1)S(1)} %collective-permute-done.5), channel_id=1, source_target_pairs={{0,32},{32,64},{64,96},{96,128},{128,160},{160,192},{192,224},{1,3... | collective-permute-start | bytes 1572872 | tf_op jit(solution)/shard_map/ppermute | solution.py:14
  114.6 7.2 %copy-start.2 = (bf16[1024,128]{1,0:T(8,128)(2,1)S(1)}, bf16[1024,128]{1,0:T(8,128)(2,1)}, u32[]{:S(2)}) copy-start(bf16[1024,128]{1,0:T(8,128)(2,1)} %param.11) | copy-start | bytes 786436
  134.3 2.8 copy-start.5
  134.3 2.9 copy-start.6
  137.0 203.0 %all-gather.5.cloned.1.call-start = ((), (), s32[]{:S(2)}) async-start(), calls=%async_computation.1 | async-start | bytes 15138816 | tf_op jit(solution)/shard_map/all_gather | solution.py:92
  353.6 17.6 %copy-start.3 = (bf16[896,128]{1,0:T(8,128)(2,1)S(1)}, bf16[896,128]{1,0:T(8,128)(2,1)}, u32[]{:S(2)}) copy-start(bf16[896,128]{1,0:T(8,128)(2,1)} %param.16) | copy-start | bytes 688132
  371.1 2.2 copy-start.4
Sparse Core Ops, SparseCore 0:
  137.1 114.2 all-gather.2
  253.3 86.6 all-gather.4

commit v2 on v1

v2 whole, which is shorter than its diff:
```python
import functools
import math

import jax
import jax.numpy as jnp
from jax import lax
from jax.experimental import pallas as pl
from jax.experimental.pallas import tpu as pltpu
from jax.sharding import Mesh
from jax.sharding import PartitionSpec as P

HD = 128
AXES = ("x_hi", "y", "z", "x_lo", "core")
CTX = ("x_hi", "y")
DB = ("z", "x_lo", "core")
XC = ("x_lo", "core")
XX = ("x_hi", "x_lo")
LOW = -1e30
EXP2_SCALE = math.log2(math.e) / math.sqrt(HD)
BF = jnp.bfloat16
F32 = jnp.float32


def ring(value, axis, step):
    n = lax.axis_size(axis)
    return lax.ppermute(value, axis, [(i, (i + step) % n) for i in range(n)])


def swap(value, axis):
    return lax.ppermute(value, axis, [(0, 1), (1, 0)])


def params(megabytes):
    return pltpu.CompilerParams(
        dimension_semantics=("arbitrary",), vmem_limit_bytes=megabytes << 20
    )


def dot_t(a, b):
    return lax.dot_general(a, b, (((1,), (1,)), ((), ())), preferred_element_type=F32)


def attend_kernel(
    tile, flags, q_ref, qs_ref, kv0, kv1, kv2, k3, v3, o_ref, lse_ref, os_ref, lses_ref, kx, vx, m_ref, acc
):
    t = pl.program_id(0)
    rows = kx.shape[1]
    tiles = rows // tile

    @pl.when(t == 0)
    def _():
        for b, (key, value) in enumerate(
            ((kv0.at[0], kv0.at[1]), (kv1.at[0], kv1.at[1]), (kv2.at[0], kv2.at[1]), (k3, v3))
        ):
            kx[b] = key[...]
            vx[b, :, :HD] = value[...]
            vx[b, :, HD:] = jnp.ones((rows, HD), BF)

    def step(q, b, masked):
        s = dot_t(q, kx[b])
        if masked:
            row = lax.broadcasted_iota(jnp.int32, s.shape, 0) + t * tile
            s = jnp.where(row >= lax.broadcasted_iota(jnp.int32, s.shape, 1), s, LOW)
        before = m_ref[...]
        now = jnp.maximum(before, jnp.max(s, axis=1, keepdims=True))
        p = jnp.exp2((s - now[:, :1]) * EXP2_SCALE)
        factor = jnp.exp2((before - now) * EXP2_SCALE)
        m_ref[...] = now
        acc[...] = acc[...] * jnp.concatenate([factor, factor], axis=1) + jnp.dot(
            p.astype(BF), vx[b], preferred_element_type=F32
        )

    def finish():
        total = acc[:, HD:]
        lse = m_ref[...] * EXP2_SCALE + jnp.log2(total)
        return acc[:, :HD] / total, lse.T[:1]

    m_ref[...] = jnp.full_like(m_ref, LOW)
    acc[...] = jnp.zeros_like(acc)

    @pl.when(t < tiles)
    def _():
        q = q_ref[...]
        step(q, 0, True)

        @pl.loop(1, 4)
        def _(b):
            @pl.when(flags[b] == 1)
            def _():
                step(q, b, False)

        o, lse = finish()
        o_ref[...] = o
        lse_ref[0] = lse

    @pl.when((t >= tiles) & (flags[0] == 1))
    def _():
        q = qs_ref[...]

        @pl.loop(0, 4)
        def _(b):
            step(q, b, False)

        o, lse = finish()
        os_ref[...] = o.astype(BF)
        lses_ref[0] = lse


def attend(flags, q, qs, kv0, kv1, kv2, k3, v3):
    rows = q.shape[0]
    tile = 256
    tiles = rows // tile
    first = lambda t, f: (jnp.minimum(t, tiles - 1), 0)
    second = lambda t, f: (jnp.maximum(t - tiles, 0), 0)
    whole3 = pl.BlockSpec((2, rows, HD), lambda t, f: (0, 0, 0))
    whole2 = pl.BlockSpec((rows, HD), lambda t, f: (0, 0))
    stat = jax.ShapeDtypeStruct((tiles, 1, tile), F32)
    return pl.pallas_call(
        functools.partial(attend_kernel, tile),
        grid_spec=pltpu.PrefetchScalarGridSpec(
            num_scalar_prefetch=1,
            grid=(2 * tiles,),
            in_specs=[
                pl.BlockSpec((tile, HD), first),
                pl.BlockSpec((tile, HD), second),
                whole3,
                whole3,
                whole3,
                whole2,
                whole2,
            ],
            out_specs=[
                pl.BlockSpec((tile, HD), first),
                pl.BlockSpec((1, 1, tile), lambda t, f: (jnp.minimum(t, tiles - 1), 0, 0)),
                pl.BlockSpec((tile, HD), second),
                pl.BlockSpec((1, 1, tile), lambda t, f: (jnp.maximum(t - tiles, 0), 0, 0)),
            ],
            scratch_shapes=[
                pltpu.VMEM((4, rows, HD), BF),
                pltpu.VMEM((4, rows, 2 * HD), BF),
                pltpu.VMEM((tile, HD), F32),
                pltpu.VMEM((tile, 2 * HD), F32),
            ],
        ),
        out_shape=[
            jax.ShapeDtypeStruct((rows, HD), F32),
            stat,
            jax.ShapeDtypeStruct((rows, HD), BF),
            stat,
        ],
        compiler_params=params(40),
        cost_estimate=pl.CostEstimate(flops=3 << 30, bytes_accessed=4 << 20, transcendentals=0),
        name="attend",
    )(flags, q, qs, kv0, kv1, kv2, k3, v3)


def pick_rows(states, rows):
    return jnp.concatenate([lax.dynamic_slice_in_dim(states, rows[i], 1, 0) for i in range(rows.shape[0])], axis=0)


def cross_queries(z, parts, weights):
    total = 0.0
    for back, part in enumerate(parts):
        a = part.transpose(1, 0, 2).reshape(part.shape[1], -1)
        w = lax.dynamic_index_in_dim(weights, (z + 8 - back) % 8, 0, keepdims=False)
        total = total + jnp.dot(a, w, preferred_element_type=F32)
    return total.astype(BF)


def cross(slots, gathered, wk4, wv4, queries):
    picked = jnp.concatenate([lax.dynamic_slice_in_dim(gathered, slots[i], 1, 0) for i in range(slots.shape[0])], axis=0)
    picked = picked.reshape(-1, picked.shape[2])
    keys = jnp.dot(picked, wk4, preferred_element_type=F32).astype(BF).reshape(4, -1, 4, HD)
    values = jnp.dot(picked, wv4, preferred_element_type=F32).astype(BF).reshape(4, -1, 4, HD)
    q = queries.reshape(4, -1, 4, HD)
    scores = jnp.einsum("cqhd,ckhd->chqk", q, keys, preferred_element_type=F32)
    p = jnp.exp2((scores - jnp.max(scores, axis=3, keepdims=True)) * EXP2_SCALE)
    total = jnp.sum(p, axis=3, keepdims=True)
    o = jnp.einsum("chqk,ckhd->chqd", p.astype(BF), values, preferred_element_type=F32) / total
    o = o.astype(BF).transpose(1, 0, 2, 3).reshape(4, -1, HD)
    o = jnp.where(lax.axis_index("x_lo") == 1, jnp.concatenate([o[2:], o[:2]]), o)
    return jnp.where(lax.axis_index("core") == 1, jnp.stack([o[1], o[0], o[3], o[2]]), o)


def local(q, k, v, states, nb_shard, nb_row, wk, wv, wq):
    rows = q.shape[0]
    y = lax.axis_index("y")
    z = lax.axis_index("z")
    late = lax.axis_index("x_hi") == 1
    xc = lax.axis_index(XC)
    db_index = lax.axis_index(DB)
    db_size = lax.axis_size(DB)

    requests = nb_shard.size
    capacity = 2 * ((requests + db_size - 1) // db_size)
    shard_flat = nb_shard.reshape(requests)
    row_flat = nb_row.reshape(requests)
    same = shard_flat[:, None] == shard_flat[None, :]
    earlier = jnp.arange(requests)[None, :] < jnp.arange(requests)[:, None]
    rank = jnp.sum((same & earlier).astype(jnp.int32), axis=1)
    picked = (shard_flat[None, :] == db_index) & (rank[None, :] == jnp.arange(capacity)[:, None])
    slot_rows = jnp.sum(jnp.where(picked, row_flat[None, :], 0), axis=1)
    slot_of = shard_flat * capacity + rank
    gathered = lax.all_gather(pick_rows(states, slot_rows), DB, axis=0, tiled=True)

    kv0 = jnp.stack([k, v])
    kv1 = ring(kv0, "y", 1)
    kv2 = ring(kv0, "y", -1)
    qs = lax.ppermute(q, "x_hi", [(1, 0)])
    k3 = ring(kv1[0], "y", 1)
    v3 = ring(kv2[1], "y", -1)
    flags = jnp.stack([~late, y >= 1, y >= 3, y >= 2]).astype(jnp.int32)
    o, lse, o_sent, lse_sent = attend(flags, q, qs, kv0, kv1, kv2, k3, v3)
    o_back = lax.ppermute(o_sent, "x_hi", [(0, 1)])
    lse_back = lax.ppermute(lse_sent, "x_hi", [(0, 1)])
    lse_own = lse.reshape(rows, 1)
    lse_back = jnp.where(late, lse_back.reshape(rows, 1), LOW)
    top = jnp.maximum(lse_own, lse_back)
    e_own = jnp.exp2(lse_own - top)
    e_back = jnp.exp2(lse_back - top)
    self_out = ((o * e_own + o_back.astype(F32) * e_back) / (e_own + e_back)).astype(BF)

    wall = jnp.concatenate([wq, wk, wv], axis=0)
    half = wall.shape[0] // 2
    w_x = jnp.concatenate([ring(wall[:half], XX, -1), ring(wall[half:], XX, 1)], axis=0)
    w4 = jnp.concatenate([wall, swap(wall, "core"), w_x, swap(w_x, "core")], axis=1)
    depth, width = wq.shape[0], wk.shape[0]
    wq4 = w4[:depth].reshape(8, depth // 8, 4 * HD)
    wk4 = w4[depth : depth + width]
    wv4 = w4[depth + width :]

    mine = lax.all_to_all(self_out.reshape(4, rows // 4, HD), XC, 0, 0)
    f1 = ring(mine, "z", 1)
    b1 = ring(mine, "z", -1)
    f2 = ring(f1, "z", 1)
    b2 = ring(b1, "z", -1)
    f3 = ring(f2, "z", 1)
    b3 = ring(b2, "z", -1)
    far = jnp.concatenate([ring(f3[:2], "z", 1), ring(b3[2:], "z", -1)], axis=0)
    queries = cross_queries(z, (mine, f1, f2, f3, far, b3, b2, b1), wq4)

    per = requests // 4
    slots = lax.dynamic_slice(slot_of, (xc * per,), (per,))
    out = cross(slots, gathered, wk4, wv4, queries)
    cross_out = lax.all_to_all(out, XC, 0, 0).reshape(rows, HD)
    return (self_out, cross_out)


def solution(mesh):
    fine = Mesh(mesh.devices.reshape(2, 4, 8, 2, 2), AXES)
    return jax.shard_map(
        local,
        mesh=fine,
        in_specs=(
            P(CTX, DB),
            P(CTX, DB),
            P(CTX, DB),
            P(DB, None, None),
            P(CTX, None),
            P(CTX, None),
            P(None, DB),
            P(None, DB),
            P(None, DB),
        ),
        out_specs=(P(CTX, DB), P(CTX, DB)),
        check_vma=False,
    )
```

time: 392 us -> 217 us (0.55)
  the two profiles are of different devices: /device:TPU:1 before, /device:TPU:31 now
where the time goes in v2:
time: 217 us; the launch traced here: 214 us
  waiting for transfers between devices  58.8 us (27%)
  starting transfers between devices  34.9 us (16%)
  between operations  33.3 us (15%)
  local copies, waits for them, and re-layouts  26.5 us (12%)
  blocking collectives  21.9 us (10%)
  Pallas kernels  17.5 us (8%)
  matrix products  12.8 us (6%)
  other arithmetic  7.97 us (4%)
    ppermute x14, waiting for transfers between devices, ring(): return lax.ppermute(value, axis, [(i, (i + step) % n) for i in range(n)])  39.9 us
    ppermute x14, starting transfers between devices, ring(): return lax.ppermute(value, axis, [(i, (i + step) % n) for i in range(n)])  21 us
    pallas_call x1, Pallas kernels, attend(): pl.pallas_call(functools.partial(attend_kernel, tile), grid_spec=pltpu.Pr...  17.5 us
    ppermute x1, waiting for transfers between devices, local(): o_back = lax.ppermute(o_sent, 'x_hi', [(0, 1)])  15.8 us
    unnamed x31, local copies, waits for them, and re-layouts  13.7 us
    all_to_all x1, blocking collectives, local(): mine = lax.all_to_all(self_out.reshape(4, rows // 4, HD), XC, 0, 0)  11.2 us
    all_to_all x1, blocking collectives, local(): cross_out = lax.all_to_all(out, XC, 0, 0).reshape(rows, HD)  10.7 us
    ppermute x2, starting transfers between devices, swap(): return lax.ppermute(value, axis, [(0, 1), (1, 0)])  8.2 us
  transfers between devices with their start and end apart: 20, of which 9 were waited for; matrix products, arithmetic and copies ran while one was open for 8% of the time, Pallas kernels for 8%

profile of v2, /device:TPU:31, one launch (start us, length us, event | category | flops | bytes accessed | tf_op | source)
XLA Modules:
  0.0 213.7 jit_solution(16665368062399549248)
XLA Ops:
  7.3 0.9 copy.35
  13.9 1.1 constant_dynamic-slice_fusion.1
  15.0 0.8 pad_maximum_fusion.2
  16.0 1.5 collective-permute-start.2
  17.4 3.0 %collective-permute-start = (bf16[1024,128]{1,0:T(8,128)(2,1)S(1)}, bf16[1024,128]{1,0:T(8,128)(2,1)S(1)}, u32[]{:S(2)}, u32[]{:S(2)}) collective-permute-start(bf16[1024,128]{1,0:T(8,128)(2,1)S(1)} %copy-done), channel_id=1, source_target_pairs={{128,0},{129,1},{130,2},{131,3},{132,4},{133,5},{134,6},{135,7},{1... | collective-permute-start | bytes 786440 | tf_op jit(solution)/shard_map/ppermute | solution.py:209
  20.5 0.9 slice.83
  21.4 1.1 constant_dynamic-update-slice_fusion.2
  23.9 1.5 collective-permute-start.7
  25.4 1.2 slice.110
  26.7 2.2 %collective-permute-done.1.kv1 = bf16[2,1024,128]{2,1,0:T(8,128)(2,1)S(1)} collective-permute-done((bf16[2,1024,128]{2,1,0:T(8,128)(2,1)S(1)}, bf16[2,1024,128]{2,1,0:T(8,128)(2,1)S(1)}, u32[]{:S(2)}, u32[]{:S(2)}) %collective-permute-start.1) | collective-permute-done | bytes 524320 | tf_op jit(solution)/shard_map/ppermute | solution.py:26
  28.9 0.8 collective-permute-start.9
  30.0 0.9 collective-permute-start.3
  30.9 20.6 %collective-permute-done.8 = bf16[2944,128]{1,0:T(8,128)(2,1)} collective-permute-done((bf16[2944,128]{1,0:T(8,128)(2,1)}, bf16[2944,128]{1,0:T(8,128)(2,1)}, u32[]{:S(2)}, u32[]{:S(2)}) %collective-permute-start.8) | collective-permute-done | bytes 753696 | tf_op jit(solution)/shard_map/ppermute | solution.py:26
  51.9 2.1 constant_dynamic-update-slice_fusion.4
  54.0 4.0 %collective-permute-done.4.v3 = bf16[1024,128]{1,0:T(8,128)(2,1)S(1)} collective-permute-done((bf16[1024,128]{1,0:T(8,128)(2,1)S(1)}, bf16[1024,128]{1,0:T(8,128)(2,1)S(1)}, u32[]{:S(2)}, u32[]{:S(2)}) %collective-permute-start.4) | collective-permute-done | bytes 262176 | tf_op jit(solution)/shard_map/ppermute | solution.py:26
  58.0 17.5 %attend.1 = (f32[1024,128]{1,0:T(8,128)S(1)}, f32[4,1,256]{2,1,0:T(1,128)S(1)}, bf16[1024,128]{1,0:T(8,128)(2,1)S(1)}, f32[4,1,256]{2,1,0:T(1,128)S(1)}) custom-call(s32[4]{0:T(128)S(1)} %add_convert_fusion.flags, bf16[1024,128]{1,0:T(8,128)(2,1)S(1)} %copy-done, bf16[1024,128]{1,0:T(8,128)(2,1)S(1)} %collective-permute-done.qs_ref, ...), custom_call_target="tpu_custom_call" | custom-call | flops 3221225472 | bytes 4194304 | tf_op jit(solution)/shard_map/attend/pallas_call | solution.py:118
  75.5 1.3 collective-permute-start.5
  76.8 0.9 constant_dynamic-update-slice_fusion.3
  77.7 6.7 %collective-permute-start.10 = (bf16[5888,128]{1,0:T(8,128)(2,1)}, bf16[5888,128]{1,0:T(8,128)(2,1)S(1)}, u32[]{:S(2)}, u32[]{:S(2)}) collective-permute-start(bf16[5888,128]{1,0:T(8,128)(2,1)} %constant_dynamic-update-slice_fusion.3), channel_id=1, source_target_pairs={{0,1},{1,0},{2,3},{3,2},{4,5},{5,4},{6,7},{7,6},{8,9},{9,8},{10,11... | collective-permute-start | bytes 4521992 | tf_op jit(solution)/shard_map/ppermute | solution.py:30
  84.4 1.3 collective-permute-start.6
  85.7 3.1 %collective-permute-done.5 = f32[4,1,256]{2,1,0:T(1,128)S(1)} collective-permute-done((f32[4,1,256]{2,1,0:T(1,128)S(1)}, f32[4,1,256]{2,1,0:T(1,128)S(1)}, u32[]{:S(2)}, u32[]{:S(2)}) %collective-permute-start.5) | collective-permute-done | bytes 4128 | tf_op jit(solution)/shard_map/ppermute | solution.py:215
  88.8 15.8 %collective-permute-done.6 = bf16[1024,128]{1,0:T(8,128)(2,1)S(1)} collective-permute-done((bf16[1024,128]{1,0:T(8,128)(2,1)S(1)}, bf16[1024,128]{1,0:T(8,128)(2,1)S(1)}, u32[]{:S(2)}, u32[]{:S(2)}) %collective-permute-start.6) | collective-permute-done | bytes 262176 | tf_op jit(solution)/shard_map/ppermute | solution.py:214
  106.0 11.2 %all_to_all.10 = bf16[4,256,128]{1,2,0:T(8,128)(2,1)S(1)} all-to-all(bf16[4,256,128]{1,2,0:T(8,128)(2,1)S(1)} %copy.34), channel_id=1, replica_groups=mesh['x_hi'=2,'y'=4,'z'=8,'x_lo'=2,'core'=2] {'x_lo','core'}, dimensions={0} | all-to-all | bytes 524288 | tf_op jit(solution)/shard_map/all_to_all | solution.py:232
  117.2 7.1 %collective-permute-start.15 = (bf16[4,256,128]{1,2,0:T(8,128)(2,1)S(1)}, bf16[4,256,128]{1,2,0:T(8,128)(2,1)S(1)}, u32[]{:S(2)}, u32[]{:S(2)}) collective-permute-start(bf16[4,256,128]{1,2,0:T(8,128)(2,1)S(1)} %all_to_all.10), channel_id=1, source_target_pairs={{0,28},{4,0},{8,4},{12,8},{16,12},{20,16},{24,20},{28,24},{1,29},{... | collective-permute-start | bytes 786440 | tf_op jit(solution)/shard_map/ppermute | solution.py:26
  124.3 5.2 %collective-permute-done.15 = bf16[4,256,128]{1,2,0:T(8,128)(2,1)S(1)} collective-permute-done((bf16[4,256,128]{1,2,0:T(8,128)(2,1)S(1)}, bf16[4,256,128]{1,2,0:T(8,128)(2,1)S(1)}, u32[]{:S(2)}, u32[]{:S(2)}) %collective-permute-start.15) | collective-permute-done | bytes 262176 | tf_op jit(solution)/shard_map/ppermute | solution.py:26
  129.5 3.4 %collective-permute-start.16 = (bf16[4,256,128]{1,2,0:T(8,128)(2,1)S(1)}, bf16[4,256,128]{1,2,0:T(8,128)(2,1)S(1)}, u32[]{:S(2)}, u32[]{:S(2)}) collective-permute-start(bf16[4,256,128]{1,2,0:T(8,128)(2,1)S(1)} %collective-permute-done.15), channel_id=1, source_target_pairs={{0,28},{4,0},{8,4},{12,8},{16,12},{20,16},{24,20},{28,24},{1,29},{... | collective-permute-start | bytes 786440 | tf_op jit(solution)/shard_map/ppermute | solution.py:26
  132.9 4.3 %collective-permute-done.16 = bf16[4,256,128]{1,2,0:T(8,128)(2,1)S(1)} collective-permute-done((bf16[4,256,128]{1,2,0:T(8,128)(2,1)S(1)}, bf16[4,256,128]{1,2,0:T(8,128)(2,1)S(1)}, u32[]{:S(2)}, u32[]{:S(2)}) %collective-permute-start.16) | collective-permute-done | bytes 262176 | tf_op jit(solution)/shard_map/ppermute | solution.py:26
  137.1 3.4 %collective-permute-start.17 = (bf16[4,256,128]{1,2,0:T(8,128)(2,1)S(1)}, bf16[4,256,128]{1,2,0:T(8,128)(2,1)S(1)}, u32[]{:S(2)}, u32[]{:S(2)}) collective-permute-start(bf16[4,256,128]{1,2,0:T(8,128)(2,1)S(1)} %collective-permute-done.16), channel_id=1, source_target_pairs={{0,28},{4,0},{8,4},{12,8},{16,12},{20,16},{24,20},{28,24},{1,29},{... | collective-permute-start | bytes 786440 | tf_op jit(solution)/shard_map/ppermute | solution.py:26
  140.6 3.3 %collective-permute-done.17 = bf16[4,256,128]{1,2,0:T(8,128)(2,1)S(1)} collective-permute-done((bf16[4,256,128]{1,2,0:T(8,128)(2,1)S(1)}, bf16[4,256,128]{1,2,0:T(8,128)(2,1)S(1)}, u32[]{:S(2)}, u32[]{:S(2)}) %collective-permute-start.17) | collective-permute-done | bytes 262176 | tf_op jit(solution)/shard_map/ppermute | solution.py:26
  143.9 3.5 %collective-permute-start.18 = (bf16[2,256,128]{1,2,0:T(8,128)(2,1)S(1)}, bf16[2,256,128]{1,2,0:T(8,128)(2,1)}, u32[]{:S(2)}, u32[]{:S(2)}) collective-permute-start(bf16[2,256,128]{1,2,0:T(8,128)(2,1)S(1)} %slice.113), channel_id=1, source_target_pairs={{0,28},{4,0},{8,4},{12,8},{16,12},{20,16},{24,20},{28,24},{1,29},{... | collective-permute-start | bytes 393224 | tf_op jit(solution)/shard_map/ppermute | solution.py:26
  163.8 1.0 pad_maximum_fusion.3
  164.8 3.2 %pad_maximum_fusion = bf16[5888,512]{1,0:T(8,128)(2,1)S(1)} fusion(bf16[5888,128]{1,0:T(8,128)(2,1)S(1)} %collective-permute-done.10, bf16[5888,128]{1,0:T(8,128)(2,1)} %constant_dynamic-update-slice_fusion.3, bf16[5888,128]{1,0:T(8,128)(2,1)} %collective-permute-done.7, bf16[5888,128]{1,0:T(8,128)(2,1)} %constant_dynamic-update-slice_fusion), kind=kLoop, calls=%fused_computation.1 | loop fusion | flops 24117248 | bytes 12058624 | tf_op jit(solution)/shard_map/concatenate | solution.py:226
  171.7 1.0 dynamic-slice_dynamic-update-slice_fusion.7
  172.6 1.0 dynamic-slice_dynamic-update-slice_fusion.6
  173.6 1.0 dynamic-slice_dynamic-update-slice_fusion.5
  174.6 1.0 dynamic-slice_dynamic-update-slice_fusion.4
  175.6 1.0 dynamic-slice_dynamic-update-slice_fusion.3
  176.5 1.0 dynamic-slice_dynamic-update-slice_fusion.2
  177.5 1.0 dynamic-slice_dynamic-update-slice_fusion.1
  178.5 1.0 dynamic-slice_dynamic-update-slice_fusion
  179.4 3.4 %convolution_convert_fusion = bf16[1024,512]{1,0:T(8,128)(2,1)} fusion(bf16[1024,896]{1,0:T(8,128)(2,1)S(1)} %bitcast.106, bf16[5888,128]{1,0:T(8,128)(2,1)S(1)} %collective-permute-done.10, bf16[5888,128]{1,0:T(8,128)(2,1)} %constant_dynamic-update-slice_fusion.3, bf16[5888,128]{1,0:T(8,128)(2,1)} %collective-permute-done.7, ...), kind=kOutput, calls=%fused_computation.3 | convolution fusion | flops 943718400 | bytes 8912896 | tf_op jit(solution)/shard_map/dot_general | solution.py:174
  182.8 2.2 %reshape.137 = bf16[4,256,4,128]{3,2,1,0:T(4,128)(2,1)} reshape(bf16[1024,512]{1,0:T(8,128)(2,1)} %convolution_convert_fusion) | data formatting | bytes 2097152 | tf_op jit(solution)/shard_map/reshape | solution.py:174
  185.0 3.4 %convolution_convert_fusion.1 = bf16[1024,512]{1,0:T(8,128)(2,1)} fusion(bf16[1024,896]{1,0:T(8,128)(2,1)S(1)} %bitcast.107, bf16[5888,128]{1,0:T(8,128)(2,1)S(1)} %collective-permute-done.10, bf16[5888,128]{1,0:T(8,128)(2,1)} %constant_dynamic-update-slice_fusion.3, bf16[5888,128]{1,0:T(8,128)(2,1)} %collective-permute-done.7, ...), kind=kOutput, calls=%fused_computation.4 | convolution fusion | flops 943718400 | bytes 8912896 | tf_op jit(solution)/shard_map/dot_general | solution.py:173
  188.4 1.4 reshape.136
  189.8 1.4 fusion.11
  191.2 1.9 fusion.74
  193.2 2.0 fusion.8
  195.4 10.7 %all_to_all.11 = bf16[4,256,128]{2,1,0:T(8,128)(2,1)S(1)} all-to-all(bf16[4,256,128]{2,1,0:T(8,128)(2,1)S(1)} %maximum_select_fusion.1), channel_id=1, replica_groups=mesh['x_hi'=2,'y'=4,'z'=8,'x_lo'=2,'core'=2] {'x_lo','core'}, dimensions={0} | all-to-all | bytes 524288 | tf_op jit(solution)/shard_map/all_to_all | solution.py:245
  (79 shorter events, 11.6 us)
Async XLA Ops:
  7.2 8.6 %copy-start.5 = (bf16[1024,128]{1,0:T(8,128)(2,1)S(1)}, bf16[1024,128]{1,0:T(8,128)(2,1)}, u32[]{:S(2)}) copy-start(bf16[1024,128]{1,0:T(8,128)(2,1)} %param.11) | copy-start | bytes 786436
  7.2 8.6 %copy-start.6 = (bf16[1024,128]{1,0:T(8,128)(2,1)S(1)}, bf16[1024,128]{1,0:T(8,128)(2,1)}, u32[]{:S(2)}) copy-start(bf16[1024,128]{1,0:T(8,128)(2,1)} %param.10) | copy-start | bytes 786436
  7.2 10.3 %copy-start = (bf16[1024,128]{1,0:T(8,128)(2,1)S(1)}, bf16[1024,128]{1,0:T(8,128)(2,1)}, u32[]{:S(2)}) copy-start(bf16[1024,128]{1,0:T(8,128)(2,1)} %q_ref.1) | copy-start | bytes 786436
  7.2 13.3 %copy-start.1 = (bf16[4096,128]{1,0:T(8,128)(2,1)S(1)}, bf16[4096,128]{1,0:T(8,128)(2,1)}, u32[]{:S(2)}) copy-start(bf16[4096,128]{1,0:T(8,128)(2,1)} %param.17) | copy-start | bytes 3145732
  7.2 164.5 %all-gather.2.cloned.1.call-start = ((), (), s32[]{:S(2)}) async-start(), calls=%async_computation.2 | async-start | bytes 15138816 | tf_op jit(solution)/shard_map/all_gather | solution.py:204
  15.9 6.6 %copy-start.7 = (bf16[896,128]{1,0:T(8,128)(2,1)S(1)}, bf16[896,128]{1,0:T(8,128)(2,1)}, u32[]{:S(2)}) copy-start(bf16[896,128]{1,0:T(8,128)(2,1)} %param.15) | copy-start | bytes 688132
  15.9 7.3 %copy-start.8 = (bf16[896,128]{1,0:T(8,128)(2,1)S(1)}, bf16[896,128]{1,0:T(8,128)(2,1)}, u32[]{:S(2)}) copy-start(bf16[896,128]{1,0:T(8,128)(2,1)} %param.16) | copy-start | bytes 688132
  15.9 13.0 %collective-permute-start.1 = (bf16[2,1024,128]{2,1,0:T(8,128)(2,1)S(1)}, bf16[2,1024,128]{2,1,0:T(8,128)(2,1)S(1)}, u32[]{:S(2)}, u32[]{:S(2)}) collective-permute-start(bf16[2,1024,128]{2,1,0:T(8,128)(2,1)S(1)} %pad_maximum_fusion.1.kv0), channel_id=1, source_target_pairs={{0,32},{32,64},{64,96},{96,0},{1,33},{33,65},{65,97},{97,1},{2,34}... | collective-permute-start | bytes 1572872 | tf_op jit(solution)/shard_map/ppermute | solution.py:26
  16.0 14.0 %collective-permute-start.2 = (bf16[2,1024,128]{2,1,0:T(8,128)(2,1)S(1)}, bf16[2,1024,128]{2,1,0:T(8,128)(2,1)S(1)}, u32[]{:S(2)}, u32[]{:S(2)}) collective-permute-start(bf16[2,1024,128]{2,1,0:T(8,128)(2,1)S(1)} %pad_maximum_fusion.1.kv0), channel_id=1, source_target_pairs={{0,96},{32,0},{64,32},{96,64},{1,97},{33,1},{65,33},{97,65},{2,98}... | collective-permute-start | bytes 1572872 | tf_op jit(solution)/shard_map/ppermute | solution.py:26
  17.4 36.5 %collective-permute-start = (bf16[1024,128]{1,0:T(8,128)(2,1)S(1)}, bf16[1024,128]{1,0:T(8,128)(2,1)S(1)}, u32[]{:S(2)}, u32[]{:S(2)}) collective-permute-start(bf16[1024,128]{1,0:T(8,128)(2,1)S(1)} %copy-done), channel_id=1, source_target_pairs={{128,0},{129,1},{130,2},{131,3},{132,4},{133,5},{134,6},{135,7},{1... | collective-permute-start | bytes 786440 | tf_op jit(solution)/shard_map/ppermute | solution.py:209
  21.4 30.1 %collective-permute-start.8 = (bf16[2944,128]{1,0:T(8,128)(2,1)}, bf16[2944,128]{1,0:T(8,128)(2,1)}, u32[]{:S(2)}, u32[]{:S(2)}) collective-permute-start(bf16[2944,128]{1,0:T(8,128)(2,1)} %slice.83), channel_id=1, source_target_pairs={{0,130},{2,0},{128,2},{130,128},{1,131},{3,1},{129,3},{131,129},{4... | collective-permute-start | bytes 2261000 | tf_op jit(solution)/shard_map/ppermute | solution.py:26
  23.9 140.9 %collective-permute-start.7 = (bf16[5888,128]{1,0:T(8,128)(2,1)}, bf16[5888,128]{1,0:T(8,128)(2,1)}, u32[]{:S(2)}, u32[]{:S(2)}) collective-permute-start(bf16[5888,128]{1,0:T(8,128)(2,1)} %constant_dynamic-update-slice_fusion), channel_id=1, source_target_pairs={{0,1},{1,0},{2,3},{3,2},{4,5},{5,4},{6,7},{7,6},{8,9},{9,8},{10,11... | collective-permute-start | bytes 4521992 | tf_op jit(solution)/shard_map/ppermute | solution.py:30
  28.9 47.9 %collective-permute-start.9 = (bf16[2944,128]{1,0:T(8,128)(2,1)S(1)}, bf16[2944,128]{1,0:T(8,128)(2,1)S(1)}, u32[]{:S(2)}, u32[]{:S(2)}) collective-permute-start(bf16[2944,128]{1,0:T(8,128)(2,1)S(1)} %slice.110), channel_id=1, source_target_pairs={{0,2},{2,128},{128,130},{130,0},{1,3},{3,129},{129,131},{131,1},{4... | collective-permute-start | bytes 2261000 | tf_op jit(solution)/shard_map/ppermute | solution.py:26
  30.0 24.0 %collective-permute-start.3 = (bf16[1024,128]{1,0:T(8,128)(2,1)S(1)}, bf16[1024,128]{1,0:T(8,128)(2,1)S(1)}, u32[]{:S(2)}, u32[]{:S(2)}) collective-permute-start(bf16[1024,128]{1,0:T(8,128)(2,1)S(1)} %slice_bitcast_fusion.1), channel_id=1, source_target_pairs={{0,32},{32,64},{64,96},{96,0},{1,33},{33,65},{65,97},{97,1},{2,34}... | collective-permute-start | bytes 786440 | tf_op jit(solution)/shard_map/ppermute | solution.py:26
  51.5 6.4 %collective-permute-start.4 = (bf16[1024,128]{1,0:T(8,128)(2,1)S(1)}, bf16[1024,128]{1,0:T(8,128)(2,1)S(1)}, u32[]{:S(2)}, u32[]{:S(2)}) collective-permute-start(bf16[1024,128]{1,0:T(8,128)(2,1)S(1)} %slice_bitcast_fusion), channel_id=1, source_target_pairs={{0,96},{32,0},{64,32},{96,64},{1,97},{33,1},{65,33},{97,65},{2,98}... | collective-permute-start | bytes 786440 | tf_op jit(solution)/shard_map/ppermute | solution.py:26
  75.5 13.3 %collective-permute-start.5 = (f32[4,1,256]{2,1,0:T(1,128)S(1)}, f32[4,1,256]{2,1,0:T(1,128)S(1)}, u32[]{:S(2)}, u32[]{:S(2)}) collective-permute-start(f32[4,1,256]{2,1,0:T(1,128)S(1)} %get-tuple-element.8), channel_id=1, source_target_pairs={{0,128},{1,129},{2,130},{3,131},{4,132},{5,133},{6,134},{7,135},{8... | collective-permute-start | bytes 12296 | tf_op jit(solution)/shard_map/ppermute | solution.py:215
  77.7 87.0 %collective-permute-start.10 = (bf16[5888,128]{1,0:T(8,128)(2,1)}, bf16[5888,128]{1,0:T(8,128)(2,1)S(1)}, u32[]{:S(2)}, u32[]{:S(2)}) collective-permute-start(bf16[5888,128]{1,0:T(8,128)(2,1)} %constant_dynamic-update-slice_fusion.3), channel_id=1, source_target_pairs={{0,1},{1,0},{2,3},{3,2},{4,5},{5,4},{6,7},{7,6},{8,9},{9,8},{10,11... | collective-permute-start | bytes 4521992 | tf_op jit(solution)/shard_map/ppermute | solution.py:30
  84.4 20.2 %collective-permute-start.6 = (bf16[1024,128]{1,0:T(8,128)(2,1)S(1)}, bf16[1024,128]{1,0:T(8,128)(2,1)S(1)}, u32[]{:S(2)}, u32[]{:S(2)}) collective-permute-start(bf16[1024,128]{1,0:T(8,128)(2,1)S(1)} %get-tuple-element.9), channel_id=1, source_target_pairs={{0,128},{1,129},{2,130},{3,131},{4,132},{5,133},{6,134},{7,135},{8... | collective-permute-start | bytes 786440 | tf_op jit(solution)/shard_map/ppermute | solution.py:214
  105.1 0.7 copy-start.4
  117.2 12.3 %collective-permute-start.15 = (bf16[4,256,128]{1,2,0:T(8,128)(2,1)S(1)}, bf16[4,256,128]{1,2,0:T(8,128)(2,1)S(1)}, u32[]{:S(2)}, u32[]{:S(2)}) collective-permute-start(bf16[4,256,128]{1,2,0:T(8,128)(2,1)S(1)} %all_to_all.10), channel_id=1, source_target_pairs={{0,28},{4,0},{8,4},{12,8},{16,12},{20,16},{24,20},{28,24},{1,29},{... | collective-permute-start | bytes 786440 | tf_op jit(solution)/shard_map/ppermute | solution.py:26
  124.3 8.6 %collective-permute-start.11 = (bf16[4,256,128]{1,2,0:T(8,128)(2,1)S(1)}, bf16[4,256,128]{1,2,0:T(8,128)(2,1)S(1)}, u32[]{:S(2)}, u32[]{:S(2)}) collective-permute-start(bf16[4,256,128]{1,2,0:T(8,128)(2,1)S(1)} %all_to_all.10), channel_id=1, source_target_pairs={{0,4},{4,8},{8,12},{12,16},{16,20},{20,24},{24,28},{28,0},{1,5},{5... | collective-permute-start | bytes 786440 | tf_op jit(solution)/shard_map/ppermute | solution.py:26
  129.5 7.7 %collective-permute-start.16 = (bf16[4,256,128]{1,2,0:T(8,128)(2,1)S(1)}, bf16[4,256,128]{1,2,0:T(8,128)(2,1)S(1)}, u32[]{:S(2)}, u32[]{:S(2)}) collective-permute-start(bf16[4,256,128]{1,2,0:T(8,128)(2,1)S(1)} %collective-permute-done.15), channel_id=1, source_target_pairs={{0,28},{4,0},{8,4},{12,8},{16,12},{20,16},{24,20},{28,24},{1,29},{... | collective-permute-start | bytes 786440 | tf_op jit(solution)/shard_map/ppermute | solution.py:26
  132.9 7.7 %collective-permute-start.12 = (bf16[4,256,128]{1,2,0:T(8,128)(2,1)S(1)}, bf16[4,256,128]{1,2,0:T(8,128)(2,1)S(1)}, u32[]{:S(2)}, u32[]{:S(2)}) collective-permute-start(bf16[4,256,128]{1,2,0:T(8,128)(2,1)S(1)} %collective-permute-done.11), channel_id=1, source_target_pairs={{0,4},{4,8},{8,12},{12,16},{16,20},{20,24},{24,28},{28,0},{1,5},{5... | collective-permute-start | bytes 786440 | tf_op jit(solution)/shard_map/ppermute | solution.py:26
  137.1 6.7 %collective-permute-start.17 = (bf16[4,256,128]{1,2,0:T(8,128)(2,1)S(1)}, bf16[4,256,128]{1,2,0:T(8,128)(2,1)S(1)}, u32[]{:S(2)}, u32[]{:S(2)}) collective-permute-start(bf16[4,256,128]{1,2,0:T(8,128)(2,1)S(1)} %collective-permute-done.16), channel_id=1, source_target_pairs={{0,28},{4,0},{8,4},{12,8},{16,12},{20,16},{24,20},{28,24},{1,29},{... | collective-permute-start | bytes 786440 | tf_op jit(solution)/shard_map/ppermute | solution.py:26
  140.6 6.8 %collective-permute-start.13 = (bf16[4,256,128]{1,2,0:T(8,128)(2,1)S(1)}, bf16[4,256,128]{1,2,0:T(8,128)(2,1)S(1)}, u32[]{:S(2)}, u32[]{:S(2)}) collective-permute-start(bf16[4,256,128]{1,2,0:T(8,128)(2,1)S(1)} %collective-permute-done.12), channel_id=1, source_target_pairs={{0,4},{4,8},{8,12},{12,16},{16,20},{20,24},{24,28},{28,0},{1,5},{5... | collective-permute-start | bytes 786440 | tf_op jit(solution)/shard_map/ppermute | solution.py:26
  143.9 19.9 %collective-permute-start.18 = (bf16[2,256,128]{1,2,0:T(8,128)(2,1)S(1)}, bf16[2,256,128]{1,2,0:T(8,128)(2,1)}, u32[]{:S(2)}, u32[]{:S(2)}) collective-permute-start(bf16[2,256,128]{1,2,0:T(8,128)(2,1)S(1)} %slice.113), channel_id=1, source_target_pairs={{0,28},{4,0},{8,4},{12,8},{16,12},{20,16},{24,20},{28,24},{1,29},{... | collective-permute-start | bytes 393224 | tf_op jit(solution)/shard_map/ppermute | solution.py:26
  148.1 15.7 %collective-permute-start.14 = (bf16[2,256,128]{1,2,0:T(8,128)(2,1)}, bf16[2,256,128]{1,2,0:T(8,128)(2,1)}, u32[]{:S(2)}, u32[]{:S(2)}) collective-permute-start(bf16[2,256,128]{1,2,0:T(8,128)(2,1)} %slice.112), channel_id=1, source_target_pairs={{0,4},{4,8},{8,12},{12,16},{16,20},{20,24},{24,28},{28,0},{1,5},{5... | collective-permute-start | bytes 393224 | tf_op jit(solution)/shard_map/ppermute | solution.py:26
  188.4 1.4 copy-start.2
  189.8 3.4 %copy-start.3 = (bf16[4,256,4,128]{3,2,1,0:T(4,128)(2,1)S(1)}, bf16[4,256,4,128]{3,2,1,0:T(4,128)(2,1)}, u32[]{:S(2)}) copy-start(bf16[4,256,4,128]{3,2,1,0:T(4,128)(2,1)} %reshape.137) | copy-start | bytes 3145732
Sparse Core Ops, SparseCore 0:
  15.9 110.2 all-gather.1

commit v3 on v2

--- a/solution.py
+++ b/solution.py
@@ -154,54 +154,148 @@
     )(flags, q, qs, kv0, kv1, kv2, k3, v3)
 
 
-def pick_rows(states, rows):
-    return jnp.concatenate([lax.dynamic_slice_in_dim(states, rows[i], 1, 0) for i in range(rows.shape[0])], axis=0)
-
-
 def cross_queries(z, parts, weights):
     total = 0.0
-    for back, part in enumerate(parts):
-        a = part.transpose(1, 0, 2).reshape(part.shape[1], -1)
+    for back, part in parts:
+        a = jnp.concatenate([part[h] for h in range(part.shape[0])], axis=1)
         w = lax.dynamic_index_in_dim(weights, (z + 8 - back) % 8, 0, keepdims=False)
         total = total + jnp.dot(a, w, preferred_element_type=F32)
-    return total.astype(BF)
-
-
-def cross(slots, gathered, wk4, wv4, queries):
-    picked = jnp.concatenate([lax.dynamic_slice_in_dim(gathered, slots[i], 1, 0) for i in range(slots.shape[0])], axis=0)
-    picked = picked.reshape(-1, picked.shape[2])
-    keys = jnp.dot(picked, wk4, preferred_element_type=F32).astype(BF).reshape(4, -1, 4, HD)
-    values = jnp.dot(picked, wv4, preferred_element_type=F32).astype(BF).reshape(4, -1, 4, HD)
-    q = queries.reshape(4, -1, 4, HD)
-    scores = jnp.einsum("cqhd,ckhd->chqk", q, keys, preferred_element_type=F32)
-    p = jnp.exp2((scores - jnp.max(scores, axis=3, keepdims=True)) * EXP2_SCALE)
-    total = jnp.sum(p, axis=3, keepdims=True)
-    o = jnp.einsum("chqk,ckhd->chqd", p.astype(BF), values, preferred_element_type=F32) / total
-    o = o.astype(BF).transpose(1, 0, 2, 3).reshape(4, -1, HD)
-    o = jnp.where(lax.axis_index("x_lo") == 1, jnp.concatenate([o[2:], o[:2]]), o)
-    return jnp.where(lax.axis_index("core") == 1, jnp.stack([o[1], o[0], o[3], o[2]]), o)
+    return total
+
+
+def project_kernel(s_ref, w_ref, out):
+    a = s_ref[...].reshape(-1, s_ref.shape[2])
+    out[...] = jnp.dot(a, w_ref[...], preferred_element_type=F32).astype(BF).reshape(out.shape)
+
+
+def project(slots, weights):
+    n, length, width = slots.shape
+    columns = weights.shape[1]
+    return pl.pallas_call(
+        project_kernel,
+        grid=(n // 2,),
+        in_specs=[
+            pl.BlockSpec((2, length, width), lambda i: (i, 0, 0)),
+            pl.BlockSpec(weights.shape, lambda i: (0, 0)),
+        ],
+        out_specs=pl.BlockSpec((2, length, columns), lambda i: (i, 0, 0)),
+        out_shape=jax.ShapeDtypeStruct((n, length, columns), BF),
+        compiler_params=params(24),
+        cost_estimate=pl.CostEstimate(flops=4 << 30, bytes_accessed=10 << 20, transcendentals=0),
+        name="project",
+    )(slots, weights)
+
+
+def cross_kernel(info, qa_ref, qb_ref, kva, kvb, o_ref, lse_ref, m_ref, l_ref, acc):
+    g = pl.program_id(0)
+    half = pl.num_programs(0) // 2
+    slots = kva.shape[0]
+    m_ref[...] = jnp.full_like(m_ref, LOW)
+    l_ref[...] = jnp.zeros_like(l_ref)
+    acc[...] = jnp.zeros_like(acc)
+    q = jnp.where(g < half, qa_ref[...], qb_ref[...])
+
+    def attend_slot(kv):
+        for r in range(4):
+            cut = slice(r * HD, (r + 1) * HD)
+            s = dot_t(q[:, cut], kv[:, cut])
+            before = m_ref[r]
+            now = jnp.maximum(before, jnp.max(s, axis=1, keepdims=True))
+            p = jnp.exp2((s - now) * EXP2_SCALE)
+            factor = jnp.exp2((before - now) * EXP2_SCALE)
+            m_ref[r] = now
+            l_ref[r] = l_ref[r] * factor + jnp.sum(p, axis=1, keepdims=True)
+            acc[r] = acc[r] * factor + jnp.dot(
+                p.astype(BF), kv[:, 4 * HD + r * HD : 4 * HD + (r + 1) * HD], preferred_element_type=F32
+            )
+
+    for n in range(2):
+        slot = info[2 * g + n]
+
+        @pl.when((slot >= 0) & (slot < slots))
+        def _():
+            attend_slot(kva[slot])
+
+        @pl.when(slot >= slots)
+        def _():
+            attend_slot(kvb[slot - slots])
+
+    lane = lax.broadcasted_iota(jnp.int32, acc.shape[1:], 1)
+    stats = jnp.full(acc.shape[1:], LOW, F32)
+    for r in range(4):
+        total = l_ref[r]
+        some = total > 0
+        safe = jnp.where(some, total, 1.0)
+        o_ref[r] = (acc[r] / safe).astype(BF)
+        stats = jnp.where((lane == r) & some, m_ref[r] * EXP2_SCALE + jnp.log2(safe), stats)
+    lse_ref[0] = stats.T[:8]
+
+
+def cross(info, queries_a, queries_b, kva, kvb):
+    groups = 8
+    group = queries_a.shape[0] // 4
+    width = queries_a.shape[1]
+    whole = pl.BlockSpec(kva.shape, lambda g, s: (0, 0, 0))
+    return pl.pallas_call(
+        cross_kernel,
+        grid_spec=pltpu.PrefetchScalarGridSpec(
+            num_scalar_prefetch=1,
+            grid=(groups,),
+            in_specs=[
+                pl.BlockSpec((group, width), lambda g, s: (jnp.minimum(g, 3), 0)),
+                pl.BlockSpec((group, width), lambda g, s: (jnp.maximum(g - 4, 0), 0)),
+                whole,
+                whole,
+            ],
+            out_specs=[
+                pl.BlockSpec((4, group, HD), lambda g, s: (0, g, 0)),
+                pl.BlockSpec((1, 8, group), lambda g, s: (g, 0, 0)),
+            ],
+            scratch_shapes=[
+                pltpu.VMEM((4, group, HD), F32),
+                pltpu.VMEM((4, group, HD), F32),
+                pltpu.VMEM((4, group, HD), F32),
+            ],
+        ),
+        out_shape=[
+            jax.ShapeDtypeStruct((4, groups * group, HD), BF),
+            jax.ShapeDtypeStruct((groups, 8, group), F32),
+        ],
+        compiler_params=params(40),
+        cost_estimate=pl.CostEstimate(flops=1 << 30, bytes_accessed=9 << 20, transcendentals=0),
+        name="cross",
+    )(info, queries_a, queries_b, kva, kvb)
+
+
+def merge(o_a, lse_a, o_b, lse_b):
+    top = jnp.maximum(lse_a, lse_b)
+    e_a = jnp.exp2(lse_a - top)
+    e_b = jnp.exp2(lse_b - top)
+    return ((o_a.astype(F32) * e_a + o_b.astype(F32) * e_b) / (e_a + e_b)).astype(BF)
 
 
 def local(q, k, v, states, nb_shard, nb_row, wk, wv, wq):
     rows = q.shape[0]
+    quarter = rows // 4
     y = lax.axis_index("y")
     z = lax.axis_index("z")
+    x_lo = lax.axis_index("x_lo")
+    core = lax.axis_index("core")
     late = lax.axis_index("x_hi") == 1
-    xc = lax.axis_index(XC)
     db_index = lax.axis_index(DB)
-    db_size = lax.axis_size(DB)
-
-    requests = nb_shard.size
-    capacity = 2 * ((requests + db_size - 1) // db_size)
-    shard_flat = nb_shard.reshape(requests)
-    row_flat = nb_row.reshape(requests)
-    same = shard_flat[:, None] == shard_flat[None, :]
-    earlier = jnp.arange(requests)[None, :] < jnp.arange(requests)[:, None]
-    rank = jnp.sum((same & earlier).astype(jnp.int32), axis=1)
-    picked = (shard_flat[None, :] == db_index) & (rank[None, :] == jnp.arange(capacity)[:, None])
-    slot_rows = jnp.sum(jnp.where(picked, row_flat[None, :], 0), axis=1)
-    slot_of = shard_flat * capacity + rank
-    gathered = lax.all_gather(pick_rows(states, slot_rows), DB, axis=0, tiled=True)
+
+    place = 2 * lax.broadcasted_iota(jnp.int32, nb_shard.shape, 0) + lax.broadcasted_iota(
+        jnp.int32, nb_shard.shape, 1
+    )
+    coded = place * states.shape[0] + nb_row
+    asked = nb_shard == db_index
+    none = nb_shard.size * states.shape[0]
+    first = jnp.min(jnp.where(asked, coded, none)) % states.shape[0]
+    last = jnp.max(jnp.where(asked, coded, 0)) % states.shape[0]
+    pair = jnp.concatenate(
+        [lax.dynamic_slice_in_dim(states, i, 1, 0) for i in (first, last)], axis=0
+    )
+    held_a = lax.all_gather(pair, "z", axis=0, tiled=True)
 
     kv0 = jnp.stack([k, v])
     kv1 = ring(kv0, "y", 1)
@@ -210,39 +304,73 @@
     k3 = ring(kv1[0], "y", 1)
     v3 = ring(kv2[1], "y", -1)
     flags = jnp.stack([~late, y >= 1, y >= 3, y >= 2]).astype(jnp.int32)
+    wall = jnp.concatenate([wq, wk, wv], axis=0)
+    half = wall.shape[0] // 2
+    w_up = ring(wall[:half], XX, -1)
+    w_down = ring(wall[half:], XX, 1)
     o, lse, o_sent, lse_sent = attend(flags, q, qs, kv0, kv1, kv2, k3, v3)
+
+    o_sent, lse_sent, w_up, w_down = lax.optimization_barrier((o_sent, lse_sent, w_up, w_down))
     o_back = lax.ppermute(o_sent, "x_hi", [(0, 1)])
     lse_back = lax.ppermute(lse_sent, "x_hi", [(0, 1)])
-    lse_own = lse.reshape(rows, 1)
-    lse_back = jnp.where(late, lse_back.reshape(rows, 1), LOW)
-    top = jnp.maximum(lse_own, lse_back)
-    e_own = jnp.exp2(lse_own - top)
-    e_back = jnp.exp2(lse_back - top)
-    self_out = ((o * e_own + o_back.astype(F32) * e_back) / (e_own + e_back)).astype(BF)
-
-    wall = jnp.concatenate([wq, wk, wv], axis=0)
-    half = wall.shape[0] // 2
-    w_x = jnp.concatenate([ring(wall[:half], XX, -1), ring(wall[half:], XX, 1)], axis=0)
+    w_x = jnp.concatenate([w_up, w_down], axis=0)
     w4 = jnp.concatenate([wall, swap(wall, "core"), w_x, swap(w_x, "core")], axis=1)
     depth, width = wq.shape[0], wk.shape[0]
     wq4 = w4[:depth].reshape(8, depth // 8, 4 * HD)
-    wk4 = w4[depth : depth + width]
-    wv4 = w4[depth + width :]
-
-    mine = lax.all_to_all(self_out.reshape(4, rows // 4, HD), XC, 0, 0)
+    wkv4 = jnp.concatenate([w4[depth : depth + width], w4[depth + width :]], axis=1)
+    o_back, lse_back, wq4, wkv4 = lax.optimization_barrier((o_back, lse_back, wq4, wkv4))
+
+    lse_back = jnp.where(late, lse_back.reshape(rows, 1), LOW)
+    self_out = merge(o, lse.reshape(rows, 1), o_back, lse_back)
+
+    mine = lax.all_to_all(self_out.reshape(4, quarter, HD), XC, 0, 0)
     f1 = ring(mine, "z", 1)
     b1 = ring(mine, "z", -1)
     f2 = ring(f1, "z", 1)
     b2 = ring(b1, "z", -1)
+    held_b = swap(held_a, "core")
     f3 = ring(f2, "z", 1)
     b3 = ring(b2, "z", -1)
-    far = jnp.concatenate([ring(f3[:2], "z", 1), ring(b3[2:], "z", -1)], axis=0)
-    queries = cross_queries(z, (mine, f1, f2, f3, far, b3, b2, b1), wq4)
-
-    per = requests // 4
-    slots = lax.dynamic_slice(slot_of, (xc * per,), (per,))
-    out = cross(slots, gathered, wk4, wv4, queries)
-    cross_out = lax.all_to_all(out, XC, 0, 0).reshape(rows, HD)
+    far_f = ring(f3[:2], "z", 1)
+    far_b = ring(b3[2:], "z", -1)
+    near = cross_queries(
+        z, ((0, mine), (1, f1), (2, f2), (3, f3), (5, b3), (6, b2), (7, b1)), wq4
+    )
+    kva = project(held_a, wkv4)
+    kvb = project(held_b, wkv4)
+    far_f, far_b, near, kva, kvb = lax.optimization_barrier((far_f, far_b, near, kva, kvb))
+    far = jnp.concatenate([far_f, far_b], axis=0)
+    queries = (near + cross_queries(z, ((4, far),), wq4)).astype(BF)
+
+    other = swap(queries, "x_lo")
+    other = jnp.concatenate([other[:, 2 * HD :], other[:, : 2 * HD]], axis=1)
+    same = nb_shard.reshape(-1)[:, None] == nb_shard.reshape(-1)[None, :]
+    n = nb_shard.size
+    before = lax.broadcasted_iota(jnp.int32, (n, n), 1) < lax.broadcasted_iota(jnp.int32, (n, n), 0)
+    rank = jnp.max((same & before).astype(jnp.int32), axis=1)
+    shard = nb_shard.reshape(-1)
+    slot = ((shard % 2) ^ core) * 16 + (shard // 4) * 2 + rank
+    slot = jnp.where((shard // 2) % 2 == x_lo, slot, -1).reshape(4, n // 4)
+    info = jnp.concatenate(
+        [
+            lax.dynamic_slice_in_dim(slot, 2 * x_lo + core, 1, 0),
+            lax.dynamic_slice_in_dim(slot, 2 * (1 - x_lo) + core, 1, 0),
+        ],
+        axis=1,
+    ).reshape(-1)
+    o, lse = cross(info, queries, other, kva, kvb)
+
+    lse = lse[:, :4].transpose(1, 0, 2).reshape(4, 2, 2 * HD)
+    o_got = swap(o[2:], "x_lo").reshape(2, 2, quarter, HD)[:, ::-1]
+    lse_got = swap(lse[2:], "x_lo")[:, ::-1]
+    both = merge(
+        o[:2].reshape(2, 2, quarter, HD), lse[:2][..., None], o_got, lse_got[..., None]
+    )
+    kept, got = both[0], swap(both[1], "core")
+    kept, got = (jnp.where(x_lo == 0, a, a[::-1]) for a in (kept, got))
+    cross_out = jnp.where(
+        core == 0, jnp.stack([kept, got], axis=1), jnp.stack([got, kept], axis=1)
+    ).reshape(rows, HD)
     return (self_out, cross_out)
 
 

time: 217 us -> 186 us (0.86); the launches traced: 214 us -> 187 us
  Pallas kernels: 17.5 us -> 41.1 us
  blocking collectives: 21.9 us -> 0 us
  between operations: 33.3 us -> 18.6 us
  matrix products: 12.8 us -> 4.53 us
  starting transfers between devices: 34.9 us -> 42.7 us
  local copies, waits for them, and re-layouts: 26.5 us -> 18.9 us
  waiting for transfers between devices: 58.8 us -> 52.2 us
    pallas_call x0 -> x3, Pallas kernels: none -> 23.7 us  [the longest x2 13.5 us: project(): pl.pallas_call(project_kernel, grid=(n // 2,), in_specs=[pl.BlockSpec((2,...]
    all_to_all x2 -> x0, blocking collectives: 21.9 us -> none  [the longest x1 11.2 us: local(): mine = lax.all_to_all(self_out.reshape(4, rows // 4, HD), XC, 0, 0)]
    ppermute x14, waiting for transfers between devices: 39.9 us -> 22.3 us  [ring(): return lax.ppermute(value, axis, [(i, (i + step) % n) for i in range(n)])]
    ppermute x1, waiting for transfers between devices: 15.8 us -> 0.01 us  [local(): o_back = lax.ppermute(o_sent, 'x_hi', [(0, 1)])]
    ppermute x1, waiting for transfers between devices: 3.12 us -> 17.1 us  [local(): lse_back = lax.ppermute(lse_sent, 'x_hi', [(0, 1)])]
    dot_general x4 -> x0, matrix products: 10.2 us -> none  [the longest x1 3.37 us: cross(): jnp.dot(picked, wv4, preferred_element_type=F32).astype(BF)]
    ppermute x2 -> x7, waiting for transfers between devices: 0.01 us -> 9.98 us  [swap(): return lax.ppermute(value, axis, [(0, 1), (1, 0)])]
    ppermute x2 -> x7, starting transfers between devices: 8.2 us -> 15.3 us  [swap(): return lax.ppermute(value, axis, [(0, 1), (1, 0)])]
  transfers between devices with their start and end apart: 20 -> 26, of which waited for: 9 -> 12; matrix products, arithmetic and copies ran while one was open for 8% -> 9% of each run, Pallas kernels for 8% -> 17%
where the time goes in v3:
time: 186 us; the launch traced here: 187 us
  waiting for transfers between devices  52.2 us (28%)
  starting transfers between devices  42.7 us (23%)
  Pallas kernels  41.1 us (22%)
  local copies, waits for them, and re-layouts  18.9 us (10%)
  between operations  18.6 us (10%)
  other arithmetic  8.42 us (5%)
  matrix products  4.53 us (2%)
    ppermute x14, waiting for transfers between devices, ring(): return lax.ppermute(value, axis, [(i, (i + step) % n) for i in range(n)])  22.3 us
    ppermute x14, starting transfers between devices, ring(): return lax.ppermute(value, axis, [(i, (i + step) % n) for i in range(n)])  18.3 us
    pallas_call x1, Pallas kernels, attend(): pl.pallas_call(functools.partial(attend_kernel, tile), grid_spec=pltpu.Pr...  17.5 us
    ppermute x1, waiting for transfers between devices, local(): lse_back = lax.ppermute(lse_sent, 'x_hi', [(0, 1)])  17.1 us
    ppermute x7, starting transfers between devices, swap(): return lax.ppermute(value, axis, [(0, 1), (1, 0)])  15.3 us
    pallas_call x2, Pallas kernels, project(): pl.pallas_call(project_kernel, grid=(n // 2,), in_specs=[pl.BlockSpec((2,...  13.5 us
    pallas_call x1, Pallas kernels, cross(): pl.pallas_call(cross_kernel, grid_spec=pltpu.PrefetchScalarGridSpec(num_s...  10.2 us
    ppermute x7, waiting for transfers between devices, swap(): return lax.ppermute(value, axis, [(0, 1), (1, 0)])  9.98 us
  transfers between devices with their start and end apart: 26, of which 12 were waited for; matrix products, arithmetic and copies ran while one was open for 9% of the time, Pallas kernels for 17%

profile of v3, /device:TPU:31, one launch (start us, length us, event | category | flops | bytes accessed | tf_op | source)
XLA Modules:
  0.0 186.5 jit_solution(1712577188246050477)
XLA Ops:
  7.3 1.4 select_reduce_fusion.1
  12.6 1.1 constant_dynamic-slice_fusion.1
  13.7 0.9 pad_maximum_fusion.8
  14.6 1.1 pad_maximum_fusion.7.kv0
  15.8 1.5 collective-permute-start.2
  17.3 3.0 %collective-permute-start = (bf16[1024,128]{1,0:T(8,128)(2,1)}, bf16[1024,128]{1,0:T(8,128)(2,1)S(1)}, u32[]{:S(2)}, u32[]{:S(2)}) collective-permute-start(bf16[1024,128]{1,0:T(8,128)(2,1)} %q_ref.1), channel_id=1, source_target_pairs={{128,0},{129,1},{130,2},{131,3},{132,4},{133,5},{134,6},{135,7},{1... | collective-permute-start | bytes 786440 | tf_op jit(solution)/shard_map/ppermute | solution.py:303
  20.5 1.0 slice.207
  21.5 0.9 slice.156
  22.4 1.5 collective-permute-start.5
  23.9 4.7 %collective-permute-done.1.kv1 = bf16[2,1024,128]{2,1,0:T(8,128)(2,1)S(1)} collective-permute-done((bf16[2,1024,128]{2,1,0:T(8,128)(2,1)S(1)}, bf16[2,1024,128]{2,1,0:T(8,128)(2,1)S(1)}, u32[]{:S(2)}, u32[]{:S(2)}) %collective-permute-start.1) | collective-permute-done | bytes 524320 | tf_op jit(solution)/shard_map/ppermute | solution.py:26
  29.3 1.3 collective-permute-start.3
  31.6 2.1 %collective-permute-start.9 = (bf16[5888,128]{1,0:T(8,128)(2,1)}, bf16[5888,128]{1,0:T(8,128)(2,1)S(1)}, u32[]{:S(2)}, u32[]{:S(2)}) collective-permute-start(bf16[5888,128]{1,0:T(8,128)(2,1)} %copy-done.6), channel_id=1, source_target_pairs={{0,1},{1,0},{2,3},{3,2},{4,5},{5,4},{6,7},{7,6},{8,9},{9,8},{10,11... | collective-permute-start | bytes 4521992 | tf_op jit(solution)/shard_map/ppermute | solution.py:30
  33.7 2.2 %collective-permute-done.3.k3 = bf16[1024,128]{1,0:T(8,128)(2,1)S(1)} collective-permute-done((bf16[1024,128]{1,0:T(8,128)(2,1)}, bf16[1024,128]{1,0:T(8,128)(2,1)S(1)}, u32[]{:S(2)}, u32[]{:S(2)}) %collective-permute-start.3) | collective-permute-done | bytes 262176 | tf_op jit(solution)/shard_map/ppermute | solution.py:26
  35.9 3.0 %collective-permute-done.4.v3 = bf16[1024,128]{1,0:T(8,128)(2,1)S(1)} collective-permute-done((bf16[1024,128]{1,0:T(8,128)(2,1)}, bf16[1024,128]{1,0:T(8,128)(2,1)S(1)}, u32[]{:S(2)}, u32[]{:S(2)}) %collective-permute-start.4) | collective-permute-done | bytes 262176 | tf_op jit(solution)/shard_map/ppermute | solution.py:26
  38.9 17.5 %attend.1 = (f32[1024,128]{1,0:T(8,128)S(1)}, f32[4,1,256]{2,1,0:T(1,128)S(1)}, bf16[1024,128]{1,0:T(8,128)(2,1)S(1)}, f32[4,1,256]{2,1,0:T(1,128)S(1)}) custom-call(s32[4]{0:T(128)S(1)} %add_convert_fusion.1.flags, bf16[1024,128]{1,0:T(8,128)(2,1)S(1)} %copy-done.5, bf16[1024,128]{1,0:T(8,128)(2,1)S(1)} %collective-permute-done.qs_ref, ...), custom_call_target="tpu_custom_call" | custom-call | flops 3221225472 | bytes 4194304 | tf_op jit(solution)/shard_map/attend/pallas_call | solution.py:118
  56.5 1.3 constant_dynamic-update-slice_fusion.3
  57.8 2.7 %collective-permute-start.10 = (bf16[5888,128]{1,0:T(8,128)(2,1)S(1)}, bf16[5888,128]{1,0:T(8,128)(2,1)S(1)}, u32[]{:S(2)}, u32[]{:S(2)}) collective-permute-start(bf16[5888,128]{1,0:T(8,128)(2,1)S(1)} %constant_dynamic-update-slice_fusion.3), channel_id=1, source_target_pairs={{0,1},{1,0},{2,3},{3,2},{4,5},{5,4},{6,7},{7,6},{8,9},{9,8},{10,11... | collective-permute-start | bytes 4521992 | tf_op jit(solution)/shard_map/ppermute | solution.py:30
  60.5 1.3 collective-permute-start.7
  61.8 1.3 collective-permute-start.8
  64.1 2.1 %fusion.w_ref = bf16[896,1024]{1,0:T(8,128)(2,1)S(1)} fusion(bf16[5888,128]{1,0:T(8,128)(2,1)S(1)} %collective-permute-done.10, bf16[5888,128]{1,0:T(8,128)(2,1)S(1)} %constant_dynamic-update-slice_fusion.3, bf16[5888,128]{1,0:T(8,128)(2,1)S(1)} %collective-permute-done.9, bf16[5888,128]{1,0:T(8,128)(2,1)S(1)} %copy-done.7), kind=kLoop, calls=%fused_computation.2 | loop fusion | flops 14680064 | bytes 7864320 | tf_op jit(solution)/shard_map/concatenate | solution.py:320
  66.2 2.2 %slice.208 = bf16[4096,512]{1,0:T(8,128)(2,1)} slice(bf16[5888,512]{1,0:T(8,128)(2,1)S(1)} %pad_maximum_fusion), slice={[0:4096], [0:512]} | slice | bytes 8388608 | tf_op jit(solution)/shard_map/slice | solution.py:319
  68.4 17.1 %collective-permute-done.8 = f32[4,1,256]{2,1,0:T(1,128)S(1)} collective-permute-done((f32[4,1,256]{2,1,0:T(1,128)S(1)}, f32[4,1,256]{2,1,0:T(1,128)S(1)}, u32[]{:S(2)}, u32[]{:S(2)}) %collective-permute-start.8) | collective-permute-done | bytes 4128 | tf_op jit(solution)/shard_map/ppermute | solution.py:315
  85.6 1.2 divide_convert_fusion
  86.8 3.5 %all-to-all-start = ((bf16[4,256,128]{2,1,0:T(8,128)(2,1)}), bf16[4,256,128]{2,1,0:T(8,128)(2,1)S(1)}, u32[]{:S(2)}, u32[]{:S(2)}) async-start(bf16[4,256,128]{2,1,0:T(8,128)(2,1)} %bitcast.12), calls=%async_computation | async-start | bytes 524288 | tf_op jit(solution)/shard_map/all_to_all | solution.py:326
  91.7 2.8 %all-to-all-done = bf16[4,256,128]{2,1,0:T(8,128)(2,1)S(1)} async-done(((bf16[4,256,128]{2,1,0:T(8,128)(2,1)}), bf16[4,256,128]{2,1,0:T(8,128)(2,1)S(1)}, u32[]{:S(2)}, u32[]{:S(2)}) %all-to-all-start) | async-done | bytes 262176 | tf_op jit(solution)/shard_map/all_to_all | solution.py:326
  94.5 1.7 collective-permute-start.11
  96.2 3.9 %collective-permute-start.15 = (bf16[4,256,128]{2,1,0:T(8,128)(2,1)S(1)}, bf16[4,256,128]{2,1,0:T(8,128)(2,1)S(1)}, u32[]{:S(2)}, u32[]{:S(2)}) collective-permute-start(bf16[4,256,128]{2,1,0:T(8,128)(2,1)S(1)} %all-to-all-done), channel_id=1, source_target_pairs={{0,28},{4,0},{8,4},{12,8},{16,12},{20,16},{24,20},{28,24},{1,29},{... | collective-permute-start | bytes 786440 | tf_op jit(solution)/shard_map/ppermute | solution.py:26
  100.2 1.3 fusion.12
  101.5 4.7 %collective-permute-done.11 = bf16[4,256,128]{2,1,0:T(8,128)(2,1)S(1)} collective-permute-done((bf16[4,256,128]{2,1,0:T(8,128)(2,1)S(1)}, bf16[4,256,128]{2,1,0:T(8,128)(2,1)S(1)}, u32[]{:S(2)}, u32[]{:S(2)}) %collective-permute-start.11) | collective-permute-done | bytes 262176 | tf_op jit(solution)/shard_map/ppermute | solution.py:26
  106.3 2.7 %collective-permute-start.16 = (bf16[4,256,128]{2,1,0:T(8,128)(2,1)S(1)}, bf16[4,256,128]{2,1,0:T(8,128)(2,1)S(1)}, u32[]{:S(2)}, u32[]{:S(2)}) collective-permute-start(bf16[4,256,128]{2,1,0:T(8,128)(2,1)S(1)} %collective-permute-done.15), channel_id=1, source_target_pairs={{0,28},{4,0},{8,4},{12,8},{16,12},{20,16},{24,20},{28,24},{1,29},{... | collective-permute-start | bytes 786440 | tf_op jit(solution)/shard_map/ppermute | solution.py:26
  109.0 1.4 convolution_add_fusion.5
  110.3 3.8 %collective-permute-done.12 = bf16[4,256,128]{2,1,0:T(8,128)(2,1)S(1)} collective-permute-done((bf16[4,256,128]{2,1,0:T(8,128)(2,1)S(1)}, bf16[4,256,128]{2,1,0:T(8,128)(2,1)S(1)}, u32[]{:S(2)}, u32[]{:S(2)}) %collective-permute-start.12) | collective-permute-done | bytes 262176 | tf_op jit(solution)/shard_map/ppermute | solution.py:26
  114.1 2.7 %collective-permute-start.17 = (bf16[4,256,128]{2,1,0:T(8,128)(2,1)S(1)}, bf16[4,256,128]{2,1,0:T(8,128)(2,1)S(1)}, u32[]{:S(2)}, u32[]{:S(2)}) collective-permute-start(bf16[4,256,128]{2,1,0:T(8,128)(2,1)S(1)} %collective-permute-done.16), channel_id=1, source_target_pairs={{0,28},{4,0},{8,4},{12,8},{16,12},{20,16},{24,20},{28,24},{1,29},{... | collective-permute-start | bytes 786440 | tf_op jit(solution)/shard_map/ppermute | solution.py:26
  117.2 3.9 %collective-permute-done.13 = bf16[4,256,128]{2,1,0:T(8,128)(2,1)S(1)} collective-permute-done((bf16[4,256,128]{2,1,0:T(8,128)(2,1)S(1)}, bf16[4,256,128]{2,1,0:T(8,128)(2,1)S(1)}, u32[]{:S(2)}, u32[]{:S(2)}) %collective-permute-start.13) | collective-permute-done | bytes 262176 | tf_op jit(solution)/shard_map/ppermute | solution.py:26
  121.2 2.7 %collective-permute-start.18 = (bf16[2,256,128]{2,1,0:T(8,128)(2,1)S(1)}, bf16[2,256,128]{2,1,0:T(8,128)(2,1)S(1)}, u32[]{:S(2)}, u32[]{:S(2)}) collective-permute-start(bf16[2,256,128]{2,1,0:T(8,128)(2,1)S(1)} %slice.210), channel_id=1, source_target_pairs={{0,28},{4,0},{8,4},{12,8},{16,12},{20,16},{24,20},{28,24},{1,29},{... | collective-permute-start | bytes 393224 | tf_op jit(solution)/shard_map/ppermute | solution.py:26
  125.2 0.8 copy-done.4
  126.0 5.7 %project.2.kva = bf16[16,128,1024]{2,1,0:T(8,128)(2,1)S(1)} custom-call(bf16[16,128,896]{2,1,0:T(8,128)(2,1)S(1)} %copy-done.4, bf16[896,1024]{1,0:T(8,128)(2,1)S(1)} %fusion.w_ref), custom_call_target="tpu_custom_call" | custom-call | flops 4294967296 | bytes 10485760 | tf_op jit(solution)/shard_map/project/pallas_call | solution.py:174
  131.7 2.0 %copy-done = bf16[16,128,1024]{2,1,0:T(8,128)(2,1)} copy-done((bf16[16,128,1024]{2,1,0:T(8,128)(2,1)}, bf16[16,128,1024]{2,1,0:T(8,128)(2,1)S(1)}, u32[]{:S(2)}) %copy-start) | copy-done | bytes 4194328
  133.7 7.8 %project.3.kvb = bf16[16,128,1024]{2,1,0:T(8,128)(2,1)S(1)} custom-call(bf16[16,128,896]{2,1,0:T(8,128)(2,1)} %collective-permute-done.19.s_ref, bf16[896,1024]{1,0:T(8,128)(2,1)S(1)} %fusion.w_ref), custom_call_target="tpu_custom_call" | custom-call | flops 4294967296 | bytes 10485760 | tf_op jit(solution)/shard_map/project/pallas_call | solution.py:174
  141.5 2.0 %copy-done.2 = bf16[16,128,1024]{2,1,0:T(8,128)(2,1)} copy-done((bf16[16,128,1024]{2,1,0:T(8,128)(2,1)}, bf16[16,128,1024]{2,1,0:T(8,128)(2,1)S(1)}, u32[]{:S(2)}) %copy-start.2) | copy-done | bytes 4194328
  144.1 5.1 %collective-permute-done.20 = bf16[256,512]{1,0:T(8,128)(2,1)S(1)} collective-permute-done((bf16[256,512]{1,0:T(8,128)(2,1)S(1)}, bf16[256,512]{1,0:T(8,128)(2,1)S(1)}, u32[]{:S(2)}, u32[]{:S(2)}) %collective-permute-start.20) | collective-permute-done | bytes 262176 | tf_op jit(solution)/shard_map/ppermute | solution.py:30
  149.3 2.2 %copy-done.1 = bf16[16,128,1024]{2,1,0:T(8,128)(2,1)S(1)} copy-done((bf16[16,128,1024]{2,1,0:T(8,128)(2,1)S(1)}, bf16[16,128,1024]{2,1,0:T(8,128)(2,1)}, u32[]{:S(2)}) %copy-start.1) | copy-done | bytes 4194328
  151.5 2.2 %copy-done.3 = bf16[16,128,1024]{2,1,0:T(8,128)(2,1)S(1)} copy-done((bf16[16,128,1024]{2,1,0:T(8,128)(2,1)S(1)}, bf16[16,128,1024]{2,1,0:T(8,128)(2,1)}, u32[]{:S(2)}) %copy-start.3) | copy-done | bytes 4194328
  153.6 10.2 %cross.1 = (bf16[4,512,128]{2,1,0:T(8,128)(2,1)S(1)}, f32[8,8,64]{2,1,0:T(8,128)S(1)}) custom-call(s32[16]{0:T(128)S(1)} %add_bitcast_fusion.info, bf16[256,512]{1,0:T(8,128)(2,1)S(1)} %add_convert_fusion.qa_ref, bf16[256,512]{1,0:T(8,128)(2,1)S(1)} %pad_maximum_fusion.9.qb_ref, bf16[16,128,1024]{2,1,0:T(8,128)(2,1)S(1)} %copy-done.1, ...), custom_call_target="tpu_custom_call" | custom-call | flops 1073741824 | bytes 9437184 | tf_op jit(solution)/shard_map/cross/pallas_call | solution.py:239
  164.1 1.5 collective-permute-start.21
  165.6 3.6 %collective-permute-done.21 = f32[2,2,256]{2,1,0:T(2,128)S(1)} collective-permute-done((f32[2,2,256]{2,1,0:T(2,128)S(1)}, f32[2,2,256]{2,1,0:T(2,128)S(1)}, u32[]{:S(2)}, u32[]{:S(2)}) %collective-permute-start.21) | collective-permute-done | bytes 4128 | tf_op jit(solution)/shard_map/ppermute | solution.py:30
  169.8 8.1 %collective-permute-start.23 = (bf16[2,256,128]{2,1,0:T(8,128)(2,1)S(1)}, bf16[2,256,128]{2,1,0:T(8,128)(2,1)S(1)}, u32[]{:S(2)}, u32[]{:S(2)}) collective-permute-start(bf16[2,256,128]{2,1,0:T(8,128)(2,1)S(1)} %get-tuple-element.53), channel_id=1, source_target_pairs={{0,1},{1,0},{2,3},{3,2},{4,5},{5,4},{6,7},{7,6},{8,9},{9,8},{10,11... | collective-permute-start | bytes 393224 | tf_op jit(solution)/shard_map/ppermute | solution.py:30
  177.9 1.0 collective-permute-done.23
  (100 shorter events, 8.6 us)
Async XLA Ops:
  7.2 13.1 %copy-start.9 = (bf16[4096,128]{1,0:T(8,128)(2,1)S(1)}, bf16[4096,128]{1,0:T(8,128)(2,1)}, u32[]{:S(2)}) copy-start(bf16[4096,128]{1,0:T(8,128)(2,1)} %param.17) | copy-start | bytes 3145732
  7.2 13.2 %copy-start.10 = (bf16[896,128]{1,0:T(8,128)(2,1)S(1)}, bf16[896,128]{1,0:T(8,128)(2,1)}, u32[]{:S(2)}) copy-start(bf16[896,128]{1,0:T(8,128)(2,1)} %param.15) | copy-start | bytes 688132
  7.2 83.3 %all-gather.2.cloned.1.call-start = ((), (), s32[]{:S(2)}) async-start(), calls=%async_computation.1 | async-start | bytes 4128768 | tf_op jit(solution)/shard_map/all_gather | solution.py:298
  14.6 5.9 %copy-start.11 = (bf16[896,128]{1,0:T(8,128)(2,1)S(1)}, bf16[896,128]{1,0:T(8,128)(2,1)}, u32[]{:S(2)}) copy-start(bf16[896,128]{1,0:T(8,128)(2,1)} %param.16) | copy-start | bytes 688132
  15.7 23.2 %copy-start.5 = (bf16[1024,128]{1,0:T(8,128)(2,1)S(1)}, bf16[1024,128]{1,0:T(8,128)(2,1)}, u32[]{:S(2)}) copy-start(bf16[1024,128]{1,0:T(8,128)(2,1)} %q_ref.1) | copy-start | bytes 786436
  15.7 12.9 %collective-permute-start.1 = (bf16[2,1024,128]{2,1,0:T(8,128)(2,1)S(1)}, bf16[2,1024,128]{2,1,0:T(8,128)(2,1)S(1)}, u32[]{:S(2)}, u32[]{:S(2)}) collective-permute-start(bf16[2,1024,128]{2,1,0:T(8,128)(2,1)S(1)} %pad_maximum_fusion.7.kv0), channel_id=1, source_target_pairs={{0,32},{32,64},{64,96},{96,0},{1,33},{33,65},{65,97},{97,1},{2,34}... | collective-permute-start | bytes 1572872 | tf_op jit(solution)/shard_map/ppermute | solution.py:26
  15.8 14.8 %collective-permute-start.2 = (bf16[2,1024,128]{2,1,0:T(8,128)(2,1)S(1)}, bf16[2,1024,128]{2,1,0:T(8,128)(2,1)S(1)}, u32[]{:S(2)}, u32[]{:S(2)}) collective-permute-start(bf16[2,1024,128]{2,1,0:T(8,128)(2,1)S(1)} %pad_maximum_fusion.7.kv0), channel_id=1, source_target_pairs={{0,96},{32,0},{64,32},{96,64},{1,97},{33,1},{65,33},{97,65},{2,98}... | collective-permute-start | bytes 1572872 | tf_op jit(solution)/shard_map/ppermute | solution.py:26
  17.3 14.3 %collective-permute-start = (bf16[1024,128]{1,0:T(8,128)(2,1)}, bf16[1024,128]{1,0:T(8,128)(2,1)S(1)}, u32[]{:S(2)}, u32[]{:S(2)}) collective-permute-start(bf16[1024,128]{1,0:T(8,128)(2,1)} %q_ref.1), channel_id=1, source_target_pairs={{128,0},{129,1},{130,2},{131,3},{132,4},{133,5},{134,6},{135,7},{1... | collective-permute-start | bytes 786440 | tf_op jit(solution)/shard_map/ppermute | solution.py:303
  20.5 10.1 %copy-start.6 = (bf16[5888,128]{1,0:T(8,128)(2,1)}, bf16[5888,128]{1,0:T(8,128)(2,1)S(1)}, u32[]{:S(2)}) copy-start(bf16[5888,128]{1,0:T(8,128)(2,1)S(1)} %constant_dynamic-update-slice_fusion) | copy-start | bytes 4521988
  21.5 34.9 %collective-permute-start.6 = (bf16[2944,128]{1,0:T(8,128)(2,1)}, bf16[2944,128]{1,0:T(8,128)(2,1)}, u32[]{:S(2)}, u32[]{:S(2)}) collective-permute-start(bf16[2944,128]{1,0:T(8,128)(2,1)} %slice.207), channel_id=1, source_target_pairs={{0,2},{2,128},{128,130},{130,0},{1,3},{3,129},{129,131},{131,1},{4... | collective-permute-start | bytes 2261000 | tf_op jit(solution)/shard_map/ppermute | solution.py:26
  22.4 34.0 %collective-permute-start.5 = (bf16[2944,128]{1,0:T(8,128)(2,1)}, bf16[2944,128]{1,0:T(8,128)(2,1)S(1)}, u32[]{:S(2)}, u32[]{:S(2)}) collective-permute-start(bf16[2944,128]{1,0:T(8,128)(2,1)} %slice.156), channel_id=1, source_target_pairs={{0,130},{2,0},{128,2},{130,128},{1,131},{3,1},{129,3},{131,129},{4... | collective-permute-start | bytes 2261000 | tf_op jit(solution)/shard_map/ppermute | solution.py:26
  29.3 6.6 %collective-permute-start.3 = (bf16[1024,128]{1,0:T(8,128)(2,1)}, bf16[1024,128]{1,0:T(8,128)(2,1)S(1)}, u32[]{:S(2)}, u32[]{:S(2)}) collective-permute-start(bf16[1024,128]{1,0:T(8,128)(2,1)} %slice_bitcast_fusion.1), channel_id=1, source_target_pairs={{0,32},{32,64},{64,96},{96,0},{1,33},{33,65},{65,97},{97,1},{2,34}... | collective-permute-start | bytes 786440 | tf_op jit(solution)/shard_map/ppermute | solution.py:26
  31.3 7.6 %collective-permute-start.4 = (bf16[1024,128]{1,0:T(8,128)(2,1)}, bf16[1024,128]{1,0:T(8,128)(2,1)S(1)}, u32[]{:S(2)}, u32[]{:S(2)}) collective-permute-start(bf16[1024,128]{1,0:T(8,128)(2,1)} %slice_bitcast_fusion), channel_id=1, source_target_pairs={{0,96},{32,0},{64,32},{96,64},{1,97},{33,1},{65,33},{97,65},{2,98}... | collective-permute-start | bytes 786440 | tf_op jit(solution)/shard_map/ppermute | solution.py:26
  31.6 31.5 %collective-permute-start.9 = (bf16[5888,128]{1,0:T(8,128)(2,1)}, bf16[5888,128]{1,0:T(8,128)(2,1)S(1)}, u32[]{:S(2)}, u32[]{:S(2)}) collective-permute-start(bf16[5888,128]{1,0:T(8,128)(2,1)} %copy-done.6), channel_id=1, source_target_pairs={{0,1},{1,0},{2,3},{3,2},{4,5},{5,4},{6,7},{7,6},{8,9},{9,8},{10,11... | collective-permute-start | bytes 4521992 | tf_op jit(solution)/shard_map/ppermute | solution.py:30
  56.4 7.0 %copy-start.7 = (bf16[5888,128]{1,0:T(8,128)(2,1)S(1)}, bf16[5888,128]{1,0:T(8,128)(2,1)}, u32[]{:S(2)}) copy-start(bf16[5888,128]{1,0:T(8,128)(2,1)} %copy-done.6) | copy-start | bytes 4521988
  57.8 5.6 %collective-permute-start.10 = (bf16[5888,128]{1,0:T(8,128)(2,1)S(1)}, bf16[5888,128]{1,0:T(8,128)(2,1)S(1)}, u32[]{:S(2)}, u32[]{:S(2)}) collective-permute-start(bf16[5888,128]{1,0:T(8,128)(2,1)S(1)} %constant_dynamic-update-slice_fusion.3), channel_id=1, source_target_pairs={{0,1},{1,0},{2,3},{3,2},{4,5},{5,4},{6,7},{7,6},{8,9},{9,8},{10,11... | collective-permute-start | bytes 4521992 | tf_op jit(solution)/shard_map/ppermute | solution.py:30
  60.5 25.1 %collective-permute-start.7 = (bf16[1024,128]{1,0:T(8,128)(2,1)S(1)}, bf16[1024,128]{1,0:T(8,128)(2,1)S(1)}, u32[]{:S(2)}, u32[]{:S(2)}) collective-permute-start(bf16[1024,128]{1,0:T(8,128)(2,1)S(1)} %get-tuple-element.25), channel_id=1, source_target_pairs={{0,128},{1,129},{2,130},{3,131},{4,132},{5,133},{6,134},{7,135},{8... | collective-permute-start | bytes 786440 | tf_op jit(solution)/shard_map/ppermute | solution.py:314
  61.8 23.8 %collective-permute-start.8 = (f32[4,1,256]{2,1,0:T(1,128)S(1)}, f32[4,1,256]{2,1,0:T(1,128)S(1)}, u32[]{:S(2)}, u32[]{:S(2)}) collective-permute-start(f32[4,1,256]{2,1,0:T(1,128)S(1)} %get-tuple-element.26), channel_id=1, source_target_pairs={{0,128},{1,129},{2,130},{3,131},{4,132},{5,133},{6,134},{7,135},{8... | collective-permute-start | bytes 12296 | tf_op jit(solution)/shard_map/ppermute | solution.py:315
  66.2 24.1 %copy-start.12 = (s32[16,2]{0,1:T(2,128)S(1)}, s32[16,2]{0,1:T(2,128)}, u32[]{:S(2)}) copy-start(s32[16,2]{0,1:T(2,128)} %param.13) | copy-start | bytes 388
  86.8 7.7 %all-to-all-start = ((bf16[4,256,128]{2,1,0:T(8,128)(2,1)}), bf16[4,256,128]{2,1,0:T(8,128)(2,1)S(1)}, u32[]{:S(2)}, u32[]{:S(2)}) async-start(bf16[4,256,128]{2,1,0:T(8,128)(2,1)} %bitcast.12), calls=%async_computation | async-start | bytes 524288 | tf_op jit(solution)/shard_map/all_to_all | solution.py:326
  90.5 43.2 %collective-permute-start.19 = (bf16[16,128,896]{2,1,0:T(8,128)(2,1)}, bf16[16,128,896]{2,1,0:T(8,128)(2,1)}, u32[]{:S(2)}, u32[]{:S(2)}) collective-permute-start(bf16[16,128,896]{2,1,0:T(8,128)(2,1)} %all-gather.2.cloned.1.call-done.s_ref), channel_id=1, source_target_pairs={{0,1},{1,0},{2,3},{3,2},{4,5},{5,4},{6,7},{7,6},{8,9},{9,8},{10,11... | collective-permute-start | bytes 11010056 | tf_op jit(solution)/shard_map/ppermute | solution.py:30
  94.5 22.4 %copy-start.8 = (bf16[4096,512]{1,0:T(8,128)(2,1)S(1)}, bf16[4096,512]{1,0:T(8,128)(2,1)}, u32[]{:S(2)}) copy-start(bf16[4096,512]{1,0:T(8,128)(2,1)} %slice.208) | copy-start | bytes 12582916
  94.5 11.8 %collective-permute-start.11 = (bf16[4,256,128]{2,1,0:T(8,128)(2,1)S(1)}, bf16[4,256,128]{2,1,0:T(8,128)(2,1)S(1)}, u32[]{:S(2)}, u32[]{:S(2)}) collective-permute-start(bf16[4,256,128]{2,1,0:T(8,128)(2,1)S(1)} %all-to-all-done), channel_id=1, source_target_pairs={{0,4},{4,8},{8,12},{12,16},{16,20},{20,24},{24,28},{28,0},{1,5},{5... | collective-permute-start | bytes 786440 | tf_op jit(solution)/shard_map/ppermute | solution.py:26
  96.2 10.1 %collective-permute-start.15 = (bf16[4,256,128]{2,1,0:T(8,128)(2,1)S(1)}, bf16[4,256,128]{2,1,0:T(8,128)(2,1)S(1)}, u32[]{:S(2)}, u32[]{:S(2)}) collective-permute-start(bf16[4,256,128]{2,1,0:T(8,128)(2,1)S(1)} %all-to-all-done), channel_id=1, source_target_pairs={{0,28},{4,0},{8,4},{12,8},{16,12},{20,16},{24,20},{28,24},{1,29},{... | collective-permute-start | bytes 786440 | tf_op jit(solution)/shard_map/ppermute | solution.py:26
  106.3 7.9 %collective-permute-start.12 = (bf16[4,256,128]{2,1,0:T(8,128)(2,1)S(1)}, bf16[4,256,128]{2,1,0:T(8,128)(2,1)S(1)}, u32[]{:S(2)}, u32[]{:S(2)}) collective-permute-start(bf16[4,256,128]{2,1,0:T(8,128)(2,1)S(1)} %collective-permute-done.11), channel_id=1, source_target_pairs={{0,4},{4,8},{8,12},{12,16},{16,20},{20,24},{24,28},{28,0},{1,5},{5... | collective-permute-start | bytes 786440 | tf_op jit(solution)/shard_map/ppermute | solution.py:26
  106.3 7.9 %collective-permute-start.16 = (bf16[4,256,128]{2,1,0:T(8,128)(2,1)S(1)}, bf16[4,256,128]{2,1,0:T(8,128)(2,1)S(1)}, u32[]{:S(2)}, u32[]{:S(2)}) collective-permute-start(bf16[4,256,128]{2,1,0:T(8,128)(2,1)S(1)} %collective-permute-done.15), channel_id=1, source_target_pairs={{0,28},{4,0},{8,4},{12,8},{16,12},{20,16},{24,20},{28,24},{1,29},{... | collective-permute-start | bytes 786440 | tf_op jit(solution)/shard_map/ppermute | solution.py:26
  114.1 6.9 %collective-permute-start.13 = (bf16[4,256,128]{2,1,0:T(8,128)(2,1)S(1)}, bf16[4,256,128]{2,1,0:T(8,128)(2,1)S(1)}, u32[]{:S(2)}, u32[]{:S(2)}) collective-permute-start(bf16[4,256,128]{2,1,0:T(8,128)(2,1)S(1)} %collective-permute-done.12), channel_id=1, source_target_pairs={{0,4},{4,8},{8,12},{12,16},{16,20},{20,24},{24,28},{28,0},{1,5},{5... | collective-permute-start | bytes 786440 | tf_op jit(solution)/shard_map/ppermute | solution.py:26
  114.1 7.0 %collective-permute-start.17 = (bf16[4,256,128]{2,1,0:T(8,128)(2,1)S(1)}, bf16[4,256,128]{2,1,0:T(8,128)(2,1)S(1)}, u32[]{:S(2)}, u32[]{:S(2)}) collective-permute-start(bf16[4,256,128]{2,1,0:T(8,128)(2,1)S(1)} %collective-permute-done.16), channel_id=1, source_target_pairs={{0,28},{4,0},{8,4},{12,8},{16,12},{20,16},{24,20},{28,24},{1,29},{... | collective-permute-start | bytes 786440 | tf_op jit(solution)/shard_map/ppermute | solution.py:26
  121.1 22.4 %collective-permute-start.14 = (bf16[2,256,128]{2,1,0:T(8,128)(2,1)S(1)}, bf16[2,256,128]{2,1,0:T(8,128)(2,1)S(1)}, u32[]{:S(2)}, u32[]{:S(2)}) collective-permute-start(bf16[2,256,128]{2,1,0:T(8,128)(2,1)S(1)} %slice.209), channel_id=1, source_target_pairs={{0,4},{4,8},{8,12},{12,16},{16,20},{20,24},{24,28},{28,0},{1,5},{5... | collective-permute-start | bytes 393224 | tf_op jit(solution)/shard_map/ppermute | solution.py:26
  121.2 22.3 %collective-permute-start.18 = (bf16[2,256,128]{2,1,0:T(8,128)(2,1)S(1)}, bf16[2,256,128]{2,1,0:T(8,128)(2,1)S(1)}, u32[]{:S(2)}, u32[]{:S(2)}) collective-permute-start(bf16[2,256,128]{2,1,0:T(8,128)(2,1)S(1)} %slice.210), channel_id=1, source_target_pairs={{0,28},{4,0},{8,4},{12,8},{16,12},{20,16},{24,20},{28,24},{1,29},{... | collective-permute-start | bytes 393224 | tf_op jit(solution)/shard_map/ppermute | solution.py:26
  124.0 2.0 %copy-start.4 = (bf16[16,128,896]{2,1,0:T(8,128)(2,1)S(1)}, bf16[16,128,896]{2,1,0:T(8,128)(2,1)}, u32[]{:S(2)}) copy-start(bf16[16,128,896]{2,1,0:T(8,128)(2,1)} %all-gather.2.cloned.1.call-done.s_ref) | copy-start | bytes 11010052
  131.7 2.0 %copy-start = (bf16[16,128,1024]{2,1,0:T(8,128)(2,1)}, bf16[16,128,1024]{2,1,0:T(8,128)(2,1)S(1)}, u32[]{:S(2)}) copy-start(bf16[16,128,1024]{2,1,0:T(8,128)(2,1)S(1)} %project.2.kva) | copy-start | bytes 12582916
  141.4 2.0 %copy-start.2 = (bf16[16,128,1024]{2,1,0:T(8,128)(2,1)}, bf16[16,128,1024]{2,1,0:T(8,128)(2,1)S(1)}, u32[]{:S(2)}) copy-start(bf16[16,128,1024]{2,1,0:T(8,128)(2,1)S(1)} %project.3.kvb) | copy-start | bytes 12582916
  143.9 5.3 %collective-permute-start.20 = (bf16[256,512]{1,0:T(8,128)(2,1)S(1)}, bf16[256,512]{1,0:T(8,128)(2,1)S(1)}, u32[]{:S(2)}, u32[]{:S(2)}) collective-permute-start(bf16[256,512]{1,0:T(8,128)(2,1)S(1)} %add_convert_fusion.qa_ref), channel_id=1, source_target_pairs={{0,2},{2,0},{1,3},{3,1},{4,6},{6,4},{5,7},{7,5},{8,10},{10,8},{9,1... | collective-permute-start | bytes 786440 | tf_op jit(solution)/shard_map/ppermute | solution.py:30
  149.3 2.2 %copy-start.1 = (bf16[16,128,1024]{2,1,0:T(8,128)(2,1)S(1)}, bf16[16,128,1024]{2,1,0:T(8,128)(2,1)}, u32[]{:S(2)}) copy-start(bf16[16,128,1024]{2,1,0:T(8,128)(2,1)} %copy-done) | copy-start | bytes 12582916
  151.5 2.2 %copy-start.3 = (bf16[16,128,1024]{2,1,0:T(8,128)(2,1)S(1)}, bf16[16,128,1024]{2,1,0:T(8,128)(2,1)}, u32[]{:S(2)}) copy-start(bf16[16,128,1024]{2,1,0:T(8,128)(2,1)} %copy-done.2) | copy-start | bytes 12582916
  163.9 5.4 %collective-permute-start.22 = (bf16[2,512,128]{2,1,0:T(8,128)(2,1)S(1)}, bf16[2,512,128]{2,1,0:T(8,128)(2,1)S(1)}, u32[]{:S(2)}, u32[]{:S(2)}) collective-permute-start(bf16[2,512,128]{2,1,0:T(8,128)(2,1)S(1)} %get-tuple-element.50), channel_id=1, source_target_pairs={{0,2},{2,0},{1,3},{3,1},{4,6},{6,4},{5,7},{7,5},{8,10},{10,8},{9,1... | collective-permute-start | bytes 786440 | tf_op jit(solution)/shard_map/ppermute | solution.py:30
  164.1 5.1 %collective-permute-start.21 = (f32[2,2,256]{2,1,0:T(2,128)S(1)}, f32[2,2,256]{2,1,0:T(2,128)S(1)}, u32[]{:S(2)}, u32[]{:S(2)}) collective-permute-start(f32[2,2,256]{2,1,0:T(2,128)S(1)} %slice.201), channel_id=1, source_target_pairs={{0,2},{2,0},{1,3},{3,1},{4,6},{6,4},{5,7},{7,5},{8,10},{10,8},{9,1... | collective-permute-start | bytes 12296 | tf_op jit(solution)/shard_map/ppermute | solution.py:30
  169.8 9.0 %collective-permute-start.23 = (bf16[2,256,128]{2,1,0:T(8,128)(2,1)S(1)}, bf16[2,256,128]{2,1,0:T(8,128)(2,1)S(1)}, u32[]{:S(2)}, u32[]{:S(2)}) collective-permute-start(bf16[2,256,128]{2,1,0:T(8,128)(2,1)S(1)} %get-tuple-element.53), channel_id=1, source_target_pairs={{0,1},{1,0},{2,3},{3,2},{4,5},{5,4},{6,7},{7,6},{8,9},{9,8},{10,11... | collective-permute-start | bytes 393224 | tf_op jit(solution)/shard_map/ppermute | solution.py:30
Sparse Core Ops, SparseCore 0:
  14.7 52.5 all-gather.1

commit v4 on v3

v4 whole, which is shorter than its diff:
```python
import functools
import math

import jax
import jax.numpy as jnp
from jax import lax
from jax.experimental import pallas as pl
from jax.experimental.pallas import tpu as pltpu
from jax.sharding import Mesh
from jax.sharding import PartitionSpec as P

HD = 128
AXES = ("x_hi", "y", "z", "x_lo", "core")
CTX = ("x_hi", "y")
DB = ("z", "x_lo", "core")
XC = ("x_lo", "core")
XX = ("x_hi", "x_lo")
LOW = -1e30
EXP2_SCALE = math.log2(math.e) / math.sqrt(HD)
BF = jnp.bfloat16
F32 = jnp.float32


def ring(value, axis, step):
    n = lax.axis_size(axis)
    return lax.ppermute(value, axis, [(i, (i + step) % n) for i in range(n)])


def swap(value, axis):
    return lax.ppermute(value, axis, [(0, 1), (1, 0)])


def params(megabytes):
    return pltpu.CompilerParams(
        dimension_semantics=("arbitrary",), vmem_limit_bytes=megabytes << 20
    )


def dot_t(a, b):
    return lax.dot_general(a, b, (((1,), (1,)), ((), ())), preferred_element_type=F32)


SUB = 256


def load_block(kx, vx, key, value):
    kx[...] = key.T
    vx[:, :HD] = value
    vx[:, HD:] = jnp.ones_like(value)


def absorb(q_ref, kx, vx, m_ref, acc):
    def scores(i):
        return jnp.dot(q_ref[i * SUB : (i + 1) * SUB, :], kx[...], preferred_element_type=F32)

    n = q_ref.shape[0] // SUB
    s = scores(0)
    for i in range(n):
        ahead = scores(i + 1) if i + 1 < n else None
        r = slice(i * SUB, (i + 1) * SUB)
        before = m_ref[r]
        now = jnp.maximum(before, jnp.max(s, axis=1, keepdims=True))
        p = jnp.exp2((s - now[:, :1]) * EXP2_SCALE)
        factor = jnp.exp2((before - now) * EXP2_SCALE)
        m_ref[r] = now
        acc[r] = acc[r] * jnp.concatenate([factor, factor], axis=1) + jnp.dot(
            p.astype(BF), vx[...], preferred_element_type=F32
        )
        s = ahead


def own_kernel(q_ref, kv_ref, m_ref, acc, kx, vx):
    load_block(kx, vx, kv_ref[0], kv_ref[1])

    def scores(i):
        seen = (i + 1) * SUB
        s = jnp.dot(q_ref[i * SUB : seen, :], kx[:, :seen], preferred_element_type=F32)
        row = lax.broadcasted_iota(jnp.int32, s.shape, 0) + i * SUB
        return jnp.where(row >= lax.broadcasted_iota(jnp.int32, s.shape, 1), s, LOW)

    n = q_ref.shape[0] // SUB
    s = scores(0)
    for i in range(n):
        ahead = scores(i + 1) if i + 1 < n else None
        r = slice(i * SUB, (i + 1) * SUB)
        now = jnp.max(s, axis=1, keepdims=True)
        p = jnp.exp2((s - now) * EXP2_SCALE)
        m_ref[r] = jnp.broadcast_to(now, (SUB, HD))
        acc[r] = jnp.dot(p.astype(BF), vx[: (i + 1) * SUB, :], preferred_element_type=F32)
        s = ahead


def attend_own(q, kv):
    rows = q.shape[0]
    return pl.pallas_call(
        own_kernel,
        in_specs=[pl.BlockSpec(memory_space=pltpu.VMEM)] * 2,
        out_specs=[pl.BlockSpec(memory_space=pltpu.VMEM)] * 2,
        out_shape=[jax.ShapeDtypeStruct((rows, HD), F32), jax.ShapeDtypeStruct((rows, 2 * HD), F32)],
        scratch_shapes=[pltpu.VMEM((HD, rows), BF), pltpu.VMEM((rows, 2 * HD), BF)],
        compiler_params=pltpu.CompilerParams(vmem_limit_bytes=24 << 20),
        cost_estimate=pl.CostEstimate(flops=1 << 30, bytes_accessed=3 << 20, transcendentals=0),
        name="attend_own",
    )(q, kv)


def middle_kernel(flags, q_ref, qs_ref, m_in, acc_in, kv0, kv1, kv2, m_ref, acc, qx, kx, vx):
    which = pl.program_id(0)

    @pl.when(which == 0)
    def _():
        for b, kv in enumerate((kv0, kv1, kv2)):
            load_block(kx.at[b], vx.at[b], kv[0], kv[1])
        qx[...] = q_ref[...]
        m_ref[0] = m_in[...]
        acc[0] = acc_in[...]

    @pl.when(which == 1)
    def _():
        qx[...] = qs_ref[...]
        m_ref[0] = jnp.full(m_in.shape, LOW, F32)
        acc[0] = jnp.zeros(acc_in.shape, F32)

    @pl.loop(0, 3)
    def _(b):
        @pl.when(flags[4 * which + b] == 1)
        def _():
            absorb(qx, kx.at[b], vx.at[b], m_ref.at[0], acc.at[0])


def attend_middle(flags, q, qs, m, acc, kv0, kv1, kv2):
    rows = q.shape[0]
    whole2 = pl.BlockSpec((rows, HD), lambda t, f: (0, 0))
    whole3 = pl.BlockSpec((2, rows, HD), lambda t, f: (0, 0, 0))
    return pl.pallas_call(
        middle_kernel,
        grid_spec=pltpu.PrefetchScalarGridSpec(
            num_scalar_prefetch=1,
            grid=(2,),
            in_specs=[
                whole2,
                whole2,
                whole2,
                pl.BlockSpec((rows, 2 * HD), lambda t, f: (0, 0)),
                whole3,
                whole3,
                whole3,
            ],
            out_specs=[
                pl.BlockSpec((1, rows, HD), lambda t, f: (t, 0, 0)),
                pl.BlockSpec((1, rows, 2 * HD), lambda t, f: (t, 0, 0)),
            ],
            scratch_shapes=[
                pltpu.VMEM((rows, HD), BF),
                pltpu.VMEM((3, HD, rows), BF),
                pltpu.VMEM((3, rows, 2 * HD), BF),
            ],
        ),
        out_shape=[
            jax.ShapeDtypeStruct((2, rows, HD), F32),
            jax.ShapeDtypeStruct((2, rows, 2 * HD), F32),
        ],
        compiler_params=params(40),
        cost_estimate=pl.CostEstimate(flops=8 << 30, bytes_accessed=6 << 20, transcendentals=0),
        name="attend_middle",
    )(flags, q, qs, m, acc, kv0, kv1, kv2)


def last_kernel(flags, q_ref, qs_ref, m_in, acc_in, k3, v3, o_ref, os_ref, lse_ref, qx, kx, vx, m_ref, acc):
    which = pl.program_id(0)
    m_ref[...] = m_in[0]
    acc[...] = acc_in[0]

    @pl.when(which == 0)
    def _():
        load_block(kx, vx, k3[...], v3[...])
        qx[...] = q_ref[...]

    @pl.when(which == 1)
    def _():
        qx[...] = qs_ref[...]

    @pl.when(flags[4 * which + 3] == 1)
    def _():
        absorb(qx, kx, vx, m_ref, acc)

    total = acc[:, HD:]
    o = acc[:, :HD] / total
    lse = m_ref[...] * EXP2_SCALE + jnp.log2(total)
    for i in range(lse.shape[0] // SUB):
        lse_ref[0, i] = lse[i * SUB : (i + 1) * SUB].T[:1]

    @pl.when(which == 0)
    def _():
        o_ref[...] = o

    @pl.when(which == 1)
    def _():
        os_ref[...] = o.astype(BF)


def attend_last(flags, q, qs, m, acc, k3, v3):
    rows = q.shape[0]
    n = rows // SUB
    whole2 = pl.BlockSpec((rows, HD), lambda t, f: (0, 0))
    return pl.pallas_call(
        last_kernel,
        grid_spec=pltpu.PrefetchScalarGridSpec(
            num_scalar_prefetch=1,
            grid=(2,),
            in_specs=[
                whole2,
                whole2,
                pl.BlockSpec((1, rows, HD), lambda t, f: (t, 0, 0)),
                pl.BlockSpec((1, rows, 2 * HD), lambda t, f: (t, 0, 0)),
                whole2,
                whole2,
            ],
            out_specs=[whole2, whole2, pl.BlockSpec((1, n, 1, SUB), lambda t, f: (t, 0, 0, 0))],
            scratch_shapes=[
                pltpu.VMEM((rows, HD), BF),
                pltpu.VMEM((HD, rows), BF),
                pltpu.VMEM((rows, 2 * HD), BF),
                pltpu.VMEM((rows, HD), F32),
                pltpu.VMEM((rows, 2 * HD), F32),
            ],
        ),
        out_shape=[
            jax.ShapeDtypeStruct((rows, HD), F32),
            jax.ShapeDtypeStruct((rows, HD), BF),
            jax.ShapeDtypeStruct((2, n, 1, SUB), F32),
        ],
        compiler_params=params(40),
        cost_estimate=pl.CostEstimate(flops=3 << 30, bytes_accessed=6 << 20, transcendentals=0),
        name="attend_last",
    )(flags, q, qs, m, acc, k3, v3)


def cross_queries(z, parts, weights):
    total = 0.0
    for back, part in parts:
        a = jnp.concatenate([part[h] for h in range(part.shape[0])], axis=1)
        w = lax.dynamic_index_in_dim(weights, (z + 8 - back) % 8, 0, keepdims=False)
        total = total + jnp.dot(a, w, preferred_element_type=F32)
    return total


def project_kernel(info, a_ref, b_ref, w_ref, k_ref, v_ref):
    g = pl.program_id(0)
    slots = a_ref.shape[0]

    def pick(n):
        slot = jnp.maximum(info[2 * g + n], 0)
        at = slot & (slots - 1)
        return jnp.where(slot < slots, a_ref[at], b_ref[at])

    states = jnp.concatenate([pick(0), pick(1)], axis=0)
    both = jnp.dot(states, w_ref[...], preferred_element_type=F32).astype(BF)
    half = both.shape[1] // 2
    k_ref[0] = both[:, :half].T
    v_ref[0] = both[:, half:]


def project(info, held_a, held_b, weights):
    n, length, width = held_a.shape
    groups = info.shape[0] // 2
    half = weights.shape[1] // 2
    whole = pl.BlockSpec((n, length, width), lambda g, s: (0, 0, 0))
    return pl.pallas_call(
        project_kernel,
        grid_spec=pltpu.PrefetchScalarGridSpec(
            num_scalar_prefetch=1,
            grid=(groups,),
            in_specs=[whole, whole, pl.BlockSpec(weights.shape, lambda g, s: (0, 0))],
            out_specs=[
                pl.BlockSpec((1, half, 2 * length), lambda g, s: (g, 0, 0)),
                pl.BlockSpec((1, 2 * length, half), lambda g, s: (g, 0, 0)),
            ],
        ),
        out_shape=[
            jax.ShapeDtypeStruct((groups, half, 2 * length), BF),
            jax.ShapeDtypeStruct((groups, 2 * length, half), BF),
        ],
        compiler_params=params(40),
        cost_estimate=pl.CostEstimate(flops=4 << 30, bytes_accessed=12 << 20, transcendentals=0),
        name="project",
    )(info, held_a, held_b, weights)


def cross_kernel(info, qa_ref, qb_ref, k_ref, v_ref, o_ref, lse_ref):
    step = pl.program_id(0)
    per = k_ref.shape[0]
    group = lse_ref.shape[2]
    late = step * 2 >= pl.num_programs(0)
    for c in range(per):
        rows = slice(c * group, (c + 1) * group)
        g = per * step + c
        q = jnp.where(late, qb_ref[rows], qa_ref[rows])
        first, second = info[2 * g] >= 0, info[2 * g + 1] >= 0
        column = lax.broadcasted_iota(jnp.int32, (1, k_ref.shape[2]), 1)
        bias = jnp.where(
            column < k_ref.shape[2] // 2, jnp.where(first, 0.0, LOW), jnp.where(second, 0.0, LOW)
        )
        some = first | second
        lane = lax.broadcasted_iota(jnp.int32, (group, HD), 1)
        stats = jnp.full((group, HD), LOW, F32)
        for r in range(4):
            cut = slice(r * HD, (r + 1) * HD)
            s = jnp.dot(q[:, cut], k_ref[c, cut, :], preferred_element_type=F32) + bias
            top = jnp.max(s, axis=1, keepdims=True)
            p = jnp.exp2((s - top) * EXP2_SCALE)
            total = jnp.sum(p, axis=1, keepdims=True)
            o = jnp.dot(p.astype(BF), v_ref[c, :, cut], preferred_element_type=F32) / total
            o_ref[r, rows] = o.astype(BF)
            stats = jnp.where((lane == r) & some, top * EXP2_SCALE + jnp.log2(total), stats)
        lse_ref[c] = stats.T[:8]


def cross(info, queries_a, queries_b, keys, values):
    groups = keys.shape[0]
    per = 2
    steps = groups // per
    group = queries_a.shape[0] * 2 // groups
    width = queries_a.shape[1]
    return pl.pallas_call(
        cross_kernel,
        grid_spec=pltpu.PrefetchScalarGridSpec(
            num_scalar_prefetch=1,
            grid=(steps,),
            in_specs=[
                pl.BlockSpec((per * group, width), lambda g, s: (jnp.minimum(g, steps // 2 - 1), 0)),
                pl.BlockSpec((per * group, width), lambda g, s: (jnp.maximum(g - steps // 2, 0), 0)),
                pl.BlockSpec((per,) + keys.shape[1:], lambda g, s: (g, 0, 0)),
                pl.BlockSpec((per,) + values.shape[1:], lambda g, s: (g, 0, 0)),
            ],
            out_specs=[
                pl.BlockSpec((4, per * group, HD), lambda g, s: (0, g, 0)),
                pl.BlockSpec((per, 8, group), lambda g, s: (g, 0, 0)),
            ],
        ),
        out_shape=[
            jax.ShapeDtypeStruct((4, groups * group, HD), BF),
            jax.ShapeDtypeStruct((groups, 8, group), F32),
        ],
        compiler_params=params(32),
        cost_estimate=pl.CostEstimate(flops=1 << 30, bytes_accessed=5 << 20, transcendentals=0),
        name="cross",
    )(info, queries_a, queries_b, keys, values)


def merge(o_a, lse_a, o_b, lse_b):
    top = jnp.maximum(lse_a, lse_b)
    e_a = jnp.exp2(lse_a - top)
    e_b = jnp.exp2(lse_b - top)
    return ((o_a.astype(F32) * e_a + o_b.astype(F32) * e_b) / (e_a + e_b)).astype(BF)


def local(q, k, v, states, nb_shard, nb_row, wk, wv, wq):
    rows = q.shape[0]
    quarter = rows // 4
    y = lax.axis_index("y")
    z = lax.axis_index("z")
    x_lo = lax.axis_index("x_lo")
    core = lax.axis_index("core")
    late = lax.axis_index("x_hi") == 1
    db_index = lax.axis_index(DB)

    kv0, shard, row = lax.optimization_barrier((jnp.stack([k, v]), nb_shard, nb_row))

    place = 2 * lax.broadcasted_iota(jnp.int32, nb_shard.shape, 0) + lax.broadcasted_iota(
        jnp.int32, nb_shard.shape, 1
    )
    coded = place * states.shape[0] + row
    asked = shard == db_index
    none = nb_shard.size * states.shape[0]
    first = jnp.min(jnp.where(asked, coded, none)) & (states.shape[0] - 1)
    last = jnp.max(jnp.where(asked, coded, 0)) & (states.shape[0] - 1)
    pair = jnp.concatenate(
        [lax.dynamic_slice_in_dim(states, i, 1, 0) for i in (first, last)], axis=0
    )
    held_a = lax.all_gather(pair, "z", axis=0, tiled=True)

    kv1 = ring(kv0, "y", 1)
    kv2 = ring(kv0, "y", -1)
    qs = lax.ppermute(q, "x_hi", [(1, 0)])
    k3 = ring(kv1[0], "y", 1)
    v3 = ring(kv2[1], "y", -1)
    flags = jnp.stack([y < 0, y >= 1, y >= 3, y >= 2] + [~late] * 4).astype(jnp.int32)
    m, acc = attend_own(q, kv0)
    m, acc = attend_middle(flags, q, qs, m, acc, kv0, kv1, kv2)
    wall = jnp.concatenate([wq, wk, wv], axis=0)
    half = wall.shape[0] // 2
    w_up = ring(wall[:half], XX, -1)
    w_down = ring(wall[half:], XX, 1)
    o, o_sent, lse = attend_last(flags, q, qs, m, acc, k3, v3)
    lse, lse_sent = lse[0], lse[1]

    o_sent, lse_sent, w_up, w_down = lax.optimization_barrier((o_sent, lse_sent, w_up, w_down))
    o_back = lax.ppermute(o_sent, "x_hi", [(0, 1)])
    lse_back = lax.ppermute(lse_sent, "x_hi", [(0, 1)])
    w_x = jnp.concatenate([w_up, w_down], axis=0)
    w4 = jnp.concatenate([wall, swap(wall, "core"), w_x, swap(w_x, "core")], axis=1)
    depth, width = wq.shape[0], wk.shape[0]
    wq4 = w4[:depth].reshape(8, depth // 8, 4 * HD)
    wkv4 = jnp.concatenate([w4[depth : depth + width], w4[depth + width :]], axis=1)
    o_back, lse_back, wq4, wkv4 = lax.optimization_barrier((o_back, lse_back, wq4, wkv4))

    lse_back = jnp.where(late, lse_back.reshape(rows, 1), LOW)
    self_out = merge(o, lse.reshape(rows, 1), o_back, lse_back)

    held_b = swap(held_a, "core")
    same = nb_shard.reshape(-1)[:, None] == nb_shard.reshape(-1)[None, :]
    n = nb_shard.size
    before = lax.broadcasted_iota(jnp.int32, (n, n), 1) < lax.broadcasted_iota(jnp.int32, (n, n), 0)
    rank = jnp.max((same & before).astype(jnp.int32), axis=1)
    shard = nb_shard.reshape(-1)
    slot = ((shard % 2) ^ core) * 16 + (shard // 4) * 2 + rank
    slot = jnp.where((shard // 2) % 2 == x_lo, slot, -1).reshape(4, n // 4)
    info = jnp.concatenate(
        [
            lax.dynamic_slice_in_dim(slot, 2 * x_lo + core, 1, 0),
            lax.dynamic_slice_in_dim(slot, 2 * (1 - x_lo) + core, 1, 0),
        ],
        axis=1,
    ).reshape(-1)
    keys, values = project(info, held_a, held_b, wkv4)

    mine = lax.all_to_all(self_out.reshape(4, quarter, HD), XC, 0, 0)
    f1 = ring(mine, "z", 1)
    b1 = ring(mine, "z", -1)
    f2 = ring(f1, "z", 1)
    b2 = ring(b1, "z", -1)
    f3 = ring(f2, "z", 1)
    b3 = ring(b2, "z", -1)
    f3, b3, keys, values = lax.optimization_barrier((f3, b3, keys, values))
    far_f = ring(f3[:2], "z", 1)
    far_b = ring(b3[2:], "z", -1)
    near = cross_queries(
        z, ((0, mine), (1, f1), (2, f2), (3, f3), (5, b3), (6, b2), (7, b1)), wq4
    )
    far_f, far_b, near = lax.optimization_barrier((far_f, far_b, near))
    far = jnp.concatenate([far_f, far_b], axis=0)
    queries = (near + cross_queries(z, ((4, far),), wq4)).astype(BF)

    other = swap(queries, "x_lo")
    other = jnp.concatenate([other[:, 2 * HD :], other[:, : 2 * HD]], axis=1)
    o, lse = cross(info, queries, other, keys, values)

    lse = lse[:, :4].transpose(1, 0, 2).reshape(4, 2, 2 * HD)
    o_got = swap(o[2:], "x_lo").reshape(2, 2, quarter, HD)[:, ::-1]
    lse_got = swap(lse[2:], "x_lo")[:, ::-1]
    both = merge(
        o[:2].reshape(2, 2, quarter, HD), lse[:2][..., None], o_got, lse_got[..., None]
    )
    kept, got = both[0], swap(both[1], "core")
    kept, got = (jnp.where(x_lo == 0, a, a[::-1]) for a in (kept, got))
    cross_out = jnp.where(
        core == 0, jnp.stack([kept, got], axis=1), jnp.stack([got, kept], axis=1)
    ).reshape(rows, HD)
    return (self_out, cross_out)


def solution(mesh):
    fine = Mesh(mesh.devices.reshape(2, 4, 8, 2, 2), AXES)
    return jax.shard_map(
        local,
        mesh=fine,
        in_specs=(
            P(CTX, DB),
            P(CTX, DB),
            P(CTX, DB),
            P(DB, None, None),
            P(CTX, None),
            P(CTX, None),
            P(None, DB),
            P(None, DB),
            P(None, DB),
        ),
        out_specs=(P(CTX, DB), P(CTX, DB)),
        check_vma=False,
    )
```

time: 186 us -> 149 us (0.80); the launches traced: 187 us -> 147 us
  Pallas kernels: 41.1 us -> 19.9 us
  waiting for transfers between devices: 52.2 us -> 44.3 us
  local copies, waits for them, and re-layouts: 18.9 us -> 12.7 us
  starting transfers between devices: 42.7 us -> 37.5 us
  other arithmetic: 8.42 us -> 11.7 us
  between operations: 18.6 us -> 15.9 us
    ppermute x1, waiting for transfers between devices: 17.1 us -> 0.01 us  [local(): lse_back = lax.ppermute(lse_sent, 'x_hi', [(0, 1)])]
    pallas_call x3 -> x4, Pallas kernels: 30.9 us -> 17.1 us  [the longest x1 8.35 us: project(): pl.pallas_call(project_kernel, grid_spec=pltpu.PrefetchScalarGridSpec(num...]
    all_gather x1, waiting for transfers between devices: 0.02 us -> 13.5 us  [local(): held_a = lax.all_gather(pair, 'z', axis=0, tiled=True)]
    unnamed x30 -> x20, local copies, waits for them, and re-layouts: 9.39 us -> 1.91 us
    pallas_call x1, Pallas kernels: 10.2 us -> 2.8 us  [cross(): pl.pallas_call(cross_kernel, grid_spec=pltpu.PrefetchScalarGridSpec(num_s...]
    ppermute x14, waiting for transfers between devices: 22.3 us -> 17.4 us  [ring(): return lax.ppermute(value, axis, [(i, (i + step) % n) for i in range(n)])]
    ppermute x14, starting transfers between devices: 18.3 us -> 15.5 us  [ring(): return lax.ppermute(value, axis, [(i, (i + step) % n) for i in range(n)])]
    ppermute x7, starting transfers between devices: 15.3 us -> 12.5 us  [swap(): return lax.ppermute(value, axis, [(0, 1), (1, 0)])]
  transfers between devices with their start and end apart: 26 -> 26, of which waited for: 12 -> 12; matrix products, arithmetic and copies ran while one was open for 9% -> 15% of each run, Pallas kernels for 17% -> 12%
where the time goes in v4:
time: 149 us; the launch traced here: 147 us
  waiting for transfers between devices  44.3 us (30%)
  starting transfers between devices  37.5 us (25%)
  Pallas kernels  19.9 us (13%)
  between operations  15.9 us (11%)
  local copies, waits for them, and re-layouts  12.7 us (9%)
  other arithmetic  11.7 us (8%)
  matrix products  4.66 us (3%)
    ppermute x14, waiting for transfers between devices, ring(): return lax.ppermute(value, axis, [(i, (i + step) % n) for i in range(n)])  17.4 us
    ppermute x14, starting transfers between devices, ring(): return lax.ppermute(value, axis, [(i, (i + step) % n) for i in range(n)])  15.5 us
    all_gather x1, waiting for transfers between devices, local(): held_a = lax.all_gather(pair, 'z', axis=0, tiled=True)  13.5 us
    ppermute x7, starting transfers between devices, swap(): return lax.ppermute(value, axis, [(0, 1), (1, 0)])  12.5 us
    ppermute x7, waiting for transfers between devices, swap(): return lax.ppermute(value, axis, [(0, 1), (1, 0)])  9.28 us
    pallas_call x1, Pallas kernels, project(): pl.pallas_call(project_kernel, grid_spec=pltpu.PrefetchScalarGridSpec(num...  8.35 us
    dot_general x8, matrix products, cross_queries(): total = total + jnp.dot(a, w, preferred_element_type=F32)  4.66 us
    pallas_call x1, Pallas kernels, attend_middle(): pl.pallas_call(middle_kernel, grid_spec=pltpu.PrefetchScalarGridSpec(num_...  4.56 us
  transfers between devices with their start and end apart: 26, of which 12 were waited for; matrix products, arithmetic and copies ran while one was open for 15% of the time, Pallas kernels for 12%

profile of v4, /device:TPU:31, one launch (start us, length us, event | category | flops | bytes accessed | tf_op | source)
XLA Modules:
  0.0 146.6 jit_solution(9310384053182848067)
XLA Ops:
  7.2 1.2 pad_maximum_fusion.7.kv_ref.kv0
  8.4 1.3 select_reduce_fusion.1
  11.1 1.1 constant_dynamic-slice_fusion.1
  12.2 0.9 pad_maximum_fusion.8
  13.2 1.5 collective-permute-start.2
  14.6 3.0 %collective-permute-start = (bf16[1024,128]{1,0:T(8,128)(2,1)}, bf16[1024,128]{1,0:T(8,128)(2,1)S(1)}, u32[]{:S(2)}, u32[]{:S(2)}) collective-permute-start(bf16[1024,128]{1,0:T(8,128)(2,1)} %q_ref.5), channel_id=1, source_target_pairs={{128,0},{129,1},{130,2},{131,3},{132,4},{133,5},{134,6},{135,7},{1... | collective-permute-start | bytes 786440 | tf_op jit(solution)/shard_map/ppermute | solution.py:385
  17.7 1.0 constant_dynamic-update-slice_fusion.2
  19.4 1.6 %constant_dynamic-update-slice_fusion = bf16[5888,128]{1,0:T(8,128)(2,1)} fusion(bf16[5888,128]{1,0:T(8,128)(2,1)} %constant_dynamic-update-slice_fusion.1, bf16[896,128]{1,0:T(8,128)(2,1)} %param.16), kind=kLoop, calls=%fused_computation.142 | loop fusion | bytes 458752 | tf_op jit(solution)/shard_map/concatenate | solution.py:391
  21.1 1.5 %collective-permute-start.9 = (bf16[5888,128]{1,0:T(8,128)(2,1)}, bf16[5888,128]{1,0:T(8,128)(2,1)}, u32[]{:S(2)}, u32[]{:S(2)}) collective-permute-start(bf16[5888,128]{1,0:T(8,128)(2,1)} %constant_dynamic-update-slice_fusion), channel_id=1, source_target_pairs={{0,1},{1,0},{2,3},{3,2},{4,5},{5,4},{6,7},{7,6},{8,9},{9,8},{10,11... | collective-permute-start | bytes 4521992 | tf_op jit(solution)/shard_map/ppermute | solution.py:30
  22.6 2.0 %slice.215 = bf16[2944,128]{1,0:T(8,128)(2,1)} slice(bf16[5888,128]{1,0:T(8,128)(2,1)} %constant_dynamic-update-slice_fusion), slice={[2944:5888], [0:128]} | slice | bytes 1507328 | tf_op jit(solution)/shard_map/slice | solution.py:394
  24.6 0.9 slice.164
  25.7 1.3 attend_own.1
  26.9 1.5 %collective-permute-start.5 = (bf16[2944,128]{1,0:T(8,128)(2,1)S(1)}, bf16[2944,128]{1,0:T(8,128)(2,1)S(1)}, u32[]{:S(2)}, u32[]{:S(2)}) collective-permute-start(bf16[2944,128]{1,0:T(8,128)(2,1)S(1)} %copy-done.5), channel_id=1, source_target_pairs={{0,130},{2,0},{128,2},{130,128},{1,131},{3,1},{129,3},{131,129},{4... | collective-permute-start | bytes 2261000 | tf_op jit(solution)/shard_map/ppermute | solution.py:26
  28.5 1.2 collective-permute-start.3
  30.2 4.6 %attend_middle.1 = (f32[2,1024,128]{2,1,0:T(8,128)S(1)}, f32[2,1024,256]{2,1,0:T(8,128)S(1)}) custom-call(s32[8]{0:T(128)S(1)} %convert_element_type.27.flags, bf16[1024,128]{1,0:T(8,128)(2,1)S(1)} %copy-done.1, bf16[1024,128]{1,0:T(8,128)(2,1)S(1)} %collective-permute-done.qs_ref, f32[1024,128]{1,0:T(8,128)S(1)} %get-tuple-element.32.m_in, ...), custom_call_target="tpu_custom_call" | custom-call | flops 8589934592 | bytes 6291456 | tf_op jit(solution)/shard_map/attend_middle/pallas_call | solution.py:135
  34.7 1.3 collective-permute-done.3.k3
  36.0 2.2 %collective-permute-done.4.v3 = bf16[1024,128]{1,0:T(8,128)(2,1)S(1)} collective-permute-done((bf16[1024,128]{1,0:T(8,128)(2,1)S(1)}, bf16[1024,128]{1,0:T(8,128)(2,1)S(1)}, u32[]{:S(2)}, u32[]{:S(2)}) %collective-permute-start.4) | collective-permute-done | bytes 262176 | tf_op jit(solution)/shard_map/ppermute | solution.py:26
  38.2 3.0 %attend_last.1 = (f32[1024,128]{1,0:T(8,128)S(1)}, bf16[1024,128]{1,0:T(8,128)(2,1)S(1)}, f32[2,4,1,256]{3,2,1,0:T(1,128)S(1)}) custom-call(s32[8]{0:T(128)S(1)} %convert_element_type.27.flags, bf16[1024,128]{1,0:T(8,128)(2,1)S(1)} %copy-done.1, bf16[1024,128]{1,0:T(8,128)(2,1)S(1)} %collective-permute-done.qs_ref, ...), custom_call_target="tpu_custom_call" | custom-call | flops 3221225472 | bytes 6291456 | tf_op jit(solution)/shard_map/attend_last/pallas_call | solution.py:206
  41.1 2.3 %collective-permute-done.6 = bf16[2944,128]{1,0:T(8,128)(2,1)} collective-permute-done((bf16[2944,128]{1,0:T(8,128)(2,1)}, bf16[2944,128]{1,0:T(8,128)(2,1)}, u32[]{:S(2)}, u32[]{:S(2)}) %collective-permute-start.6) | collective-permute-done | bytes 753696 | tf_op jit(solution)/shard_map/ppermute | solution.py:26
  43.4 2.9 %collective-permute-done.5 = bf16[2944,128]{1,0:T(8,128)(2,1)S(1)} collective-permute-done((bf16[2944,128]{1,0:T(8,128)(2,1)S(1)}, bf16[2944,128]{1,0:T(8,128)(2,1)S(1)}, u32[]{:S(2)}, u32[]{:S(2)}) %collective-permute-start.5) | collective-permute-done | bytes 753696 | tf_op jit(solution)/shard_map/ppermute | solution.py:26
  46.3 1.2 constant_dynamic-update-slice_fusion.3
  47.6 1.5 %collective-permute-start.10 = (bf16[5888,128]{1,0:T(8,128)(2,1)S(1)}, bf16[5888,128]{1,0:T(8,128)(2,1)}, u32[]{:S(2)}, u32[]{:S(2)}) collective-permute-start(bf16[5888,128]{1,0:T(8,128)(2,1)S(1)} %constant_dynamic-update-slice_fusion.3), channel_id=1, source_target_pairs={{0,1},{1,0},{2,3},{3,2},{4,5},{5,4},{6,7},{7,6},{8,9},{9,8},{10,11... | collective-permute-start | bytes 4521992 | tf_op jit(solution)/shard_map/ppermute | solution.py:30
  49.6 1.3 collective-permute-start.7
  50.9 1.3 collective-permute-start.8
  52.2 13.5 %all-gather.2.cloned.1.call-done.a_ref = bf16[16,128,896]{2,1,0:T(8,128)(2,1)} async-done(((bf16[2,128,896]{2,1,0:T(8,128)(2,1)}), bf16[16,128,896]{2,1,0:T(8,128)(2,1)}) %all-gather.2.cloned.1.call-update) | async-done | bytes 3670032 | tf_op jit(solution)/shard_map/all_gather | solution.py:381
  66.4 3.2 %pad_maximum_fusion = bf16[5888,512]{1,0:T(8,128)(2,1)S(1)} fusion(bf16[5888,128]{1,0:T(8,128)(2,1)} %collective-permute-done.10, bf16[5888,128]{1,0:T(8,128)(2,1)S(1)} %constant_dynamic-update-slice_fusion.3, bf16[5888,128]{1,0:T(8,128)(2,1)} %collective-permute-done.9, bf16[5888,128]{1,0:T(8,128)(2,1)} %constant_dynamic-update-slice_fusion), kind=kLoop, calls=%fused_computation | loop fusion | flops 24117248 | bytes 12058624 | tf_op jit(solution)/shard_map/concatenate | solution.py:402
  69.7 2.9 %fusion.w_ref = bf16[896,1024]{1,0:T(8,128)(2,1)S(1)} fusion(bf16[5888,128]{1,0:T(8,128)(2,1)} %collective-permute-done.10, bf16[5888,128]{1,0:T(8,128)(2,1)} %copy-done.3, bf16[5888,128]{1,0:T(8,128)(2,1)} %collective-permute-done.9, bf16[5888,128]{1,0:T(8,128)(2,1)} %constant_dynamic-update-slice_fusion), kind=kLoop, calls=%fused_computation.2 | loop fusion | flops 14680064 | bytes 7864320 | tf_op jit(solution)/shard_map/concatenate | solution.py:405
  72.6 2.2 %slice.216 = bf16[4096,512]{1,0:T(8,128)(2,1)} slice(bf16[5888,512]{1,0:T(8,128)(2,1)S(1)} %pad_maximum_fusion), slice={[0:4096], [0:512]} | slice | bytes 8388608 | tf_op jit(solution)/shard_map/slice | solution.py:404
  74.9 1.2 divide_convert_fusion
  76.0 3.9 %all-to-all-start = ((bf16[4,256,128]{2,1,0:T(8,128)(2,1)}), bf16[4,256,128]{2,1,0:T(8,128)(2,1)S(1)}, u32[]{:S(2)}, u32[]{:S(2)}) async-start(bf16[4,256,128]{2,1,0:T(8,128)(2,1)} %bitcast.14), calls=%async_computation | async-start | bytes 524288 | tf_op jit(solution)/shard_map/all_to_all | solution.py:428
  80.0 4.0 %all-to-all-done = bf16[4,256,128]{2,1,0:T(8,128)(2,1)S(1)} async-done(((bf16[4,256,128]{2,1,0:T(8,128)(2,1)}), bf16[4,256,128]{2,1,0:T(8,128)(2,1)S(1)}, u32[]{:S(2)}, u32[]{:S(2)}) %all-to-all-start) | async-done | bytes 262176 | tf_op jit(solution)/shard_map/all_to_all | solution.py:428
  84.0 2.7 %collective-permute-start.14 = (bf16[4,256,128]{2,1,0:T(8,128)(2,1)S(1)}, bf16[4,256,128]{2,1,0:T(8,128)(2,1)S(1)}, u32[]{:S(2)}, u32[]{:S(2)}) collective-permute-start(bf16[4,256,128]{2,1,0:T(8,128)(2,1)S(1)} %all-to-all-done), channel_id=1, source_target_pairs={{0,28},{4,0},{8,4},{12,8},{16,12},{20,16},{24,20},{28,24},{1,29},{... | collective-permute-start | bytes 786440 | tf_op jit(solution)/shard_map/ppermute | solution.py:26
  86.8 1.5 %fusion.12 = f32[256,512]{1,0:T(8,128)S(1)} fusion(bf16[8,512,512]{2,1,0:T(8,128)(2,1)} %bitcast.121, s32[]{:T(128)S(6)} %select_n.169, bf16[256,128]{1,0:T(8,128)(2,1)S(1)} %get-tuple-element.101, bf16[256,128]{1,0:T(8,128)(2,1)S(1)} %get-tuple-element.102, bf16[256,128]{1,0:T(8,128)(2,1)S(1)} %get-tuple-element.103, ...), kind=kOutput, calls=%fused_computation.27 | convolution fusion | flops 135266304 | bytes 1310724 | tf_op jit(solution)/shard_map/dot_general | solution.py:244
  88.3 4.3 %collective-permute-done.11 = bf16[4,256,128]{2,1,0:T(8,128)(2,1)S(1)} collective-permute-done((bf16[4,256,128]{2,1,0:T(8,128)(2,1)S(1)}, bf16[4,256,128]{2,1,0:T(8,128)(2,1)S(1)}, u32[]{:S(2)}, u32[]{:S(2)}) %collective-permute-start.11) | collective-permute-done | bytes 262176 | tf_op jit(solution)/shard_map/ppermute | solution.py:26
  92.5 2.7 %collective-permute-start.15 = (bf16[4,256,128]{2,1,0:T(8,128)(2,1)S(1)}, bf16[4,256,128]{2,1,0:T(8,128)(2,1)S(1)}, u32[]{:S(2)}, u32[]{:S(2)}) collective-permute-start(bf16[4,256,128]{2,1,0:T(8,128)(2,1)S(1)} %collective-permute-done.14), channel_id=1, source_target_pairs={{0,28},{4,0},{8,4},{12,8},{16,12},{20,16},{24,20},{28,24},{1,29},{... | collective-permute-start | bytes 786440 | tf_op jit(solution)/shard_map/ppermute | solution.py:26
  95.2 1.3 convolution_add_fusion.5
  96.6 3.5 %collective-permute-done.12 = bf16[4,256,128]{2,1,0:T(8,128)(2,1)S(1)} collective-permute-done((bf16[4,256,128]{2,1,0:T(8,128)(2,1)S(1)}, bf16[4,256,128]{2,1,0:T(8,128)(2,1)S(1)}, u32[]{:S(2)}, u32[]{:S(2)}) %collective-permute-start.12) | collective-permute-done | bytes 262176 | tf_op jit(solution)/shard_map/ppermute | solution.py:26
  100.1 2.7 %collective-permute-start.16 = (bf16[4,256,128]{2,1,0:T(8,128)(2,1)S(1)}, bf16[4,256,128]{2,1,0:T(8,128)(2,1)S(1)}, u32[]{:S(2)}, u32[]{:S(2)}) collective-permute-start(bf16[4,256,128]{2,1,0:T(8,128)(2,1)S(1)} %collective-permute-done.15), channel_id=1, source_target_pairs={{0,28},{4,0},{8,4},{12,8},{16,12},{20,16},{24,20},{28,24},{1,29},{... | collective-permute-start | bytes 786440 | tf_op jit(solution)/shard_map/ppermute | solution.py:26
  103.1 8.4 %project.1 = (bf16[8,512,256]{2,1,0:T(8,128)(2,1)S(1)}, bf16[8,256,512]{2,1,0:T(8,128)(2,1)S(1)}) custom-call(s32[16]{0:T(128)S(1)} %add_bitcast_fusion.info, bf16[16,128,896]{2,1,0:T(8,128)(2,1)S(1)} %copy-done, bf16[16,128,896]{2,1,0:T(8,128)(2,1)} %collective-permute-done.17.b_ref, bf16[896,1024]{1,0:T(8,128)(2,1)S(1)} %fusion.w_ref), custom_call_target="tpu_custom_call" | custom-call | flops 4294967296 | bytes 12582912 | tf_op jit(solution)/shard_map/project/pallas_call | solution.py:269
  111.7 2.7 %collective-permute-start.19 = (bf16[2,256,128]{2,1,0:T(8,128)(2,1)S(1)}, bf16[2,256,128]{2,1,0:T(8,128)(2,1)S(1)}, u32[]{:S(2)}, u32[]{:S(2)}) collective-permute-start(bf16[2,256,128]{2,1,0:T(8,128)(2,1)S(1)} %slice.170), channel_id=1, source_target_pairs={{0,28},{4,0},{8,4},{12,8},{16,12},{20,16},{24,20},{28,24},{1,29},{... | collective-permute-start | bytes 393224 | tf_op jit(solution)/shard_map/ppermute | solution.py:26
  115.6 1.1 collective-permute-done.18
  117.1 0.8 collective-permute-start.20
  118.0 4.7 %collective-permute-done.20 = bf16[256,512]{1,0:T(8,128)(2,1)S(1)} collective-permute-done((bf16[256,512]{1,0:T(8,128)(2,1)S(1)}, bf16[256,512]{1,0:T(8,128)(2,1)S(1)}, u32[]{:S(2)}, u32[]{:S(2)}) %collective-permute-start.20) | collective-permute-done | bytes 262176 | tf_op jit(solution)/shard_map/ppermute | solution.py:30
  122.7 2.8 %cross.1 = (bf16[4,512,128]{2,1,0:T(8,128)(2,1)S(1)}, f32[8,8,64]{2,1,0:T(8,128)S(1)}) custom-call(s32[16]{0:T(128)S(1)} %add_bitcast_fusion.info, bf16[256,512]{1,0:T(8,128)(2,1)S(1)} %add_convert_fusion.qa_ref, bf16[256,512]{1,0:T(8,128)(2,1)S(1)} %pad_maximum_fusion.9.qb_ref, bf16[8,512,256]{2,1,0:T(8,128)(2,1)S(1)} %get-tuple-element.56.k_ref, ...), custom_call_target="tpu_custom_call" | custom-call | flops 1073741824 | bytes 5242880 | tf_op jit(solution)/shard_map/cross/pallas_call | solution.py:325
  126.3 1.0 collective-permute-start.21
  127.3 3.6 %collective-permute-done.21 = f32[2,2,256]{2,1,0:T(2,128)S(1)} collective-permute-done((f32[2,2,256]{2,1,0:T(2,128)S(1)}, f32[2,2,256]{2,1,0:T(2,128)S(1)}, u32[]{:S(2)}, u32[]{:S(2)}) %collective-permute-start.21) | collective-permute-done | bytes 4128 | tf_op jit(solution)/shard_map/ppermute | solution.py:30
  131.5 6.5 %collective-permute-start.23 = (bf16[2,256,128]{2,1,0:T(8,128)(2,1)S(1)}, bf16[2,256,128]{2,1,0:T(8,128)(2,1)S(1)}, u32[]{:S(2)}, u32[]{:S(2)}) collective-permute-start(bf16[2,256,128]{2,1,0:T(8,128)(2,1)S(1)} %get-tuple-element.73), channel_id=1, source_target_pairs={{0,1},{1,0},{2,3},{3,2},{4,5},{5,4},{6,7},{7,6},{8,9},{9,8},{10,11... | collective-permute-start | bytes 393224 | tf_op jit(solution)/shard_map/ppermute | solution.py:30
  138.0 1.0 collective-permute-done.23
  (93 shorter events, 7.2 us)
Async XLA Ops:
  7.2 10.5 %copy-start.4 = (bf16[4096,128]{1,0:T(8,128)(2,1)S(1)}, bf16[4096,128]{1,0:T(8,128)(2,1)}, u32[]{:S(2)}) copy-start(bf16[4096,128]{1,0:T(8,128)(2,1)} %param.17) | copy-start | bytes 3145732
  7.2 11.5 %copy-start.6 = (bf16[896,128]{1,0:T(8,128)(2,1)S(1)}, bf16[896,128]{1,0:T(8,128)(2,1)}, u32[]{:S(2)}) copy-start(bf16[896,128]{1,0:T(8,128)(2,1)} %param.15) | copy-start | bytes 688132
  7.2 58.6 %all-gather.2.cloned.1.call-start = ((), (), s32[]{:S(2)}) async-start(), calls=%async_computation.1 | async-start | bytes 4128768 | tf_op jit(solution)/shard_map/all_gather | solution.py:381
  12.2 13.5 %copy-start.1 = (bf16[1024,128]{1,0:T(8,128)(2,1)S(1)}, bf16[1024,128]{1,0:T(8,128)(2,1)}, u32[]{:S(2)}) copy-start(bf16[1024,128]{1,0:T(8,128)(2,1)} %q_ref.5) | copy-start | bytes 786436
  13.1 13.9 %collective-permute-start.1 = (bf16[2,1024,128]{2,1,0:T(8,128)(2,1)S(1)}, bf16[2,1024,128]{2,1,0:T(8,128)(2,1)S(1)}, u32[]{:S(2)}, u32[]{:S(2)}) collective-permute-start(bf16[2,1024,128]{2,1,0:T(8,128)(2,1)S(1)} %pad_maximum_fusion.7.kv_ref.kv0), channel_id=1, source_target_pairs={{0,32},{32,64},{64,96},{96,0},{1,33},{33,65},{65,97},{97,1},{2,34}... | collective-permute-start | bytes 1572872 | tf_op jit(solution)/shard_map/ppermute | solution.py:26
  13.2 15.3 %collective-permute-start.2 = (bf16[2,1024,128]{2,1,0:T(8,128)(2,1)S(1)}, bf16[2,1024,128]{2,1,0:T(8,128)(2,1)S(1)}, u32[]{:S(2)}, u32[]{:S(2)}) collective-permute-start(bf16[2,1024,128]{2,1,0:T(8,128)(2,1)S(1)} %pad_maximum_fusion.7.kv_ref.kv0), channel_id=1, source_target_pairs={{0,96},{32,0},{64,32},{96,64},{1,97},{33,1},{65,33},{97,65},{2,98}... | collective-permute-start | bytes 1572872 | tf_op jit(solution)/shard_map/ppermute | solution.py:26
  14.6 15.2 %collective-permute-start = (bf16[1024,128]{1,0:T(8,128)(2,1)}, bf16[1024,128]{1,0:T(8,128)(2,1)S(1)}, u32[]{:S(2)}, u32[]{:S(2)}) collective-permute-start(bf16[1024,128]{1,0:T(8,128)(2,1)} %q_ref.5), channel_id=1, source_target_pairs={{128,0},{129,1},{130,2},{131,3},{132,4},{133,5},{134,6},{135,7},{1... | collective-permute-start | bytes 786440 | tf_op jit(solution)/shard_map/ppermute | solution.py:385
  21.1 45.4 %collective-permute-start.9 = (bf16[5888,128]{1,0:T(8,128)(2,1)}, bf16[5888,128]{1,0:T(8,128)(2,1)}, u32[]{:S(2)}, u32[]{:S(2)}) collective-permute-start(bf16[5888,128]{1,0:T(8,128)(2,1)} %constant_dynamic-update-slice_fusion), channel_id=1, source_target_pairs={{0,1},{1,0},{2,3},{3,2},{4,5},{5,4},{6,7},{7,6},{8,9},{9,8},{10,11... | collective-permute-start | bytes 4521992 | tf_op jit(solution)/shard_map/ppermute | solution.py:30
  24.6 18.8 %collective-permute-start.6 = (bf16[2944,128]{1,0:T(8,128)(2,1)}, bf16[2944,128]{1,0:T(8,128)(2,1)}, u32[]{:S(2)}, u32[]{:S(2)}) collective-permute-start(bf16[2944,128]{1,0:T(8,128)(2,1)} %slice.215), channel_id=1, source_target_pairs={{0,2},{2,128},{128,130},{130,0},{1,3},{3,129},{129,131},{131,1},{4... | collective-permute-start | bytes 2261000 | tf_op jit(solution)/shard_map/ppermute | solution.py:26
  25.5 1.4 copy-start.5
  26.9 19.3 %collective-permute-start.5 = (bf16[2944,128]{1,0:T(8,128)(2,1)S(1)}, bf16[2944,128]{1,0:T(8,128)(2,1)S(1)}, u32[]{:S(2)}, u32[]{:S(2)}) collective-permute-start(bf16[2944,128]{1,0:T(8,128)(2,1)S(1)} %copy-done.5), channel_id=1, source_target_pairs={{0,130},{2,0},{128,2},{130,128},{1,131},{3,1},{129,3},{131,129},{4... | collective-permute-start | bytes 2261000 | tf_op jit(solution)/shard_map/ppermute | solution.py:26
  28.5 7.5 %collective-permute-start.3 = (bf16[1024,128]{1,0:T(8,128)(2,1)S(1)}, bf16[1024,128]{1,0:T(8,128)(2,1)S(1)}, u32[]{:S(2)}, u32[]{:S(2)}) collective-permute-start(bf16[1024,128]{1,0:T(8,128)(2,1)S(1)} %slice_bitcast_fusion.1), channel_id=1, source_target_pairs={{0,32},{32,64},{64,96},{96,0},{1,33},{33,65},{65,97},{97,1},{2,34}... | collective-permute-start | bytes 786440 | tf_op jit(solution)/shard_map/ppermute | solution.py:26
  29.8 8.4 %collective-permute-start.4 = (bf16[1024,128]{1,0:T(8,128)(2,1)S(1)}, bf16[1024,128]{1,0:T(8,128)(2,1)S(1)}, u32[]{:S(2)}, u32[]{:S(2)}) collective-permute-start(bf16[1024,128]{1,0:T(8,128)(2,1)S(1)} %slice_bitcast_fusion), channel_id=1, source_target_pairs={{0,96},{32,0},{64,32},{96,64},{1,97},{33,1},{65,33},{97,65},{2,98}... | collective-permute-start | bytes 786440 | tf_op jit(solution)/shard_map/ppermute | solution.py:26
  38.1 10.9 %copy-start.7 = (s32[16,2]{0,1:T(2,128)S(1)}, s32[16,2]{0,1:T(2,128)}, u32[]{:S(2)}) copy-start(s32[16,2]{0,1:T(2,128)} %param.13) | copy-start | bytes 388
  47.6 18.9 %copy-start.3 = (bf16[5888,128]{1,0:T(8,128)(2,1)}, bf16[5888,128]{1,0:T(8,128)(2,1)S(1)}, u32[]{:S(2)}) copy-start(bf16[5888,128]{1,0:T(8,128)(2,1)S(1)} %constant_dynamic-update-slice_fusion.3) | copy-start | bytes 4521988
  47.6 18.9 %collective-permute-start.10 = (bf16[5888,128]{1,0:T(8,128)(2,1)S(1)}, bf16[5888,128]{1,0:T(8,128)(2,1)}, u32[]{:S(2)}, u32[]{:S(2)}) collective-permute-start(bf16[5888,128]{1,0:T(8,128)(2,1)S(1)} %constant_dynamic-update-slice_fusion.3), channel_id=1, source_target_pairs={{0,1},{1,0},{2,3},{3,2},{4,5},{5,4},{6,7},{7,6},{8,9},{9,8},{10,11... | collective-permute-start | bytes 4521992 | tf_op jit(solution)/shard_map/ppermute | solution.py:30
  49.6 25.2 %collective-permute-start.7 = (bf16[1024,128]{1,0:T(8,128)(2,1)S(1)}, bf16[1024,128]{1,0:T(8,128)(2,1)S(1)}, u32[]{:S(2)}, u32[]{:S(2)}) collective-permute-start(bf16[1024,128]{1,0:T(8,128)(2,1)S(1)} %get-tuple-element.39), channel_id=1, source_target_pairs={{0,128},{1,129},{2,130},{3,131},{4,132},{5,133},{6,134},{7,135},{8... | collective-permute-start | bytes 786440 | tf_op jit(solution)/shard_map/ppermute | solution.py:399
  50.9 23.9 %collective-permute-start.8 = (f32[4,1,256]{2,1,0:T(1,128)S(1)}, f32[4,1,256]{2,1,0:T(1,128)S(1)}, u32[]{:S(2)}, u32[]{:S(2)}) collective-permute-start(f32[4,1,256]{2,1,0:T(1,128)S(1)} %get-tuple-element.40), channel_id=1, source_target_pairs={{0,128},{1,129},{2,130},{3,131},{4,132},{5,133},{6,134},{7,135},{8... | collective-permute-start | bytes 12296 | tf_op jit(solution)/shard_map/ppermute | solution.py:400
  65.8 37.4 %collective-permute-start.17 = (bf16[16,128,896]{2,1,0:T(8,128)(2,1)}, bf16[16,128,896]{2,1,0:T(8,128)(2,1)}, u32[]{:S(2)}, u32[]{:S(2)}) collective-permute-start(bf16[16,128,896]{2,1,0:T(8,128)(2,1)} %all-gather.2.cloned.1.call-done.a_ref), channel_id=1, source_target_pairs={{0,1},{1,0},{2,3},{3,2},{4,5},{5,4},{6,7},{7,6},{8,9},{9,8},{10,11... | collective-permute-start | bytes 11010056 | tf_op jit(solution)/shard_map/ppermute | solution.py:30
  76.0 8.0 %all-to-all-start = ((bf16[4,256,128]{2,1,0:T(8,128)(2,1)}), bf16[4,256,128]{2,1,0:T(8,128)(2,1)S(1)}, u32[]{:S(2)}, u32[]{:S(2)}) async-start(bf16[4,256,128]{2,1,0:T(8,128)(2,1)} %bitcast.14), calls=%async_computation | async-start | bytes 524288 | tf_op jit(solution)/shard_map/all_to_all | solution.py:428
  84.0 18.7 %copy-start.2 = (bf16[4096,512]{1,0:T(8,128)(2,1)S(1)}, bf16[4096,512]{1,0:T(8,128)(2,1)}, u32[]{:S(2)}) copy-start(bf16[4096,512]{1,0:T(8,128)(2,1)} %slice.216) | copy-start | bytes 12582916
  84.0 8.5 %collective-permute-start.11 = (bf16[4,256,128]{2,1,0:T(8,128)(2,1)S(1)}, bf16[4,256,128]{2,1,0:T(8,128)(2,1)S(1)}, u32[]{:S(2)}, u32[]{:S(2)}) collective-permute-start(bf16[4,256,128]{2,1,0:T(8,128)(2,1)S(1)} %all-to-all-done), channel_id=1, source_target_pairs={{0,4},{4,8},{8,12},{12,16},{16,20},{20,24},{24,28},{28,0},{1,5},{5... | collective-permute-start | bytes 786440 | tf_op jit(solution)/shard_map/ppermute | solution.py:26
  84.0 8.5 %collective-permute-start.14 = (bf16[4,256,128]{2,1,0:T(8,128)(2,1)S(1)}, bf16[4,256,128]{2,1,0:T(8,128)(2,1)S(1)}, u32[]{:S(2)}, u32[]{:S(2)}) collective-permute-start(bf16[4,256,128]{2,1,0:T(8,128)(2,1)S(1)} %all-to-all-done), channel_id=1, source_target_pairs={{0,28},{4,0},{8,4},{12,8},{16,12},{20,16},{24,20},{28,24},{1,29},{... | collective-permute-start | bytes 786440 | tf_op jit(solution)/shard_map/ppermute | solution.py:26
  86.7 16.4 %copy-start = (bf16[16,128,896]{2,1,0:T(8,128)(2,1)S(1)}, bf16[16,128,896]{2,1,0:T(8,128)(2,1)}, u32[]{:S(2)}) copy-start(bf16[16,128,896]{2,1,0:T(8,128)(2,1)} %all-gather.2.cloned.1.call-done.a_ref) | copy-start | bytes 11010052
  92.5 7.5 %collective-permute-start.12 = (bf16[4,256,128]{2,1,0:T(8,128)(2,1)S(1)}, bf16[4,256,128]{2,1,0:T(8,128)(2,1)S(1)}, u32[]{:S(2)}, u32[]{:S(2)}) collective-permute-start(bf16[4,256,128]{2,1,0:T(8,128)(2,1)S(1)} %collective-permute-done.11), channel_id=1, source_target_pairs={{0,4},{4,8},{8,12},{12,16},{16,20},{20,24},{24,28},{28,0},{1,5},{5... | collective-permute-start | bytes 786440 | tf_op jit(solution)/shard_map/ppermute | solution.py:26
  92.5 7.5 %collective-permute-start.15 = (bf16[4,256,128]{2,1,0:T(8,128)(2,1)S(1)}, bf16[4,256,128]{2,1,0:T(8,128)(2,1)S(1)}, u32[]{:S(2)}, u32[]{:S(2)}) collective-permute-start(bf16[4,256,128]{2,1,0:T(8,128)(2,1)S(1)} %collective-permute-done.14), channel_id=1, source_target_pairs={{0,28},{4,0},{8,4},{12,8},{16,12},{20,16},{24,20},{28,24},{1,29},{... | collective-permute-start | bytes 786440 | tf_op jit(solution)/shard_map/ppermute | solution.py:26
  100.1 11.4 %collective-permute-start.13 = (bf16[4,256,128]{2,1,0:T(8,128)(2,1)S(1)}, bf16[4,256,128]{2,1,0:T(8,128)(2,1)S(1)}, u32[]{:S(2)}, u32[]{:S(2)}) collective-permute-start(bf16[4,256,128]{2,1,0:T(8,128)(2,1)S(1)} %collective-permute-done.12), channel_id=1, source_target_pairs={{0,4},{4,8},{8,12},{12,16},{16,20},{20,24},{24,28},{28,0},{1,5},{5... | collective-permute-start | bytes 786440 | tf_op jit(solution)/shard_map/ppermute | solution.py:26
  100.1 11.4 %collective-permute-start.16 = (bf16[4,256,128]{2,1,0:T(8,128)(2,1)S(1)}, bf16[4,256,128]{2,1,0:T(8,128)(2,1)S(1)}, u32[]{:S(2)}, u32[]{:S(2)}) collective-permute-start(bf16[4,256,128]{2,1,0:T(8,128)(2,1)S(1)} %collective-permute-done.15), channel_id=1, source_target_pairs={{0,28},{4,0},{8,4},{12,8},{16,12},{20,16},{24,20},{28,24},{1,29},{... | collective-permute-start | bytes 786440 | tf_op jit(solution)/shard_map/ppermute | solution.py:26
  111.6 5.1 %collective-permute-start.18 = (bf16[2,256,128]{2,1,0:T(8,128)(2,1)S(1)}, bf16[2,256,128]{2,1,0:T(8,128)(2,1)S(1)}, u32[]{:S(2)}, u32[]{:S(2)}) collective-permute-start(bf16[2,256,128]{2,1,0:T(8,128)(2,1)S(1)} %slice.169), channel_id=1, source_target_pairs={{0,4},{4,8},{8,12},{12,16},{16,20},{20,24},{24,28},{28,0},{1,5},{5... | collective-permute-start | bytes 393224 | tf_op jit(solution)/shard_map/ppermute | solution.py:26
  111.7 5.0 %collective-permute-start.19 = (bf16[2,256,128]{2,1,0:T(8,128)(2,1)S(1)}, bf16[2,256,128]{2,1,0:T(8,128)(2,1)S(1)}, u32[]{:S(2)}, u32[]{:S(2)}) collective-permute-start(bf16[2,256,128]{2,1,0:T(8,128)(2,1)S(1)} %slice.170), channel_id=1, source_target_pairs={{0,28},{4,0},{8,4},{12,8},{16,12},{20,16},{24,20},{28,24},{1,29},{... | collective-permute-start | bytes 393224 | tf_op jit(solution)/shard_map/ppermute | solution.py:26
  117.1 5.5 %collective-permute-start.20 = (bf16[256,512]{1,0:T(8,128)(2,1)S(1)}, bf16[256,512]{1,0:T(8,128)(2,1)S(1)}, u32[]{:S(2)}, u32[]{:S(2)}) collective-permute-start(bf16[256,512]{1,0:T(8,128)(2,1)S(1)} %add_convert_fusion.qa_ref), channel_id=1, source_target_pairs={{0,2},{2,0},{1,3},{3,1},{4,6},{6,4},{5,7},{7,5},{8,10},{10,8},{9,1... | collective-permute-start | bytes 786440 | tf_op jit(solution)/shard_map/ppermute | solution.py:30
  125.6 5.4 %collective-permute-start.22 = (bf16[2,512,128]{2,1,0:T(8,128)(2,1)S(1)}, bf16[2,512,128]{2,1,0:T(8,128)(2,1)S(1)}, u32[]{:S(2)}, u32[]{:S(2)}) collective-permute-start(bf16[2,512,128]{2,1,0:T(8,128)(2,1)S(1)} %get-tuple-element.70), channel_id=1, source_target_pairs={{0,2},{2,0},{1,3},{3,1},{4,6},{6,4},{5,7},{7,5},{8,10},{10,8},{9,1... | collective-permute-start | bytes 786440 | tf_op jit(solution)/shard_map/ppermute | solution.py:30
  126.3 4.7 %collective-permute-start.21 = (f32[2,2,256]{2,1,0:T(2,128)S(1)}, f32[2,2,256]{2,1,0:T(2,128)S(1)}, u32[]{:S(2)}, u32[]{:S(2)}) collective-permute-start(f32[2,2,256]{2,1,0:T(2,128)S(1)} %slice.209), channel_id=1, source_target_pairs={{0,2},{2,0},{1,3},{3,1},{4,6},{6,4},{5,7},{7,5},{8,10},{10,8},{9,1... | collective-permute-start | bytes 12296 | tf_op jit(solution)/shard_map/ppermute | solution.py:30
  131.5 7.5 %collective-permute-start.23 = (bf16[2,256,128]{2,1,0:T(8,128)(2,1)S(1)}, bf16[2,256,128]{2,1,0:T(8,128)(2,1)S(1)}, u32[]{:S(2)}, u32[]{:S(2)}) collective-permute-start(bf16[2,256,128]{2,1,0:T(8,128)(2,1)S(1)} %get-tuple-element.73), channel_id=1, source_target_pairs={{0,1},{1,0},{2,3},{3,2},{4,5},{5,4},{6,7},{7,6},{8,9},{9,8},{10,11... | collective-permute-start | bytes 393224 | tf_op jit(solution)/shard_map/ppermute | solution.py:30
Sparse Core Ops, SparseCore 0:
  13.2 52.5 all-gather.1

commit v5 on v4

--- a/solution.py
+++ b/solution.py
@@ -245,9 +245,16 @@
     return total
 
 
-def project_kernel(info, a_ref, b_ref, w_ref, k_ref, v_ref):
+def project_kernel(info, a_ref, b_ref, w0, w1, w2, w3, k_ref, v_ref, w_ref):
     g = pl.program_id(0)
     slots = a_ref.shape[0]
+    width = a_ref.shape[2]
+
+    @pl.when(g == 0)
+    def _():
+        for r, piece in enumerate((w0, w1, w2, w3)):
+            w_ref[:, r * HD : (r + 1) * HD] = piece[:width]
+            w_ref[:, (4 + r) * HD : (5 + r) * HD] = piece[width:]
 
     def pick(n):
         slot = jnp.maximum(info[2 * g + n], 0)
@@ -261,21 +268,22 @@
     v_ref[0] = both[:, half:]
 
 
-def project(info, held_a, held_b, weights):
+def project(info, held_a, held_b, pieces):
     n, length, width = held_a.shape
     groups = info.shape[0] // 2
-    half = weights.shape[1] // 2
+    half = 4 * HD
     whole = pl.BlockSpec((n, length, width), lambda g, s: (0, 0, 0))
     return pl.pallas_call(
         project_kernel,
         grid_spec=pltpu.PrefetchScalarGridSpec(
             num_scalar_prefetch=1,
             grid=(groups,),
-            in_specs=[whole, whole, pl.BlockSpec(weights.shape, lambda g, s: (0, 0))],
+            in_specs=[whole, whole] + [pl.BlockSpec((2 * width, HD), lambda g, s: (0, 0))] * 4,
             out_specs=[
                 pl.BlockSpec((1, half, 2 * length), lambda g, s: (g, 0, 0)),
                 pl.BlockSpec((1, 2 * length, half), lambda g, s: (g, 0, 0)),
             ],
+            scratch_shapes=[pltpu.VMEM((width, 2 * half), BF)],
         ),
         out_shape=[
             jax.ShapeDtypeStruct((groups, half, 2 * length), BF),
@@ -284,18 +292,17 @@
         compiler_params=params(40),
         cost_estimate=pl.CostEstimate(flops=4 << 30, bytes_accessed=12 << 20, transcendentals=0),
         name="project",
-    )(info, held_a, held_b, weights)
-
-
-def cross_kernel(info, qa_ref, qb_ref, k_ref, v_ref, o_ref, lse_ref):
+    )(info, held_a, held_b, *pieces)
+
+
+def cross_kernel(info, q_ref, k_ref, v_ref, o_ref, lse_ref):
     step = pl.program_id(0)
     per = k_ref.shape[0]
     group = lse_ref.shape[2]
-    late = step * 2 >= pl.num_programs(0)
     for c in range(per):
         rows = slice(c * group, (c + 1) * group)
         g = per * step + c
-        q = jnp.where(late, qb_ref[rows], qa_ref[rows])
+        q = q_ref[rows]
         first, second = info[2 * g] >= 0, info[2 * g + 1] >= 0
         column = lax.broadcasted_iota(jnp.int32, (1, k_ref.shape[2]), 1)
         bias = jnp.where(
@@ -316,22 +323,21 @@
         lse_ref[c] = stats.T[:8]
 
 
-def cross(info, queries_a, queries_b, keys, values):
-    groups = keys.shape[0]
+def cross(half, info, queries, keys, values):
+    groups = keys.shape[0] // 2
     per = 2
-    steps = groups // per
-    group = queries_a.shape[0] * 2 // groups
-    width = queries_a.shape[1]
+    start = half * groups // per
+    group = queries.shape[0] // groups
+    width = queries.shape[1]
     return pl.pallas_call(
         cross_kernel,
         grid_spec=pltpu.PrefetchScalarGridSpec(
             num_scalar_prefetch=1,
-            grid=(steps,),
+            grid=(groups // per,),
             in_specs=[
-                pl.BlockSpec((per * group, width), lambda g, s: (jnp.minimum(g, steps // 2 - 1), 0)),
-                pl.BlockSpec((per * group, width), lambda g, s: (jnp.maximum(g - steps // 2, 0), 0)),
-                pl.BlockSpec((per,) + keys.shape[1:], lambda g, s: (g, 0, 0)),
-                pl.BlockSpec((per,) + values.shape[1:], lambda g, s: (g, 0, 0)),
+                pl.BlockSpec((per * group, width), lambda g, s: (g, 0)),
+                pl.BlockSpec((per,) + keys.shape[1:], lambda g, s: (start + g, 0, 0)),
+                pl.BlockSpec((per,) + values.shape[1:], lambda g, s: (start + g, 0, 0)),
             ],
             out_specs=[
                 pl.BlockSpec((4, per * group, HD), lambda g, s: (0, g, 0)),
@@ -342,10 +348,10 @@
             jax.ShapeDtypeStruct((4, groups * group, HD), BF),
             jax.ShapeDtypeStruct((groups, 8, group), F32),
         ],
-        compiler_params=params(32),
-        cost_estimate=pl.CostEstimate(flops=1 << 30, bytes_accessed=5 << 20, transcendentals=0),
+        compiler_params=params(24),
+        cost_estimate=pl.CostEstimate(flops=2 << 30, bytes_accessed=3 << 20, transcendentals=0),
         name="cross",
-    )(info, queries_a, queries_b, keys, values)
+    )(info, queries, keys, values)
 
 
 def merge(o_a, lse_a, o_b, lse_b):
@@ -388,27 +394,30 @@
     flags = jnp.stack([y < 0, y >= 1, y >= 3, y >= 2] + [~late] * 4).astype(jnp.int32)
     m, acc = attend_own(q, kv0)
     m, acc = attend_middle(flags, q, qs, m, acc, kv0, kv1, kv2)
-    wall = jnp.concatenate([wq, wk, wv], axis=0)
-    half = wall.shape[0] // 2
-    w_up = ring(wall[:half], XX, -1)
-    w_down = ring(wall[half:], XX, 1)
+    skip = 2 * wk.shape[0]
+    cut = (wq.shape[0] - skip) // 2
+    up, down = jnp.concatenate([wk, wv, wq[:cut]], axis=0), wq[cut:]
+    up_x = ring(up, XX, -1)
+    down_x = ring(down, XX, 1)
     o, o_sent, lse = attend_last(flags, q, qs, m, acc, k3, v3)
     lse, lse_sent = lse[0], lse[1]
 
-    o_sent, lse_sent, w_up, w_down = lax.optimization_barrier((o_sent, lse_sent, w_up, w_down))
     o_back = lax.ppermute(o_sent, "x_hi", [(0, 1)])
     lse_back = lax.ppermute(lse_sent, "x_hi", [(0, 1)])
-    w_x = jnp.concatenate([w_up, w_down], axis=0)
-    w4 = jnp.concatenate([wall, swap(wall, "core"), w_x, swap(w_x, "core")], axis=1)
-    depth, width = wq.shape[0], wk.shape[0]
-    wq4 = w4[:depth].reshape(8, depth // 8, 4 * HD)
-    wkv4 = jnp.concatenate([w4[depth : depth + width], w4[depth + width :]], axis=1)
-    o_back, lse_back, wq4, wkv4 = lax.optimization_barrier((o_back, lse_back, wq4, wkv4))
+    o_back, lse_back, up_x, down_x = lax.optimization_barrier((o_back, lse_back, up_x, down_x))
+    ups = (up, swap(up, "core"), up_x, swap(up_x, "core"))
+    downs = (down, swap(down, "core"), down_x, swap(down_x, "core"))
+    wq4 = jnp.concatenate(
+        [
+            jnp.concatenate([a[skip:] for a in ups], axis=1),
+            jnp.concatenate(downs, axis=1),
+        ],
+        axis=0,
+    ).reshape(8, -1, 4 * HD)
 
     lse_back = jnp.where(late, lse_back.reshape(rows, 1), LOW)
     self_out = merge(o, lse.reshape(rows, 1), o_back, lse_back)
 
-    held_b = swap(held_a, "core")
     same = nb_shard.reshape(-1)[:, None] == nb_shard.reshape(-1)[None, :]
     n = nb_shard.size
     before = lax.broadcasted_iota(jnp.int32, (n, n), 1) < lax.broadcasted_iota(jnp.int32, (n, n), 0)
@@ -423,15 +432,17 @@
         ],
         axis=1,
     ).reshape(-1)
-    keys, values = project(info, held_a, held_b, wkv4)
 
     mine = lax.all_to_all(self_out.reshape(4, quarter, HD), XC, 0, 0)
     f1 = ring(mine, "z", 1)
     b1 = ring(mine, "z", -1)
+    f1, b1, held_a, wq4 = lax.optimization_barrier((f1, b1, held_a, wq4))
+    held_b = swap(held_a, "core")
     f2 = ring(f1, "z", 1)
     b2 = ring(b1, "z", -1)
     f3 = ring(f2, "z", 1)
     b3 = ring(b2, "z", -1)
+    keys, values = project(info, held_a, held_b, ups)
     f3, b3, keys, values = lax.optimization_barrier((f3, b3, keys, values))
     far_f = ring(f3[:2], "z", 1)
     far_b = ring(b3[2:], "z", -1)
@@ -443,14 +454,20 @@
     queries = (near + cross_queries(z, ((4, far),), wq4)).astype(BF)
 
     other = swap(queries, "x_lo")
+    o_a, lse_a = cross(0, info[: n // 4], queries, keys, values)
+    got_a = swap(o_a[2:], "x_lo")
     other = jnp.concatenate([other[:, 2 * HD :], other[:, : 2 * HD]], axis=1)
-    o, lse = cross(info, queries, other, keys, values)
-
-    lse = lse[:, :4].transpose(1, 0, 2).reshape(4, 2, 2 * HD)
-    o_got = swap(o[2:], "x_lo").reshape(2, 2, quarter, HD)[:, ::-1]
-    lse_got = swap(lse[2:], "x_lo")[:, ::-1]
-    both = merge(
-        o[:2].reshape(2, 2, quarter, HD), lse[:2][..., None], o_got, lse_got[..., None]
+    o_b, lse_b = cross(1, info[n // 4 :], other, keys, values)
+    got_b = swap(o_b[2:], "x_lo")
+
+    lse = jnp.stack([lse_a[:, :4], lse_b[:, :4]]).transpose(2, 0, 1, 3).reshape(4, 2, quarter, 1)
+    lse_got = swap(lse[2:].reshape(2, 2, quarter), "x_lo")[..., None]
+    both = jnp.stack(
+        [
+            merge(o_a[:2], lse[:2, 0], got_b, lse_got[:, 1]),
+            merge(o_b[:2], lse[:2, 1], got_a, lse_got[:, 0]),
+        ],
+        axis=1,
     )
     kept, got = both[0], swap(both[1], "core")
     kept, got = (jnp.where(x_lo == 0, a, a[::-1]) for a in (kept, got))

time: 149 us -> 139 us (0.933)
  waiting for transfers between devices: 44.3 us -> 19.7 us
  starting transfers between devices: 37.5 us -> 49 us
  Pallas kernels: 19.9 us -> 23.4 us
  other arithmetic: 11.7 us -> 14.4 us
  local copies, waits for them, and re-layouts: 12.7 us -> 10.2 us
    all_gather x1, waiting for transfers between devices: 13.5 us -> 0.01 us  [local(): held_a = lax.all_gather(pair, 'z', axis=0, tiled=True)]
    ppermute x14, waiting for transfers between devices: 17.4 us -> 5.78 us  [ring(): return lax.ppermute(value, axis, [(i, (i + step) % n) for i in range(n)])]
    ppermute x7 -> x10, starting transfers between devices: 12.5 us -> 17.7 us  [swap(): return lax.ppermute(value, axis, [(0, 1), (1, 0)])]
    ppermute x1, waiting for transfers between devices: 0.01 us -> 4.84 us  [local(): lse_back = lax.ppermute(lse_sent, 'x_hi', [(0, 1)])]
    ppermute x14, starting transfers between devices: 15.5 us -> 19.6 us  [ring(): return lax.ppermute(value, axis, [(i, (i + step) % n) for i in range(n)])]
    ppermute x7 -> x10, waiting for transfers between devices: 9.28 us -> 6.24 us  [swap(): return lax.ppermute(value, axis, [(0, 1), (1, 0)])]
    concatenate x2 -> x0, local copies, waits for them, and re-layouts: 2.88 us -> none  [the longest x1 1.65 us: local(): wall = jnp.concatenate([wq, wk, wv], axis=0)]
    concatenate x2, other arithmetic: 6.12 us -> 8.85 us  [the longest x1 7.75 us: local(): jnp.concatenate([jnp.concatenate([a[skip:] for a in ups], axis=1), jnp.co...]
  transfers between devices with their start and end apart: 26 -> 29, of which waited for: 12 -> 10; matrix products, arithmetic and copies ran while one was open for 15% -> 17% of each run, Pallas kernels for 12% -> 17%
where the time goes in v5:
time: 139 us; the launch traced here: 138 us
  starting transfers between devices  49 us (35%)
  Pallas kernels  23.4 us (17%)
  waiting for transfers between devices  19.7 us (14%)
  between operations  15.9 us (11%)
  other arithmetic  14.4 us (10%)
  local copies, waits for them, and re-layouts  10.2 us (7%)
  matrix products  5.56 us (4%)
    ppermute x14, starting transfers between devices, ring(): return lax.ppermute(value, axis, [(i, (i + step) % n) for i in range(n)])  19.6 us
    ppermute x10, starting transfers between devices, swap(): return lax.ppermute(value, axis, [(0, 1), (1, 0)])  17.7 us
    pallas_call x1, Pallas kernels, project(): pl.pallas_call(project_kernel, grid_spec=pltpu.PrefetchScalarGridSpec(num...  9.34 us
    concatenate x1, other arithmetic, local(): jnp.concatenate([jnp.concatenate([a[skip:] for a in ups], axis=1), jnp.co...  7.75 us
    ppermute x10, waiting for transfers between devices, swap(): return lax.ppermute(value, axis, [(0, 1), (1, 0)])  6.24 us
    ppermute x14, waiting for transfers between devices, ring(): return lax.ppermute(value, axis, [(i, (i + step) % n) for i in range(n)])  5.78 us
    pallas_call x1, Pallas kernels, attend_middle(): pl.pallas_call(middle_kernel, grid_spec=pltpu.PrefetchScalarGridSpec(num_...  5.58 us
    dot_general x8, matrix products, cross_queries(): total = total + jnp.dot(a, w, preferred_element_type=F32)  5.56 us
  transfers between devices with their start and end apart: 29, of which 10 were waited for; matrix products, arithmetic and copies ran while one was open for 17% of the time, Pallas kernels for 17%

profile of v5, /device:TPU:31, one launch (start us, length us, event | category | flops | bytes accessed | tf_op | source)
XLA Modules:
  0.0 138.1 jit_solution(14926346605289768644)
XLA Ops:
  7.2 1.1 pad_maximum_fusion.1.kv_ref.kv0
  8.4 1.3 select_reduce_fusion.1
  11.0 1.1 constant_dynamic-slice_fusion.2
  12.1 0.8 pad_maximum_fusion.2
  13.0 1.5 %collective-permute-start.2 = (bf16[2,1024,128]{2,1,0:T(8,128)(2,1)S(1)}, bf16[2,1024,128]{2,1,0:T(8,128)(2,1)S(1)}, u32[]{:S(2)}, u32[]{:S(2)}) collective-permute-start(bf16[2,1024,128]{2,1,0:T(8,128)(2,1)S(1)} %pad_maximum_fusion.1.kv_ref.kv0), channel_id=1, source_target_pairs={{0,96},{32,0},{64,32},{96,64},{1,97},{33,1},{65,33},{97,65},{2,98}... | collective-permute-start | bytes 1572872 | tf_op jit(solution)/shard_map/ppermute | solution.py:26
  14.5 3.7 %collective-permute-start = (bf16[1024,128]{1,0:T(8,128)(2,1)}, bf16[1024,128]{1,0:T(8,128)(2,1)}, u32[]{:S(2)}, u32[]{:S(2)}) collective-permute-start(bf16[1024,128]{1,0:T(8,128)(2,1)} %q_ref.5), channel_id=1, source_target_pairs={{128,0},{129,1},{130,2},{131,3},{132,4},{133,5},{134,6},{135,7},{1... | collective-permute-start | bytes 786440 | tf_op jit(solution)/shard_map/ppermute | solution.py:391
  18.2 1.0 slice.187
  19.9 1.1 pad_maximum_fusion.w0
  21.1 2.1 %slice.188 = bf16[2944,128]{1,0:T(8,128)(2,1)} slice(bf16[4096,128]{1,0:T(8,128)(2,1)} %param.17), slice={[1152:4096], [0:128]} | slice | bytes 1507328 | tf_op jit(solution)/shard_map/slice | solution.py:399
  23.2 2.7 %collective-permute-start.8 = (bf16[2944,128]{1,0:T(8,128)(2,1)}, bf16[2944,128]{1,0:T(8,128)(2,1)}, u32[]{:S(2)}, u32[]{:S(2)}) collective-permute-start(bf16[2944,128]{1,0:T(8,128)(2,1)} %slice.188), channel_id=1, source_target_pairs={{0,2},{2,128},{128,130},{130,0},{1,3},{3,129},{129,131},{131,1},{4... | collective-permute-start | bytes 2261000 | tf_op jit(solution)/shard_map/ppermute | solution.py:26
  26.0 1.3 attend_own.1
  27.3 1.4 %collective-permute-start.3 = (bf16[1024,128]{1,0:T(8,128)(2,1)S(1)}, bf16[1024,128]{1,0:T(8,128)(2,1)S(1)}, u32[]{:S(2)}, u32[]{:S(2)}) collective-permute-start(bf16[1024,128]{1,0:T(8,128)(2,1)S(1)} %slice_bitcast_fusion.1), channel_id=1, source_target_pairs={{0,32},{32,64},{64,96},{96,0},{1,33},{33,65},{65,97},{97,1},{2,34}... | collective-permute-start | bytes 786440 | tf_op jit(solution)/shard_map/ppermute | solution.py:26
  29.0 5.6 %attend_middle.1 = (f32[2,1024,128]{2,1,0:T(8,128)S(1)}, f32[2,1024,256]{2,1,0:T(8,128)S(1)}) custom-call(s32[8]{0:T(128)S(1)} %convert_element_type.33.flags, bf16[1024,128]{1,0:T(8,128)(2,1)S(1)} %copy-done.1, bf16[1024,128]{1,0:T(8,128)(2,1)} %collective-permute-done.qs_ref, f32[1024,128]{1,0:T(8,128)S(1)} %get-tuple-element.34.m_in, ...), custom_call_target="tpu_custom_call" | custom-call | flops 8589934592 | bytes 6291456 | tf_op jit(solution)/shard_map/attend_middle/pallas_call | solution.py:135
  34.6 1.1 collective-permute-done.4.v3
  35.7 3.9 %attend_last.1 = (f32[1024,128]{1,0:T(8,128)S(1)}, bf16[1024,128]{1,0:T(8,128)(2,1)S(1)}, f32[2,4,1,256]{3,2,1,0:T(1,128)S(1)}) custom-call(s32[8]{0:T(128)S(1)} %convert_element_type.33.flags, bf16[1024,128]{1,0:T(8,128)(2,1)S(1)} %copy-done.1, bf16[1024,128]{1,0:T(8,128)(2,1)} %collective-permute-done.qs_ref, f32[2,1024,128]{2,1,0:T(8,128)S(1)} %get-tuple-element.36.m_in, ...), custom_call_target="tpu_custom_call" | custom-call | flops 3221225472 | bytes 6291456 | tf_op jit(solution)/shard_map/attend_last/pallas_call | solution.py:206
  39.6 1.3 collective-permute-start.5
  41.0 1.3 collective-permute-start.6
  42.3 3.1 %collective-permute-start.11 = (bf16[2944,128]{1,0:T(8,128)(2,1)S(1)}, bf16[2944,128]{1,0:T(8,128)(2,1)S(1)}, u32[]{:S(2)}, u32[]{:S(2)}) collective-permute-start(bf16[2944,128]{1,0:T(8,128)(2,1)S(1)} %pad_maximum_fusion.w0), channel_id=1, source_target_pairs={{0,1},{1,0},{2,3},{3,2},{4,5},{5,4},{6,7},{7,6},{8,9},{9,8},{10,11... | collective-permute-start | bytes 2261000 | tf_op jit(solution)/shard_map/ppermute | solution.py:30
  45.5 4.8 %collective-permute-done.6 = f32[4,1,256]{2,1,0:T(1,128)S(1)} collective-permute-done((f32[4,1,256]{2,1,0:T(1,128)S(1)}, f32[4,1,256]{2,1,0:T(1,128)S(1)}, u32[]{:S(2)}, u32[]{:S(2)}) %collective-permute-start.6) | collective-permute-done | bytes 4128 | tf_op jit(solution)/shard_map/ppermute | solution.py:406
  50.3 3.2 %collective-permute-start.12 = (bf16[2944,128]{1,0:T(8,128)(2,1)S(1)}, bf16[2944,128]{1,0:T(8,128)(2,1)S(1)}, u32[]{:S(2)}, u32[]{:S(2)}) collective-permute-start(bf16[2944,128]{1,0:T(8,128)(2,1)S(1)} %collective-permute-done.7.w2), channel_id=1, source_target_pairs={{0,1},{1,0},{2,3},{3,2},{4,5},{5,4},{6,7},{7,6},{8,9},{9,8},{10,11... | collective-permute-start | bytes 2261000 | tf_op jit(solution)/shard_map/ppermute | solution.py:30
  53.5 1.2 divide_convert_fusion
  54.7 5.3 %all-to-all-start = ((bf16[4,256,128]{2,1,0:T(8,128)(2,1)}), bf16[4,256,128]{2,1,0:T(8,128)(2,1)}, u32[]{:S(2)}, u32[]{:S(2)}) async-start(bf16[4,256,128]{2,1,0:T(8,128)(2,1)} %bitcast.172), calls=%async_computation | async-start | bytes 524288 | tf_op jit(solution)/shard_map/all_to_all | solution.py:436
  60.0 0.7 slice.245
  61.4 2.8 %all-to-all-done = bf16[4,256,128]{2,1,0:T(8,128)(2,1)} async-done(((bf16[4,256,128]{2,1,0:T(8,128)(2,1)}), bf16[4,256,128]{2,1,0:T(8,128)(2,1)}, u32[]{:S(2)}, u32[]{:S(2)}) %all-to-all-start) | async-done | bytes 262176 | tf_op jit(solution)/shard_map/all_to_all | solution.py:436
  64.2 5.6 %collective-permute-start.10 = (bf16[4,256,128]{2,1,0:T(8,128)(2,1)}, bf16[4,256,128]{2,1,0:T(8,128)(2,1)}, u32[]{:S(2)}, u32[]{:S(2)}) collective-permute-start(bf16[4,256,128]{2,1,0:T(8,128)(2,1)} %all-to-all-done), channel_id=1, source_target_pairs={{0,28},{4,0},{8,4},{12,8},{16,12},{20,16},{24,20},{28,24},{1,29},{... | collective-permute-start | bytes 786440 | tf_op jit(solution)/shard_map/ppermute | solution.py:26
  69.8 7.8 %maximum_maximum_fusion = bf16[4096,512]{1,0:T(8,128)(2,1)} fusion(bf16[2944,128]{1,0:T(8,128)(2,1)} %collective-permute-done.14, bf16[2944,128]{1,0:T(8,128)(2,1)} %collective-permute-done.8, bf16[2944,128]{1,0:T(8,128)(2,1)} %collective-permute-done.13, bf16[2944,128]{1,0:T(8,128)(2,1)} %slice.188, bf16[1152,128]{1,0:T(8,128)(2,1)S(1)} %slice.246, ...), kind=kLoop, calls=%fused_computation | loop fusion | flops 33554432 | bytes 8388608 | tf_op jit(solution)/shard_map/concatenate | solution.py:410
  78.2 1.8 %collective-permute-start.19 = (bf16[16,128,896]{2,1,0:T(8,128)(2,1)}, bf16[16,128,896]{2,1,0:T(8,128)(2,1)}, u32[]{:S(2)}, u32[]{:S(2)}) collective-permute-start(bf16[16,128,896]{2,1,0:T(8,128)(2,1)} %all-gather.2.cloned.1.call-done.a_ref), channel_id=1, source_target_pairs={{0,1},{1,0},{2,3},{3,2},{4,5},{5,4},{6,7},{7,6},{8,9},{9,8},{10,11... | collective-permute-start | bytes 11010056 | tf_op jit(solution)/shard_map/ppermute | solution.py:30
  80.7 1.1 slice_bitcast_fusion.13
  81.9 2.7 %collective-permute-start.17 = (bf16[4,256,128]{2,1,0:T(8,128)(2,1)}, bf16[4,256,128]{2,1,0:T(8,128)(2,1)S(1)}, u32[]{:S(2)}, u32[]{:S(2)}) collective-permute-start(bf16[4,256,128]{2,1,0:T(8,128)(2,1)} %collective-permute-done.10), channel_id=1, source_target_pairs={{0,28},{4,0},{8,4},{12,8},{16,12},{20,16},{24,20},{28,24},{1,29},{... | collective-permute-start | bytes 786440 | tf_op jit(solution)/shard_map/ppermute | solution.py:26
  84.6 1.1 slice_bitcast_fusion.21
  85.7 1.3 fusion.8
  87.0 1.4 convolution_add_fusion.5
  88.4 2.9 %collective-permute-done.15 = bf16[4,256,128]{2,1,0:T(8,128)(2,1)S(1)} collective-permute-done((bf16[4,256,128]{2,1,0:T(8,128)(2,1)}, bf16[4,256,128]{2,1,0:T(8,128)(2,1)S(1)}, u32[]{:S(2)}, u32[]{:S(2)}) %collective-permute-start.15) | collective-permute-done | bytes 262176 | tf_op jit(solution)/shard_map/ppermute | solution.py:26
  91.3 2.7 %collective-permute-start.18 = (bf16[4,256,128]{2,1,0:T(8,128)(2,1)S(1)}, bf16[4,256,128]{2,1,0:T(8,128)(2,1)S(1)}, u32[]{:S(2)}, u32[]{:S(2)}) collective-permute-start(bf16[4,256,128]{2,1,0:T(8,128)(2,1)S(1)} %collective-permute-done.17), channel_id=1, source_target_pairs={{0,28},{4,0},{8,4},{12,8},{16,12},{20,16},{24,20},{28,24},{1,29},{... | collective-permute-start | bytes 786440 | tf_op jit(solution)/shard_map/ppermute | solution.py:26
  94.0 1.4 convolution_add_fusion.4
  95.4 9.3 %project.1 = (bf16[8,512,256]{2,1,0:T(8,128)(2,1)S(1)}, bf16[8,256,512]{2,1,0:T(8,128)(2,1)S(1)}) custom-call(s32[16]{0:T(128)S(1)} %add_bitcast_fusion.info, bf16[16,128,896]{2,1,0:T(8,128)(2,1)S(1)} %copy-done, bf16[16,128,896]{2,1,0:T(8,128)(2,1)} %collective-permute-done.19.b_ref, bf16[2944,128]{1,0:T(8,128)(2,1)S(1)} %pad_maximum_fusion.w0, ...), custom_call_target="tpu_custom_call" | custom-call | flops 4294967296 | bytes 12582912 | tf_op jit(solution)/shard_map/project/pallas_call | solution.py:276
  104.9 2.7 %collective-permute-start.21 = (bf16[2,256,128]{2,1,0:T(8,128)(2,1)S(1)}, bf16[2,256,128]{2,1,0:T(8,128)(2,1)S(1)}, u32[]{:S(2)}, u32[]{:S(2)}) collective-permute-start(bf16[2,256,128]{2,1,0:T(8,128)(2,1)S(1)} %slice.194), channel_id=1, source_target_pairs={{0,28},{4,0},{8,4},{12,8},{16,12},{20,16},{24,20},{28,24},{1,29},{... | collective-permute-start | bytes 393224 | tf_op jit(solution)/shard_map/ppermute | solution.py:26
  108.8 1.1 collective-permute-done.20
  110.4 1.2 collective-permute-start.22
  111.6 1.7 %cross.2 = (bf16[4,256,128]{2,1,0:T(8,128)(2,1)S(1)}, f32[4,8,64]{2,1,0:T(8,128)S(1)}) custom-call(s32[8]{0:T(128)S(1)} %bitcast.163, bf16[256,512]{1,0:T(8,128)(2,1)S(1)} %add_convert_fusion.q_ref, bf16[8,512,256]{2,1,0:T(8,128)(2,1)S(1)} %get-tuple-element.58.k_ref, bf16[8,256,512]{2,1,0:T(8,128)(2,1)S(1)} %get-tuple-element.59.v_ref), custom_call_target="tpu_custom_call" | custom-call | flops 2147483648 | bytes 3145728 | tf_op jit(solution)/shard_map/cross/pallas_call | solution.py:332
  113.7 2.0 %collective-permute-done.22 = bf16[256,512]{1,0:T(8,128)(2,1)S(1)} collective-permute-done((bf16[256,512]{1,0:T(8,128)(2,1)S(1)}, bf16[256,512]{1,0:T(8,128)(2,1)S(1)}, u32[]{:S(2)}, u32[]{:S(2)}) %collective-permute-start.22) | collective-permute-done | bytes 262176 | tf_op jit(solution)/shard_map/ppermute | solution.py:30
  115.7 1.7 %cross.3 = (bf16[4,256,128]{2,1,0:T(8,128)(2,1)S(1)}, f32[4,8,64]{2,1,0:T(8,128)S(1)}) custom-call(s32[8]{0:T(128)S(1)} %bitcast.162, bf16[256,512]{1,0:T(8,128)(2,1)S(1)} %pad_maximum_fusion.3.q_ref, bf16[8,512,256]{2,1,0:T(8,128)(2,1)S(1)} %get-tuple-element.58.k_ref, bf16[8,256,512]{2,1,0:T(8,128)(2,1)S(1)} %get-tuple-element.59.v_ref), custom_call_target="tpu_custom_call" | custom-call | flops 2147483648 | bytes 3145728 | tf_op jit(solution)/shard_map/cross/pallas_call | solution.py:332
  117.6 1.1 collective-permute-start.23
  119.2 1.2 collective-permute-done.23
  120.7 2.1 %collective-permute-done.24 = bf16[2,256,128]{2,1,0:T(8,128)(2,1)S(1)} collective-permute-done((bf16[2,256,128]{2,1,0:T(8,128)(2,1)S(1)}, bf16[2,256,128]{2,1,0:T(8,128)(2,1)S(1)}, u32[]{:S(2)}, u32[]{:S(2)}) %collective-permute-start.24) | collective-permute-done | bytes 131104 | tf_op jit(solution)/shard_map/ppermute | solution.py:30
  123.2 6.3 %collective-permute-start.26 = (bf16[2,256,128]{2,1,0:T(8,128)(2,1)S(1)}, bf16[2,256,128]{2,1,0:T(8,128)(2,1)S(1)}, u32[]{:S(2)}, u32[]{:S(2)}) collective-permute-start(bf16[2,256,128]{2,1,0:T(8,128)(2,1)S(1)} %get-tuple-element.78), channel_id=1, source_target_pairs={{0,1},{1,0},{2,3},{3,2},{4,5},{5,4},{6,7},{7,6},{8,9},{9,8},{10,11... | collective-permute-start | bytes 393224 | tf_op jit(solution)/shard_map/ppermute | solution.py:30
  129.5 1.0 collective-permute-done.26
  130.5 0.7 copy.37
  (96 shorter events, 7.2 us)
Async XLA Ops:
  7.2 18.8 %copy-start.1 = (bf16[1024,128]{1,0:T(8,128)(2,1)S(1)}, bf16[1024,128]{1,0:T(8,128)(2,1)}, u32[]{:S(2)}) copy-start(bf16[1024,128]{1,0:T(8,128)(2,1)} %q_ref.5) | copy-start | bytes 786436
  7.2 71.1 %all-gather.2.cloned.1.call-start = ((), (), s32[]{:S(2)}) async-start(), calls=%async_computation.1 | async-start | bytes 4128768 | tf_op jit(solution)/shard_map/all_gather | solution.py:387
  12.9 14.3 %collective-permute-start.1 = (bf16[2,1024,128]{2,1,0:T(8,128)(2,1)S(1)}, bf16[2,1024,128]{2,1,0:T(8,128)(2,1)S(1)}, u32[]{:S(2)}, u32[]{:S(2)}) collective-permute-start(bf16[2,1024,128]{2,1,0:T(8,128)(2,1)S(1)} %pad_maximum_fusion.1.kv_ref.kv0), channel_id=1, source_target_pairs={{0,32},{32,64},{64,96},{96,0},{1,33},{33,65},{65,97},{97,1},{2,34}... | collective-permute-start | bytes 1572872 | tf_op jit(solution)/shard_map/ppermute | solution.py:26
  13.0 15.7 %collective-permute-start.2 = (bf16[2,1024,128]{2,1,0:T(8,128)(2,1)S(1)}, bf16[2,1024,128]{2,1,0:T(8,128)(2,1)S(1)}, u32[]{:S(2)}, u32[]{:S(2)}) collective-permute-start(bf16[2,1024,128]{2,1,0:T(8,128)(2,1)S(1)} %pad_maximum_fusion.1.kv_ref.kv0), channel_id=1, source_target_pairs={{0,96},{32,0},{64,32},{96,64},{1,97},{33,1},{65,33},{97,65},{2,98}... | collective-permute-start | bytes 1572872 | tf_op jit(solution)/shard_map/ppermute | solution.py:26
  14.5 14.5 %collective-permute-start = (bf16[1024,128]{1,0:T(8,128)(2,1)}, bf16[1024,128]{1,0:T(8,128)(2,1)}, u32[]{:S(2)}, u32[]{:S(2)}) collective-permute-start(bf16[1024,128]{1,0:T(8,128)(2,1)} %q_ref.5), channel_id=1, source_target_pairs={{128,0},{129,1},{130,2},{131,3},{132,4},{133,5},{134,6},{135,7},{1... | collective-permute-start | bytes 786440 | tf_op jit(solution)/shard_map/ppermute | solution.py:391
  19.2 0.7 copy-start.3
  21.0 24.3 %collective-permute-start.7 = (bf16[2944,128]{1,0:T(8,128)(2,1)S(1)}, bf16[2944,128]{1,0:T(8,128)(2,1)S(1)}, u32[]{:S(2)}, u32[]{:S(2)}) collective-permute-start(bf16[2944,128]{1,0:T(8,128)(2,1)S(1)} %pad_maximum_fusion.w0), channel_id=1, source_target_pairs={{0,130},{2,0},{128,2},{130,128},{1,131},{3,1},{129,3},{131,129},{4... | collective-permute-start | bytes 2261000 | tf_op jit(solution)/shard_map/ppermute | solution.py:26
  23.2 22.2 %collective-permute-start.8 = (bf16[2944,128]{1,0:T(8,128)(2,1)}, bf16[2944,128]{1,0:T(8,128)(2,1)}, u32[]{:S(2)}, u32[]{:S(2)}) collective-permute-start(bf16[2944,128]{1,0:T(8,128)(2,1)} %slice.188), channel_id=1, source_target_pairs={{0,2},{2,128},{128,130},{130,0},{1,3},{3,129},{129,131},{131,1},{4... | collective-permute-start | bytes 2261000 | tf_op jit(solution)/shard_map/ppermute | solution.py:26
  27.3 7.2 %collective-permute-start.3 = (bf16[1024,128]{1,0:T(8,128)(2,1)S(1)}, bf16[1024,128]{1,0:T(8,128)(2,1)S(1)}, u32[]{:S(2)}, u32[]{:S(2)}) collective-permute-start(bf16[1024,128]{1,0:T(8,128)(2,1)S(1)} %slice_bitcast_fusion.1), channel_id=1, source_target_pairs={{0,32},{32,64},{64,96},{96,0},{1,33},{33,65},{65,97},{97,1},{2,34}... | collective-permute-start | bytes 786440 | tf_op jit(solution)/shard_map/ppermute | solution.py:26
  28.7 7.0 %collective-permute-start.4 = (bf16[1024,128]{1,0:T(8,128)(2,1)S(1)}, bf16[1024,128]{1,0:T(8,128)(2,1)S(1)}, u32[]{:S(2)}, u32[]{:S(2)}) collective-permute-start(bf16[1024,128]{1,0:T(8,128)(2,1)S(1)} %slice_bitcast_fusion), channel_id=1, source_target_pairs={{0,96},{32,0},{64,32},{96,64},{1,97},{33,1},{65,33},{97,65},{2,98}... | collective-permute-start | bytes 786440 | tf_op jit(solution)/shard_map/ppermute | solution.py:26
  35.7 34.1 %copy-start.4 = (bf16[1152,128]{1,0:T(8,128)(2,1)S(1)}, bf16[1152,128]{1,0:T(8,128)(2,1)}, u32[]{:S(2)}) copy-start(bf16[1152,128]{1,0:T(8,128)(2,1)} %copy-done.3) | copy-start | bytes 884740
  39.6 10.7 %collective-permute-start.5 = (bf16[1024,128]{1,0:T(8,128)(2,1)S(1)}, bf16[1024,128]{1,0:T(8,128)(2,1)S(1)}, u32[]{:S(2)}, u32[]{:S(2)}) collective-permute-start(bf16[1024,128]{1,0:T(8,128)(2,1)S(1)} %get-tuple-element.40), channel_id=1, source_target_pairs={{0,128},{1,129},{2,130},{3,131},{4,132},{5,133},{6,134},{7,135},{8... | collective-permute-start | bytes 786440 | tf_op jit(solution)/shard_map/ppermute | solution.py:405
  41.0 9.4 %collective-permute-start.6 = (f32[4,1,256]{2,1,0:T(1,128)S(1)}, f32[4,1,256]{2,1,0:T(1,128)S(1)}, u32[]{:S(2)}, u32[]{:S(2)}) collective-permute-start(f32[4,1,256]{2,1,0:T(1,128)S(1)} %get-tuple-element.116), channel_id=1, source_target_pairs={{0,128},{1,129},{2,130},{3,131},{4,132},{5,133},{6,134},{7,135},{8... | collective-permute-start | bytes 12296 | tf_op jit(solution)/shard_map/ppermute | solution.py:406
  42.3 17.7 %collective-permute-start.11 = (bf16[2944,128]{1,0:T(8,128)(2,1)S(1)}, bf16[2944,128]{1,0:T(8,128)(2,1)S(1)}, u32[]{:S(2)}, u32[]{:S(2)}) collective-permute-start(bf16[2944,128]{1,0:T(8,128)(2,1)S(1)} %pad_maximum_fusion.w0), channel_id=1, source_target_pairs={{0,1},{1,0},{2,3},{3,2},{4,5},{5,4},{6,7},{7,6},{8,9},{9,8},{10,11... | collective-permute-start | bytes 2261000 | tf_op jit(solution)/shard_map/ppermute | solution.py:30
  45.4 24.5 %collective-permute-start.13 = (bf16[2944,128]{1,0:T(8,128)(2,1)}, bf16[2944,128]{1,0:T(8,128)(2,1)}, u32[]{:S(2)}, u32[]{:S(2)}) collective-permute-start(bf16[2944,128]{1,0:T(8,128)(2,1)} %slice.188), channel_id=1, source_target_pairs={{0,1},{1,0},{2,3},{3,2},{4,5},{5,4},{6,7},{7,6},{8,9},{9,8},{10,11... | collective-permute-start | bytes 2261000 | tf_op jit(solution)/shard_map/ppermute | solution.py:30
  50.3 19.5 %collective-permute-start.12 = (bf16[2944,128]{1,0:T(8,128)(2,1)S(1)}, bf16[2944,128]{1,0:T(8,128)(2,1)S(1)}, u32[]{:S(2)}, u32[]{:S(2)}) collective-permute-start(bf16[2944,128]{1,0:T(8,128)(2,1)S(1)} %collective-permute-done.7.w2), channel_id=1, source_target_pairs={{0,1},{1,0},{2,3},{3,2},{4,5},{5,4},{6,7},{7,6},{8,9},{9,8},{10,11... | collective-permute-start | bytes 2261000 | tf_op jit(solution)/shard_map/ppermute | solution.py:30
  53.5 16.3 %collective-permute-start.14 = (bf16[2944,128]{1,0:T(8,128)(2,1)}, bf16[2944,128]{1,0:T(8,128)(2,1)}, u32[]{:S(2)}, u32[]{:S(2)}) collective-permute-start(bf16[2944,128]{1,0:T(8,128)(2,1)} %collective-permute-done.8), channel_id=1, source_target_pairs={{0,1},{1,0},{2,3},{3,2},{4,5},{5,4},{6,7},{7,6},{8,9},{9,8},{10,11... | collective-permute-start | bytes 2261000 | tf_op jit(solution)/shard_map/ppermute | solution.py:30
  54.7 9.5 %all-to-all-start = ((bf16[4,256,128]{2,1,0:T(8,128)(2,1)}), bf16[4,256,128]{2,1,0:T(8,128)(2,1)}, u32[]{:S(2)}, u32[]{:S(2)}) async-start(bf16[4,256,128]{2,1,0:T(8,128)(2,1)} %bitcast.172), calls=%async_computation | async-start | bytes 524288 | tf_op jit(solution)/shard_map/all_to_all | solution.py:436
  64.2 13.4 %collective-permute-start.10 = (bf16[4,256,128]{2,1,0:T(8,128)(2,1)}, bf16[4,256,128]{2,1,0:T(8,128)(2,1)}, u32[]{:S(2)}, u32[]{:S(2)}) collective-permute-start(bf16[4,256,128]{2,1,0:T(8,128)(2,1)} %all-to-all-done), channel_id=1, source_target_pairs={{0,28},{4,0},{8,4},{12,8},{16,12},{20,16},{24,20},{28,24},{1,29},{... | collective-permute-start | bytes 786440 | tf_op jit(solution)/shard_map/ppermute | solution.py:26
  69.8 8.5 %collective-permute-start.9 = (bf16[4,256,128]{2,1,0:T(8,128)(2,1)}, bf16[4,256,128]{2,1,0:T(8,128)(2,1)}, u32[]{:S(2)}, u32[]{:S(2)}) collective-permute-start(bf16[4,256,128]{2,1,0:T(8,128)(2,1)} %all-to-all-done), channel_id=1, source_target_pairs={{0,4},{4,8},{8,12},{12,16},{16,20},{20,24},{24,28},{28,0},{1,5},{5... | collective-permute-start | bytes 786440 | tf_op jit(solution)/shard_map/ppermute | solution.py:26
  69.8 10.2 %copy-start.5 = (s32[16,2]{0,1:T(2,128)S(1)}, s32[16,2]{0,1:T(2,128)}, u32[]{:S(2)}) copy-start(s32[16,2]{0,1:T(2,128)} %param.13) | copy-start | bytes 388
  78.2 17.1 %collective-permute-start.19 = (bf16[16,128,896]{2,1,0:T(8,128)(2,1)}, bf16[16,128,896]{2,1,0:T(8,128)(2,1)}, u32[]{:S(2)}, u32[]{:S(2)}) collective-permute-start(bf16[16,128,896]{2,1,0:T(8,128)(2,1)} %all-gather.2.cloned.1.call-done.a_ref), channel_id=1, source_target_pairs={{0,1},{1,0},{2,3},{3,2},{4,5},{5,4},{6,7},{7,6},{8,9},{9,8},{10,11... | collective-permute-start | bytes 11010056 | tf_op jit(solution)/shard_map/ppermute | solution.py:30
  80.6 14.8 %copy-start = (bf16[16,128,896]{2,1,0:T(8,128)(2,1)S(1)}, bf16[16,128,896]{2,1,0:T(8,128)(2,1)}, u32[]{:S(2)}) copy-start(bf16[16,128,896]{2,1,0:T(8,128)(2,1)} %all-gather.2.cloned.1.call-done.a_ref) | copy-start | bytes 11010052
  81.8 9.4 %collective-permute-start.15 = (bf16[4,256,128]{2,1,0:T(8,128)(2,1)}, bf16[4,256,128]{2,1,0:T(8,128)(2,1)S(1)}, u32[]{:S(2)}, u32[]{:S(2)}) collective-permute-start(bf16[4,256,128]{2,1,0:T(8,128)(2,1)} %collective-permute-done.9), channel_id=1, source_target_pairs={{0,4},{4,8},{8,12},{12,16},{16,20},{20,24},{24,28},{28,0},{1,5},{5... | collective-permute-start | bytes 786440 | tf_op jit(solution)/shard_map/ppermute | solution.py:26
  81.9 9.4 %collective-permute-start.17 = (bf16[4,256,128]{2,1,0:T(8,128)(2,1)}, bf16[4,256,128]{2,1,0:T(8,128)(2,1)S(1)}, u32[]{:S(2)}, u32[]{:S(2)}) collective-permute-start(bf16[4,256,128]{2,1,0:T(8,128)(2,1)} %collective-permute-done.10), channel_id=1, source_target_pairs={{0,28},{4,0},{8,4},{12,8},{16,12},{20,16},{24,20},{28,24},{1,29},{... | collective-permute-start | bytes 786440 | tf_op jit(solution)/shard_map/ppermute | solution.py:26
  91.3 13.5 %collective-permute-start.16 = (bf16[4,256,128]{2,1,0:T(8,128)(2,1)S(1)}, bf16[4,256,128]{2,1,0:T(8,128)(2,1)S(1)}, u32[]{:S(2)}, u32[]{:S(2)}) collective-permute-start(bf16[4,256,128]{2,1,0:T(8,128)(2,1)S(1)} %collective-permute-done.15), channel_id=1, source_target_pairs={{0,4},{4,8},{8,12},{12,16},{16,20},{20,24},{24,28},{28,0},{1,5},{5... | collective-permute-start | bytes 786440 | tf_op jit(solution)/shard_map/ppermute | solution.py:26
  91.3 13.5 %collective-permute-start.18 = (bf16[4,256,128]{2,1,0:T(8,128)(2,1)S(1)}, bf16[4,256,128]{2,1,0:T(8,128)(2,1)S(1)}, u32[]{:S(2)}, u32[]{:S(2)}) collective-permute-start(bf16[4,256,128]{2,1,0:T(8,128)(2,1)S(1)} %collective-permute-done.17), channel_id=1, source_target_pairs={{0,28},{4,0},{8,4},{12,8},{16,12},{20,16},{24,20},{28,24},{1,29},{... | collective-permute-start | bytes 786440 | tf_op jit(solution)/shard_map/ppermute | solution.py:26
  95.3 12.2 %copy-start.2 = (bf16[4096,512]{1,0:T(8,128)(2,1)S(1)}, bf16[4096,512]{1,0:T(8,128)(2,1)}, u32[]{:S(2)}) copy-start(bf16[4096,512]{1,0:T(8,128)(2,1)} %maximum_maximum_fusion) | copy-start | bytes 12582916
  104.8 5.1 %collective-permute-start.20 = (bf16[2,256,128]{2,1,0:T(8,128)(2,1)S(1)}, bf16[2,256,128]{2,1,0:T(8,128)(2,1)S(1)}, u32[]{:S(2)}, u32[]{:S(2)}) collective-permute-start(bf16[2,256,128]{2,1,0:T(8,128)(2,1)S(1)} %slice.193), channel_id=1, source_target_pairs={{0,4},{4,8},{8,12},{12,16},{16,20},{20,24},{24,28},{28,0},{1,5},{5... | collective-permute-start | bytes 393224 | tf_op jit(solution)/shard_map/ppermute | solution.py:26
  104.9 5.0 %collective-permute-start.21 = (bf16[2,256,128]{2,1,0:T(8,128)(2,1)S(1)}, bf16[2,256,128]{2,1,0:T(8,128)(2,1)S(1)}, u32[]{:S(2)}, u32[]{:S(2)}) collective-permute-start(bf16[2,256,128]{2,1,0:T(8,128)(2,1)S(1)} %slice.194), channel_id=1, source_target_pairs={{0,28},{4,0},{8,4},{12,8},{16,12},{20,16},{24,20},{28,24},{1,29},{... | collective-permute-start | bytes 393224 | tf_op jit(solution)/shard_map/ppermute | solution.py:26
  110.4 5.3 %collective-permute-start.22 = (bf16[256,512]{1,0:T(8,128)(2,1)S(1)}, bf16[256,512]{1,0:T(8,128)(2,1)S(1)}, u32[]{:S(2)}, u32[]{:S(2)}) collective-permute-start(bf16[256,512]{1,0:T(8,128)(2,1)S(1)} %add_convert_fusion.q_ref), channel_id=1, source_target_pairs={{0,2},{2,0},{1,3},{3,1},{4,6},{6,4},{5,7},{7,5},{8,10},{10,8},{9,1... | collective-permute-start | bytes 786440 | tf_op jit(solution)/shard_map/ppermute | solution.py:30
  113.3 7.2 %collective-permute-start.25 = (bf16[2,256,128]{2,1,0:T(8,128)(2,1)S(1)}, bf16[2,256,128]{2,1,0:T(8,128)(2,1)S(1)}, u32[]{:S(2)}, u32[]{:S(2)}) collective-permute-start(bf16[2,256,128]{2,1,0:T(8,128)(2,1)S(1)} %slice.240), channel_id=1, source_target_pairs={{0,2},{2,0},{1,3},{3,1},{4,6},{6,4},{5,7},{7,5},{8,10},{10,8},{9,1... | collective-permute-start | bytes 393224 | tf_op jit(solution)/shard_map/ppermute | solution.py:30
  117.6 2.9 %collective-permute-start.23 = (f32[2,2,256]{2,0,1:T(2,128)S(1)}, f32[2,2,256]{2,0,1:T(2,128)S(1)}, u32[]{:S(2)}, u32[]{:S(2)}) collective-permute-start(f32[2,2,256]{2,0,1:T(2,128)S(1)} %reshape.202), channel_id=1, source_target_pairs={{0,2},{2,0},{1,3},{3,1},{4,6},{6,4},{5,7},{7,5},{8,10},{10,8},{9,1... | collective-permute-start | bytes 12296 | tf_op jit(solution)/shard_map/ppermute | solution.py:30
  118.8 4.0 %collective-permute-start.24 = (bf16[2,256,128]{2,1,0:T(8,128)(2,1)S(1)}, bf16[2,256,128]{2,1,0:T(8,128)(2,1)S(1)}, u32[]{:S(2)}, u32[]{:S(2)}) collective-permute-start(bf16[2,256,128]{2,1,0:T(8,128)(2,1)S(1)} %slice.236), channel_id=1, source_target_pairs={{0,2},{2,0},{1,3},{3,1},{4,6},{6,4},{5,7},{7,5},{8,10},{10,8},{9,1... | collective-permute-start | bytes 393224 | tf_op jit(solution)/shard_map/ppermute | solution.py:30
  123.2 7.3 %collective-permute-start.26 = (bf16[2,256,128]{2,1,0:T(8,128)(2,1)S(1)}, bf16[2,256,128]{2,1,0:T(8,128)(2,1)S(1)}, u32[]{:S(2)}, u32[]{:S(2)}) collective-permute-start(bf16[2,256,128]{2,1,0:T(8,128)(2,1)S(1)} %get-tuple-element.78), channel_id=1, source_target_pairs={{0,1},{1,0},{2,3},{3,2},{4,5},{5,4},{6,7},{7,6},{8,9},{9,8},{10,11... | collective-permute-start | bytes 393224 | tf_op jit(solution)/shard_map/ppermute | solution.py:30
Sparse Core Ops, SparseCore 0:
  13.1 52.5 all-gather.1

commit v6 on v5

--- a/solution.py
+++ b/solution.py
@@ -236,6 +236,26 @@
     )(flags, q, qs, m, acc, k3, v3)
 
 
+def side_kernel(skip, u0, u1, u2, u3, d0, d1, d2, d3, out):
+    cut = u0.shape[0] - skip
+    for r, (u, d) in enumerate(((u0, d0), (u1, d1), (u2, d2), (u3, d3))):
+        out[:cut, r * HD : (r + 1) * HD] = u[skip:]
+        out[cut:, r * HD : (r + 1) * HD] = d[...]
+
+
+def side_by_side(skip, ups, downs):
+    depth = ups[0].shape[0] - skip + downs[0].shape[0]
+    return pl.pallas_call(
+        functools.partial(side_kernel, skip),
+        in_specs=[pl.BlockSpec(memory_space=pltpu.VMEM)] * 8,
+        out_specs=pl.BlockSpec(memory_space=pltpu.VMEM),
+        out_shape=jax.ShapeDtypeStruct((depth, 4 * HD), BF),
+        compiler_params=pltpu.CompilerParams(vmem_limit_bytes=24 << 20),
+        cost_estimate=pl.CostEstimate(flops=1 << 20, bytes_accessed=10 << 20, transcendentals=0),
+        name="side_by_side",
+    )(*ups, *downs)
+
+
 def cross_queries(z, parts, weights):
     total = 0.0
     for back, part in parts:
@@ -257,15 +277,17 @@
             w_ref[:, (4 + r) * HD : (5 + r) * HD] = piece[width:]
 
     def pick(n):
-        slot = jnp.maximum(info[2 * g + n], 0)
+        slot = jnp.maximum(info[4 * g + n], 0)
         at = slot & (slots - 1)
         return jnp.where(slot < slots, a_ref[at], b_ref[at])
 
-    states = jnp.concatenate([pick(0), pick(1)], axis=0)
+    states = jnp.concatenate([pick(n) for n in range(4)], axis=0)
     both = jnp.dot(states, w_ref[...], preferred_element_type=F32).astype(BF)
     half = both.shape[1] // 2
-    k_ref[0] = both[:, :half].T
-    v_ref[0] = both[:, half:]
+    for c in range(2):
+        rows = slice(c * both.shape[0] // 2, (c + 1) * both.shape[0] // 2)
+        k_ref[c] = both[rows, :half].T
+        v_ref[c] = both[rows, half:]
 
 
 def project(info, held_a, held_b, pieces):
@@ -277,11 +299,11 @@
         project_kernel,
         grid_spec=pltpu.PrefetchScalarGridSpec(
             num_scalar_prefetch=1,
-            grid=(groups,),
+            grid=(groups // 2,),
             in_specs=[whole, whole] + [pl.BlockSpec((2 * width, HD), lambda g, s: (0, 0))] * 4,
             out_specs=[
-                pl.BlockSpec((1, half, 2 * length), lambda g, s: (g, 0, 0)),
-                pl.BlockSpec((1, 2 * length, half), lambda g, s: (g, 0, 0)),
+                pl.BlockSpec((2, half, 2 * length), lambda g, s: (g, 0, 0)),
+                pl.BlockSpec((2, 2 * length, half), lambda g, s: (g, 0, 0)),
             ],
             scratch_shapes=[pltpu.VMEM((width, 2 * half), BF)],
         ),
@@ -407,13 +429,7 @@
     o_back, lse_back, up_x, down_x = lax.optimization_barrier((o_back, lse_back, up_x, down_x))
     ups = (up, swap(up, "core"), up_x, swap(up_x, "core"))
     downs = (down, swap(down, "core"), down_x, swap(down_x, "core"))
-    wq4 = jnp.concatenate(
-        [
-            jnp.concatenate([a[skip:] for a in ups], axis=1),
-            jnp.concatenate(downs, axis=1),
-        ],
-        axis=0,
-    ).reshape(8, -1, 4 * HD)
+    wq4 = side_by_side(skip, ups, downs).reshape(8, -1, 4 * HD)
 
     lse_back = jnp.where(late, lse_back.reshape(rows, 1), LOW)
     self_out = merge(o, lse.reshape(rows, 1), o_back, lse_back)

time: 139 us -> 136 us (0.978)
  other arithmetic: 14.4 us -> 5.99 us
  blocking collectives: 0 us -> 7.5 us
  starting transfers between devices: 49 us -> 43 us
  waiting for transfers between devices: 19.7 us -> 21.8 us
  local copies, waits for them, and re-layouts: 10.2 us -> 11.6 us
    concatenate x1 -> x0, other arithmetic: 7.75 us -> none  [local(): jnp.concatenate([jnp.concatenate([a[skip:] for a in ups], axis=1), jnp.co...]
    all_to_all x0 -> x1, blocking collectives: none -> 7.5 us  [local(): mine = lax.all_to_all(self_out.reshape(4, quarter, HD), XC, 0, 0)]
    all_to_all x1 -> x0, starting transfers between devices: 5.25 us -> none  [local(): mine = lax.all_to_all(self_out.reshape(4, quarter, HD), XC, 0, 0)]
    unnamed x13 -> x21, local copies, waits for them, and re-layouts: 0.81 us -> 5.77 us
    ppermute x14, waiting for transfers between devices: 5.78 us -> 8.72 us  [ring(): return lax.ppermute(value, axis, [(i, (i + step) % n) for i in range(n)])]
    all_to_all x1 -> x0, waiting for transfers between devices: 2.77 us -> none  [local(): mine = lax.all_to_all(self_out.reshape(4, quarter, HD), XC, 0, 0)]
    pallas_call x0 -> x1, Pallas kernels: none -> 2.11 us  [side_by_side(): pl.pallas_call(functools.partial(side_kernel, skip), in_specs=[pl.BlockSp...]
    ppermute x1, waiting for transfers between devices: 4.84 us -> 6.92 us  [local(): lse_back = lax.ppermute(lse_sent, 'x_hi', [(0, 1)])]
  transfers between devices with their start and end apart: 29 -> 28, of which waited for: 10 -> 11; matrix products, arithmetic and copies ran while one was open for 17% -> 8% of each run, Pallas kernels for 17% -> 18%
where the time goes in v6:
time: 136 us; the launch traced here: 135 us
  starting transfers between devices  43 us (32%)
  Pallas kernels  24.6 us (18%)
  waiting for transfers between devices  21.8 us (16%)
  between operations  15.9 us (12%)
  local copies, waits for them, and re-layouts  11.6 us (9%)
  blocking collectives  7.5 us (6%)
  other arithmetic  5.99 us (4%)
  matrix products  4.51 us (3%)
    ppermute x14, starting transfers between devices, ring(): return lax.ppermute(value, axis, [(i, (i + step) % n) for i in range(n)])  19.6 us
    ppermute x10, starting transfers between devices, swap(): return lax.ppermute(value, axis, [(0, 1), (1, 0)])  17.1 us
    ppermute x14, waiting for transfers between devices, ring(): return lax.ppermute(value, axis, [(i, (i + step) % n) for i in range(n)])  8.72 us
    pallas_call x1, Pallas kernels, project(): pl.pallas_call(project_kernel, grid_spec=pltpu.PrefetchScalarGridSpec(num...  8.26 us
    all_to_all x1, blocking collectives, local(): mine = lax.all_to_all(self_out.reshape(4, quarter, HD), XC, 0, 0)  7.5 us
    ppermute x1, waiting for transfers between devices, local(): lse_back = lax.ppermute(lse_sent, 'x_hi', [(0, 1)])  6.92 us
    ppermute x10, waiting for transfers between devices, swap(): return lax.ppermute(value, axis, [(0, 1), (1, 0)])  6.14 us
    unnamed x21, local copies, waits for them, and re-layouts  5.77 us
  transfers between devices with their start and end apart: 28, of which 11 were waited for; matrix products, arithmetic and copies ran while one was open for 8% of the time, Pallas kernels for 18%

profile of v6, /device:TPU:31, one launch (start us, length us, event | category | flops | bytes accessed | tf_op | source)
XLA Modules:
  0.0 134.9 jit_solution(25404662178115524)
XLA Ops:
  7.2 1.1 pad_maximum_fusion.1.kv_ref.kv0
  8.4 1.3 select_reduce_fusion.1
  11.0 1.1 constant_dynamic-slice_fusion.2
  12.1 0.9 pad_maximum_fusion.2
  13.1 1.5 %collective-permute-start.2 = (bf16[2,1024,128]{2,1,0:T(8,128)(2,1)S(1)}, bf16[2,1024,128]{2,1,0:T(8,128)(2,1)}, u32[]{:S(2)}, u32[]{:S(2)}) collective-permute-start(bf16[2,1024,128]{2,1,0:T(8,128)(2,1)S(1)} %pad_maximum_fusion.1.kv_ref.kv0), channel_id=1, source_target_pairs={{0,96},{32,0},{64,32},{96,64},{1,97},{33,1},{65,33},{97,65},{2,98}... | collective-permute-start | bytes 1572872 | tf_op jit(solution)/shard_map/ppermute | solution.py:26
  14.5 3.7 %collective-permute-start = (bf16[1024,128]{1,0:T(8,128)(2,1)}, bf16[1024,128]{1,0:T(8,128)(2,1)}, u32[]{:S(2)}, u32[]{:S(2)}) collective-permute-start(bf16[1024,128]{1,0:T(8,128)(2,1)} %q_ref.5), channel_id=1, source_target_pairs={{128,0},{129,1},{130,2},{131,3},{132,4},{133,5},{134,6},{135,7},{1... | collective-permute-start | bytes 786440 | tf_op jit(solution)/shard_map/ppermute | solution.py:413
  18.3 1.1 pad_maximum_fusion.u0.w0
  19.5 1.2 slice.179.d0
  20.6 2.7 %collective-permute-start.8 = (bf16[2944,128]{1,0:T(8,128)(2,1)S(1)}, bf16[2944,128]{1,0:T(8,128)(2,1)}, u32[]{:S(2)}, u32[]{:S(2)}) collective-permute-start(bf16[2944,128]{1,0:T(8,128)(2,1)S(1)} %slice.179.d0), channel_id=1, source_target_pairs={{0,2},{2,128},{128,130},{130,0},{1,3},{3,129},{129,131},{131,1},{4... | collective-permute-start | bytes 2261000 | tf_op jit(solution)/shard_map/ppermute | solution.py:26
  23.5 0.9 copy-done.5
  24.5 1.2 attend_own.1
  26.0 1.3 collective-permute-start.3
  27.3 1.0 slice_bitcast_fusion
  28.6 5.7 %attend_middle.1 = (f32[2,1024,128]{2,1,0:T(8,128)S(1)}, f32[2,1024,256]{2,1,0:T(8,128)S(1)}) custom-call(s32[8]{0:T(128)S(1)} %convert_element_type.33.flags, bf16[1024,128]{1,0:T(8,128)(2,1)S(1)} %copy-done.6, bf16[1024,128]{1,0:T(8,128)(2,1)} %collective-permute-done.qs_ref, f32[1024,128]{1,0:T(8,128)S(1)} %get-tuple-element.34.m_in, ...), custom_call_target="tpu_custom_call" | custom-call | flops 8589934592 | bytes 6291456 | tf_op jit(solution)/shard_map/attend_middle/pallas_call | solution.py:135
  34.3 1.0 collective-permute-done.4.v3
  35.4 3.9 %attend_last.1 = (f32[1024,128]{1,0:T(8,128)S(1)}, bf16[1024,128]{1,0:T(8,128)(2,1)S(1)}, f32[2,4,1,256]{3,2,1,0:T(1,128)S(1)}) custom-call(s32[8]{0:T(128)S(1)} %convert_element_type.33.flags, bf16[1024,128]{1,0:T(8,128)(2,1)S(1)} %copy-done.6, bf16[1024,128]{1,0:T(8,128)(2,1)} %collective-permute-done.qs_ref, f32[2,1024,128]{2,1,0:T(8,128)S(1)} %get-tuple-element.36.m_in, ...), custom_call_target="tpu_custom_call" | custom-call | flops 3221225472 | bytes 6291456 | tf_op jit(solution)/shard_map/attend_last/pallas_call | solution.py:206
  39.3 1.3 collective-permute-start.5
  40.6 1.3 collective-permute-start.6
  41.9 3.0 %collective-permute-start.11 = (bf16[2944,128]{1,0:T(8,128)(2,1)S(1)}, bf16[2944,128]{1,0:T(8,128)(2,1)S(1)}, u32[]{:S(2)}, u32[]{:S(2)}) collective-permute-start(bf16[2944,128]{1,0:T(8,128)(2,1)S(1)} %pad_maximum_fusion.u0.w0), channel_id=1, source_target_pairs={{0,1},{1,0},{2,3},{3,2},{4,5},{5,4},{6,7},{7,6},{8,9},{9,8},{10,11... | collective-permute-start | bytes 2261000 | tf_op jit(solution)/shard_map/ppermute | solution.py:30
  45.0 6.9 %collective-permute-done.6 = f32[4,1,256]{2,1,0:T(1,128)S(1)} collective-permute-done((f32[4,1,256]{2,1,0:T(1,128)S(1)}, f32[4,1,256]{2,1,0:T(1,128)S(1)}, u32[]{:S(2)}, u32[]{:S(2)}) %collective-permute-start.6) | collective-permute-done | bytes 4128 | tf_op jit(solution)/shard_map/ppermute | solution.py:428
  51.9 2.6 %collective-permute-start.12 = (bf16[2944,128]{1,0:T(8,128)(2,1)S(1)}, bf16[2944,128]{1,0:T(8,128)(2,1)S(1)}, u32[]{:S(2)}, u32[]{:S(2)}) collective-permute-start(bf16[2944,128]{1,0:T(8,128)(2,1)S(1)} %collective-permute-done.7.u2.w2), channel_id=1, source_target_pairs={{0,1},{1,0},{2,3},{3,2},{4,5},{5,4},{6,7},{7,6},{8,9},{9,8},{10,11... | collective-permute-start | bytes 2261000 | tf_op jit(solution)/shard_map/ppermute | solution.py:30
  55.0 7.5 %all_to_all.5 = bf16[4,256,128]{2,1,0:T(8,128)(2,1)S(1)} all-to-all(bf16[4,256,128]{2,1,0:T(8,128)(2,1)S(1)} %bitcast.172), channel_id=1, replica_groups=mesh['x_hi'=2,'y'=4,'z'=8,'x_lo'=2,'core'=2] {'x_lo','core'}, dimensions={0} | all-to-all | bytes 524288 | tf_op jit(solution)/shard_map/all_to_all | solution.py:452
  62.5 5.5 %collective-permute-start.10 = (bf16[4,256,128]{2,1,0:T(8,128)(2,1)S(1)}, bf16[4,256,128]{2,1,0:T(8,128)(2,1)S(1)}, u32[]{:S(2)}, u32[]{:S(2)}) collective-permute-start(bf16[4,256,128]{2,1,0:T(8,128)(2,1)S(1)} %all_to_all.5), channel_id=1, source_target_pairs={{0,28},{4,0},{8,4},{12,8},{16,12},{20,16},{24,20},{28,24},{1,29},{... | collective-permute-start | bytes 786440 | tf_op jit(solution)/shard_map/ppermute | solution.py:26
  68.0 2.1 %side_by_side.1 = bf16[4096,512]{1,0:T(8,128)(2,1)S(1)} custom-call(bf16[2944,128]{1,0:T(8,128)(2,1)S(1)} %pad_maximum_fusion.u0.w0, bf16[2944,128]{1,0:T(8,128)(2,1)S(1)} %collective-permute-done.11.u1.w1, bf16[2944,128]{1,0:T(8,128)(2,1)S(1)} %collective-permute-done.7.u2.w2, bf16[2944,128]{1,0:T(8,128)(2,1)S(1)} %collective-permute-done.12.u3.w3, ...), custom_call_target="tpu_custom_call" | custom-call | flops 1048576 | bytes 10485760 | tf_op jit(solution)/shard_map/side_by_side/pallas_call | solution.py:248
  70.2 2.0 %copy-done = bf16[4096,512]{1,0:T(8,128)(2,1)} copy-done((bf16[4096,512]{1,0:T(8,128)(2,1)}, bf16[4096,512]{1,0:T(8,128)(2,1)S(1)}, u32[]{:S(2)}) %copy-start) | copy-done | bytes 4194328
  72.2 0.9 collective-permute-done.10
  73.8 2.5 %collective-permute-done.9 = bf16[4,256,128]{2,1,0:T(8,128)(2,1)} collective-permute-done((bf16[4,256,128]{2,1,0:T(8,128)(2,1)S(1)}, bf16[4,256,128]{2,1,0:T(8,128)(2,1)}, u32[]{:S(2)}, u32[]{:S(2)}) %collective-permute-start.9) | collective-permute-done | bytes 262176 | tf_op jit(solution)/shard_map/ppermute | solution.py:26
  76.3 1.8 %collective-permute-start.19 = (bf16[16,128,896]{2,1,0:T(8,128)(2,1)}, bf16[16,128,896]{2,1,0:T(8,128)(2,1)}, u32[]{:S(2)}, u32[]{:S(2)}) collective-permute-start(bf16[16,128,896]{2,1,0:T(8,128)(2,1)} %all-gather.2.cloned.1.call-done.a_ref), channel_id=1, source_target_pairs={{0,1},{1,0},{2,3},{3,2},{4,5},{5,4},{6,7},{7,6},{8,9},{9,8},{10,11... | collective-permute-start | bytes 11010056 | tf_op jit(solution)/shard_map/ppermute | solution.py:30
  78.8 2.7 %collective-permute-start.17 = (bf16[4,256,128]{2,1,0:T(8,128)(2,1)}, bf16[4,256,128]{2,1,0:T(8,128)(2,1)S(1)}, u32[]{:S(2)}, u32[]{:S(2)}) collective-permute-start(bf16[4,256,128]{2,1,0:T(8,128)(2,1)} %copy-done.8), channel_id=1, source_target_pairs={{0,28},{4,0},{8,4},{12,8},{16,12},{20,16},{24,20},{28,24},{1,29},{... | collective-permute-start | bytes 786440 | tf_op jit(solution)/shard_map/ppermute | solution.py:26
  81.5 1.1 slice_bitcast_fusion.21
  82.6 1.3 fusion.8
  83.9 1.3 convolution_add_fusion.5
  85.3 2.9 %collective-permute-done.15 = bf16[4,256,128]{2,1,0:T(8,128)(2,1)S(1)} collective-permute-done((bf16[4,256,128]{2,1,0:T(8,128)(2,1)}, bf16[4,256,128]{2,1,0:T(8,128)(2,1)S(1)}, u32[]{:S(2)}, u32[]{:S(2)}) %collective-permute-start.15) | collective-permute-done | bytes 262176 | tf_op jit(solution)/shard_map/ppermute | solution.py:26
  88.2 2.7 %collective-permute-start.18 = (bf16[4,256,128]{2,1,0:T(8,128)(2,1)S(1)}, bf16[4,256,128]{2,1,0:T(8,128)(2,1)S(1)}, u32[]{:S(2)}, u32[]{:S(2)}) collective-permute-start(bf16[4,256,128]{2,1,0:T(8,128)(2,1)S(1)} %collective-permute-done.17), channel_id=1, source_target_pairs={{0,28},{4,0},{8,4},{12,8},{16,12},{20,16},{24,20},{28,24},{1,29},{... | collective-permute-start | bytes 786440 | tf_op jit(solution)/shard_map/ppermute | solution.py:26
  91.3 2.0 %copy-done.4 = bf16[16,128,896]{2,1,0:T(8,128)(2,1)S(1)} copy-done((bf16[16,128,896]{2,1,0:T(8,128)(2,1)S(1)}, bf16[16,128,896]{2,1,0:T(8,128)(2,1)}, u32[]{:S(2)}) %copy-start.4) | copy-done | bytes 3670040
  93.3 8.3 %project.1 = (bf16[8,512,256]{2,1,0:T(8,128)(2,1)S(1)}, bf16[8,256,512]{2,1,0:T(8,128)(2,1)S(1)}) custom-call(s32[16]{0:T(128)S(1)} %add_bitcast_fusion.info, bf16[16,128,896]{2,1,0:T(8,128)(2,1)S(1)} %copy-done.4, bf16[16,128,896]{2,1,0:T(8,128)(2,1)} %collective-permute-done.19.b_ref, bf16[2944,128]{1,0:T(8,128)(2,1)S(1)} %pad_maximum_fusion.u0.w0, ...), custom_call_target="tpu_custom_call" | custom-call | flops 4294967296 | bytes 12582912 | tf_op jit(solution)/shard_map/project/pallas_call | solution.py:298
  101.8 2.7 %collective-permute-start.21 = (bf16[2,256,128]{2,1,0:T(8,128)(2,1)S(1)}, bf16[2,256,128]{2,1,0:T(8,128)(2,1)S(1)}, u32[]{:S(2)}, u32[]{:S(2)}) collective-permute-start(bf16[2,256,128]{2,1,0:T(8,128)(2,1)S(1)} %slice.182), channel_id=1, source_target_pairs={{0,28},{4,0},{8,4},{12,8},{16,12},{20,16},{24,20},{28,24},{1,29},{... | collective-permute-start | bytes 393224 | tf_op jit(solution)/shard_map/ppermute | solution.py:26
  105.7 1.1 collective-permute-done.20
  107.2 1.2 collective-permute-start.22
  108.4 1.7 %cross.2 = (bf16[4,256,128]{2,1,0:T(8,128)(2,1)S(1)}, f32[4,8,64]{2,1,0:T(8,128)S(1)}) custom-call(s32[8]{0:T(128)S(1)} %bitcast.171, bf16[256,512]{1,0:T(8,128)(2,1)S(1)} %add_convert_fusion.q_ref, bf16[8,512,256]{2,1,0:T(8,128)(2,1)S(1)} %get-tuple-element.58.k_ref, bf16[8,256,512]{2,1,0:T(8,128)(2,1)S(1)} %get-tuple-element.59.v_ref), custom_call_target="tpu_custom_call" | custom-call | flops 2147483648 | bytes 3145728 | tf_op jit(solution)/shard_map/cross/pallas_call | solution.py:354
  110.8 2.0 %collective-permute-done.22 = bf16[256,512]{1,0:T(8,128)(2,1)S(1)} collective-permute-done((bf16[256,512]{1,0:T(8,128)(2,1)S(1)}, bf16[256,512]{1,0:T(8,128)(2,1)S(1)}, u32[]{:S(2)}, u32[]{:S(2)}) %collective-permute-start.22) | collective-permute-done | bytes 262176 | tf_op jit(solution)/shard_map/ppermute | solution.py:30
  112.8 1.7 %cross.3 = (bf16[4,256,128]{2,1,0:T(8,128)(2,1)S(1)}, f32[4,8,64]{2,1,0:T(8,128)S(1)}) custom-call(s32[8]{0:T(128)S(1)} %bitcast.170, bf16[256,512]{1,0:T(8,128)(2,1)S(1)} %pad_maximum_fusion.3.q_ref, bf16[8,512,256]{2,1,0:T(8,128)(2,1)S(1)} %get-tuple-element.58.k_ref, bf16[8,256,512]{2,1,0:T(8,128)(2,1)S(1)} %get-tuple-element.59.v_ref), custom_call_target="tpu_custom_call" | custom-call | flops 2147483648 | bytes 3145728 | tf_op jit(solution)/shard_map/cross/pallas_call | solution.py:354
  114.6 0.9 collective-permute-start.23
  116.3 1.2 collective-permute-done.23
  117.8 2.0 %collective-permute-done.24 = bf16[2,256,128]{2,1,0:T(8,128)(2,1)S(1)} collective-permute-done((bf16[2,256,128]{2,1,0:T(8,128)(2,1)S(1)}, bf16[2,256,128]{2,1,0:T(8,128)(2,1)S(1)}, u32[]{:S(2)}, u32[]{:S(2)}) %collective-permute-start.24) | collective-permute-done | bytes 131104 | tf_op jit(solution)/shard_map/ppermute | solution.py:30
  120.1 6.2 %collective-permute-start.26 = (bf16[2,256,128]{2,1,0:T(8,128)(2,1)S(1)}, bf16[2,256,128]{2,1,0:T(8,128)(2,1)S(1)}, u32[]{:S(2)}, u32[]{:S(2)}) collective-permute-start(bf16[2,256,128]{2,1,0:T(8,128)(2,1)S(1)} %get-tuple-element.78), channel_id=1, source_target_pairs={{0,1},{1,0},{2,3},{3,2},{4,5},{5,4},{6,7},{7,6},{8,9},{9,8},{10,11... | collective-permute-start | bytes 393224 | tf_op jit(solution)/shard_map/ppermute | solution.py:30
  126.3 1.0 collective-permute-done.26
  127.4 0.7 copy.37
  (101 shorter events, 7.4 us)
Async XLA Ops:
  7.2 11.1 %slice-start = ((bf16[4096,128]{1,0:T(8,128)(2,1)}), bf16[1152,128]{1,0:T(8,128)(2,1)S(1)}, s32[]{:S(2)}) async-start(bf16[4096,128]{1,0:T(8,128)(2,1)} %param.17), calls=%async_computation.2 | async-start | bytes 589824 | tf_op jit(solution)/shard_map/slice | solution.py:421
  7.2 69.1 %all-gather.2.cloned.1.call-start = ((), (), s32[]{:S(2)}) async-start(), calls=%async_computation.1 | async-start | bytes 4128768 | tf_op jit(solution)/shard_map/all_gather | solution.py:409
  13.0 13.0 %collective-permute-start.1 = (bf16[2,1024,128]{2,1,0:T(8,128)(2,1)S(1)}, bf16[2,1024,128]{2,1,0:T(8,128)(2,1)S(1)}, u32[]{:S(2)}, u32[]{:S(2)}) collective-permute-start(bf16[2,1024,128]{2,1,0:T(8,128)(2,1)S(1)} %pad_maximum_fusion.1.kv_ref.kv0), channel_id=1, source_target_pairs={{0,32},{32,64},{64,96},{96,0},{1,33},{33,65},{65,97},{97,1},{2,34}... | collective-permute-start | bytes 1572872 | tf_op jit(solution)/shard_map/ppermute | solution.py:26
  13.1 14.2 %collective-permute-start.2 = (bf16[2,1024,128]{2,1,0:T(8,128)(2,1)S(1)}, bf16[2,1024,128]{2,1,0:T(8,128)(2,1)}, u32[]{:S(2)}, u32[]{:S(2)}) collective-permute-start(bf16[2,1024,128]{2,1,0:T(8,128)(2,1)S(1)} %pad_maximum_fusion.1.kv_ref.kv0), channel_id=1, source_target_pairs={{0,96},{32,0},{64,32},{96,64},{1,97},{33,1},{65,33},{97,65},{2,98}... | collective-permute-start | bytes 1572872 | tf_op jit(solution)/shard_map/ppermute | solution.py:26
  14.5 14.1 %collective-permute-start = (bf16[1024,128]{1,0:T(8,128)(2,1)}, bf16[1024,128]{1,0:T(8,128)(2,1)}, u32[]{:S(2)}, u32[]{:S(2)}) collective-permute-start(bf16[1024,128]{1,0:T(8,128)(2,1)} %q_ref.5), channel_id=1, source_target_pairs={{128,0},{129,1},{130,2},{131,3},{132,4},{133,5},{134,6},{135,7},{1... | collective-permute-start | bytes 786440 | tf_op jit(solution)/shard_map/ppermute | solution.py:413
  19.4 25.5 %collective-permute-start.7 = (bf16[2944,128]{1,0:T(8,128)(2,1)S(1)}, bf16[2944,128]{1,0:T(8,128)(2,1)S(1)}, u32[]{:S(2)}, u32[]{:S(2)}) collective-permute-start(bf16[2944,128]{1,0:T(8,128)(2,1)S(1)} %pad_maximum_fusion.u0.w0), channel_id=1, source_target_pairs={{0,130},{2,0},{128,2},{130,128},{1,131},{3,1},{129,3},{131,129},{4... | collective-permute-start | bytes 2261000 | tf_op jit(solution)/shard_map/ppermute | solution.py:26
  20.6 24.3 %collective-permute-start.8 = (bf16[2944,128]{1,0:T(8,128)(2,1)S(1)}, bf16[2944,128]{1,0:T(8,128)(2,1)}, u32[]{:S(2)}, u32[]{:S(2)}) collective-permute-start(bf16[2944,128]{1,0:T(8,128)(2,1)S(1)} %slice.179.d0), channel_id=1, source_target_pairs={{0,2},{2,128},{128,130},{130,0},{1,3},{3,129},{129,131},{131,1},{4... | collective-permute-start | bytes 2261000 | tf_op jit(solution)/shard_map/ppermute | solution.py:26
  23.5 1.0 copy-start.5
  24.4 4.2 %copy-start.6 = (bf16[1024,128]{1,0:T(8,128)(2,1)S(1)}, bf16[1024,128]{1,0:T(8,128)(2,1)}, u32[]{:S(2)}) copy-start(bf16[1024,128]{1,0:T(8,128)(2,1)} %q_ref.5) | copy-start | bytes 786436
  26.0 8.3 %collective-permute-start.3 = (bf16[1024,128]{1,0:T(8,128)(2,1)S(1)}, bf16[1024,128]{1,0:T(8,128)(2,1)S(1)}, u32[]{:S(2)}, u32[]{:S(2)}) collective-permute-start(bf16[1024,128]{1,0:T(8,128)(2,1)S(1)} %slice_bitcast_fusion.1), channel_id=1, source_target_pairs={{0,32},{32,64},{64,96},{96,0},{1,33},{33,65},{65,97},{97,1},{2,34}... | collective-permute-start | bytes 786440 | tf_op jit(solution)/shard_map/ppermute | solution.py:26
  28.2 7.1 %collective-permute-start.4 = (bf16[1024,128]{1,0:T(8,128)(2,1)S(1)}, bf16[1024,128]{1,0:T(8,128)(2,1)S(1)}, u32[]{:S(2)}, u32[]{:S(2)}) collective-permute-start(bf16[1024,128]{1,0:T(8,128)(2,1)S(1)} %slice_bitcast_fusion), channel_id=1, source_target_pairs={{0,96},{32,0},{64,32},{96,64},{1,97},{33,1},{65,33},{97,65},{2,98}... | collective-permute-start | bytes 786440 | tf_op jit(solution)/shard_map/ppermute | solution.py:26
  39.3 12.6 %collective-permute-start.5 = (bf16[1024,128]{1,0:T(8,128)(2,1)S(1)}, bf16[1024,128]{1,0:T(8,128)(2,1)S(1)}, u32[]{:S(2)}, u32[]{:S(2)}) collective-permute-start(bf16[1024,128]{1,0:T(8,128)(2,1)S(1)} %get-tuple-element.40), channel_id=1, source_target_pairs={{0,128},{1,129},{2,130},{3,131},{4,132},{5,133},{6,134},{7,135},{8... | collective-permute-start | bytes 786440 | tf_op jit(solution)/shard_map/ppermute | solution.py:427
  40.6 11.3 %collective-permute-start.6 = (f32[4,1,256]{2,1,0:T(1,128)S(1)}, f32[4,1,256]{2,1,0:T(1,128)S(1)}, u32[]{:S(2)}, u32[]{:S(2)}) collective-permute-start(f32[4,1,256]{2,1,0:T(1,128)S(1)} %get-tuple-element.116), channel_id=1, source_target_pairs={{0,128},{1,129},{2,130},{3,131},{4,132},{5,133},{6,134},{7,135},{8... | collective-permute-start | bytes 12296 | tf_op jit(solution)/shard_map/ppermute | solution.py:428
  41.9 26.1 %collective-permute-start.11 = (bf16[2944,128]{1,0:T(8,128)(2,1)S(1)}, bf16[2944,128]{1,0:T(8,128)(2,1)S(1)}, u32[]{:S(2)}, u32[]{:S(2)}) collective-permute-start(bf16[2944,128]{1,0:T(8,128)(2,1)S(1)} %pad_maximum_fusion.u0.w0), channel_id=1, source_target_pairs={{0,1},{1,0},{2,3},{3,2},{4,5},{5,4},{6,7},{7,6},{8,9},{9,8},{10,11... | collective-permute-start | bytes 2261000 | tf_op jit(solution)/shard_map/ppermute | solution.py:30
  44.9 23.1 %collective-permute-start.13 = (bf16[2944,128]{1,0:T(8,128)(2,1)S(1)}, bf16[2944,128]{1,0:T(8,128)(2,1)S(1)}, u32[]{:S(2)}, u32[]{:S(2)}) collective-permute-start(bf16[2944,128]{1,0:T(8,128)(2,1)S(1)} %slice.179.d0), channel_id=1, source_target_pairs={{0,1},{1,0},{2,3},{3,2},{4,5},{5,4},{6,7},{7,6},{8,9},{9,8},{10,11... | collective-permute-start | bytes 2261000 | tf_op jit(solution)/shard_map/ppermute | solution.py:30
  51.9 16.1 %collective-permute-start.12 = (bf16[2944,128]{1,0:T(8,128)(2,1)S(1)}, bf16[2944,128]{1,0:T(8,128)(2,1)S(1)}, u32[]{:S(2)}, u32[]{:S(2)}) collective-permute-start(bf16[2944,128]{1,0:T(8,128)(2,1)S(1)} %collective-permute-done.7.u2.w2), channel_id=1, source_target_pairs={{0,1},{1,0},{2,3},{3,2},{4,5},{5,4},{6,7},{7,6},{8,9},{9,8},{10,11... | collective-permute-start | bytes 2261000 | tf_op jit(solution)/shard_map/ppermute | solution.py:30
  54.5 13.5 %collective-permute-start.14 = (bf16[2944,128]{1,0:T(8,128)(2,1)}, bf16[2944,128]{1,0:T(8,128)(2,1)S(1)}, u32[]{:S(2)}, u32[]{:S(2)}) collective-permute-start(bf16[2944,128]{1,0:T(8,128)(2,1)} %collective-permute-done.8.d2), channel_id=1, source_target_pairs={{0,1},{1,0},{2,3},{3,2},{4,5},{5,4},{6,7},{7,6},{8,9},{9,8},{10,11... | collective-permute-start | bytes 2261000 | tf_op jit(solution)/shard_map/ppermute | solution.py:30
  55.0 15.1 %copy-start.7 = (bf16[1024,128]{1,0:T(8,128)(2,1)}, bf16[1024,128]{1,0:T(8,128)(2,1)S(1)}, u32[]{:S(2)}) copy-start(bf16[1024,128]{1,0:T(8,128)(2,1)S(1)} %divide_convert_fusion) | copy-start | bytes 786436
  62.5 15.5 %copy-start.9 = (s32[16,2]{0,1:T(2,128)S(1)}, s32[16,2]{0,1:T(2,128)}, u32[]{:S(2)}) copy-start(s32[16,2]{0,1:T(2,128)} %param.13) | copy-start | bytes 388
  62.5 10.5 %collective-permute-start.10 = (bf16[4,256,128]{2,1,0:T(8,128)(2,1)S(1)}, bf16[4,256,128]{2,1,0:T(8,128)(2,1)S(1)}, u32[]{:S(2)}, u32[]{:S(2)}) collective-permute-start(bf16[4,256,128]{2,1,0:T(8,128)(2,1)S(1)} %all_to_all.5), channel_id=1, source_target_pairs={{0,28},{4,0},{8,4},{12,8},{16,12},{20,16},{24,20},{28,24},{1,29},{... | collective-permute-start | bytes 786440 | tf_op jit(solution)/shard_map/ppermute | solution.py:26
  68.0 8.3 %collective-permute-start.9 = (bf16[4,256,128]{2,1,0:T(8,128)(2,1)S(1)}, bf16[4,256,128]{2,1,0:T(8,128)(2,1)}, u32[]{:S(2)}, u32[]{:S(2)}) collective-permute-start(bf16[4,256,128]{2,1,0:T(8,128)(2,1)S(1)} %all_to_all.5), channel_id=1, source_target_pairs={{0,4},{4,8},{8,12},{12,16},{16,20},{20,24},{24,28},{28,0},{1,5},{5... | collective-permute-start | bytes 786440 | tf_op jit(solution)/shard_map/ppermute | solution.py:26
  68.0 2.1 %copy-start.2 = (bf16[2944,128]{1,0:T(8,128)(2,1)}, bf16[2944,128]{1,0:T(8,128)(2,1)S(1)}, u32[]{:S(2)}) copy-start(bf16[2944,128]{1,0:T(8,128)(2,1)S(1)} %collective-permute-done.12.u3.w3) | copy-start | bytes 2260996
  70.2 2.0 %copy-start = (bf16[4096,512]{1,0:T(8,128)(2,1)}, bf16[4096,512]{1,0:T(8,128)(2,1)S(1)}, u32[]{:S(2)}) copy-start(bf16[4096,512]{1,0:T(8,128)(2,1)S(1)} %side_by_side.1) | copy-start | bytes 12582916
  73.1 0.7 copy-start.8
  73.8 17.5 %copy-start.3 = (bf16[2944,128]{1,0:T(8,128)(2,1)S(1)}, bf16[2944,128]{1,0:T(8,128)(2,1)}, u32[]{:S(2)}) copy-start(bf16[2944,128]{1,0:T(8,128)(2,1)} %copy-done.2) | copy-start | bytes 2260996
  76.3 15.0 %collective-permute-start.19 = (bf16[16,128,896]{2,1,0:T(8,128)(2,1)}, bf16[16,128,896]{2,1,0:T(8,128)(2,1)}, u32[]{:S(2)}, u32[]{:S(2)}) collective-permute-start(bf16[16,128,896]{2,1,0:T(8,128)(2,1)} %all-gather.2.cloned.1.call-done.a_ref), channel_id=1, source_target_pairs={{0,1},{1,0},{2,3},{3,2},{4,5},{5,4},{6,7},{7,6},{8,9},{9,8},{10,11... | collective-permute-start | bytes 11010056 | tf_op jit(solution)/shard_map/ppermute | solution.py:30
  78.6 12.3 %copy-start.1 = (bf16[4096,512]{1,0:T(8,128)(2,1)S(1)}, bf16[4096,512]{1,0:T(8,128)(2,1)}, u32[]{:S(2)}) copy-start(bf16[4096,512]{1,0:T(8,128)(2,1)} %copy-done) | copy-start | bytes 12582916
  78.7 9.4 %collective-permute-start.15 = (bf16[4,256,128]{2,1,0:T(8,128)(2,1)}, bf16[4,256,128]{2,1,0:T(8,128)(2,1)S(1)}, u32[]{:S(2)}, u32[]{:S(2)}) collective-permute-start(bf16[4,256,128]{2,1,0:T(8,128)(2,1)} %collective-permute-done.9), channel_id=1, source_target_pairs={{0,4},{4,8},{8,12},{12,16},{16,20},{20,24},{24,28},{28,0},{1,5},{5... | collective-permute-start | bytes 786440 | tf_op jit(solution)/shard_map/ppermute | solution.py:26
  78.8 9.4 %collective-permute-start.17 = (bf16[4,256,128]{2,1,0:T(8,128)(2,1)}, bf16[4,256,128]{2,1,0:T(8,128)(2,1)S(1)}, u32[]{:S(2)}, u32[]{:S(2)}) collective-permute-start(bf16[4,256,128]{2,1,0:T(8,128)(2,1)} %copy-done.8), channel_id=1, source_target_pairs={{0,28},{4,0},{8,4},{12,8},{16,12},{20,16},{24,20},{28,24},{1,29},{... | collective-permute-start | bytes 786440 | tf_op jit(solution)/shard_map/ppermute | solution.py:26
  88.2 13.4 %collective-permute-start.16 = (bf16[4,256,128]{2,1,0:T(8,128)(2,1)S(1)}, bf16[4,256,128]{2,1,0:T(8,128)(2,1)S(1)}, u32[]{:S(2)}, u32[]{:S(2)}) collective-permute-start(bf16[4,256,128]{2,1,0:T(8,128)(2,1)S(1)} %collective-permute-done.15), channel_id=1, source_target_pairs={{0,4},{4,8},{8,12},{12,16},{16,20},{20,24},{24,28},{28,0},{1,5},{5... | collective-permute-start | bytes 786440 | tf_op jit(solution)/shard_map/ppermute | solution.py:26
  88.2 13.4 %collective-permute-start.18 = (bf16[4,256,128]{2,1,0:T(8,128)(2,1)S(1)}, bf16[4,256,128]{2,1,0:T(8,128)(2,1)S(1)}, u32[]{:S(2)}, u32[]{:S(2)}) collective-permute-start(bf16[4,256,128]{2,1,0:T(8,128)(2,1)S(1)} %collective-permute-done.17), channel_id=1, source_target_pairs={{0,28},{4,0},{8,4},{12,8},{16,12},{20,16},{24,20},{28,24},{1,29},{... | collective-permute-start | bytes 786440 | tf_op jit(solution)/shard_map/ppermute | solution.py:26
  91.3 2.0 %copy-start.4 = (bf16[16,128,896]{2,1,0:T(8,128)(2,1)S(1)}, bf16[16,128,896]{2,1,0:T(8,128)(2,1)}, u32[]{:S(2)}) copy-start(bf16[16,128,896]{2,1,0:T(8,128)(2,1)} %all-gather.2.cloned.1.call-done.a_ref) | copy-start | bytes 11010052
  101.7 5.1 %collective-permute-start.20 = (bf16[2,256,128]{2,1,0:T(8,128)(2,1)S(1)}, bf16[2,256,128]{2,1,0:T(8,128)(2,1)S(1)}, u32[]{:S(2)}, u32[]{:S(2)}) collective-permute-start(bf16[2,256,128]{2,1,0:T(8,128)(2,1)S(1)} %slice.181), channel_id=1, source_target_pairs={{0,4},{4,8},{8,12},{12,16},{16,20},{20,24},{24,28},{28,0},{1,5},{5... | collective-permute-start | bytes 393224 | tf_op jit(solution)/shard_map/ppermute | solution.py:26
  101.8 5.0 %collective-permute-start.21 = (bf16[2,256,128]{2,1,0:T(8,128)(2,1)S(1)}, bf16[2,256,128]{2,1,0:T(8,128)(2,1)S(1)}, u32[]{:S(2)}, u32[]{:S(2)}) collective-permute-start(bf16[2,256,128]{2,1,0:T(8,128)(2,1)S(1)} %slice.182), channel_id=1, source_target_pairs={{0,28},{4,0},{8,4},{12,8},{16,12},{20,16},{24,20},{28,24},{1,29},{... | collective-permute-start | bytes 393224 | tf_op jit(solution)/shard_map/ppermute | solution.py:26
  107.2 5.5 %collective-permute-start.22 = (bf16[256,512]{1,0:T(8,128)(2,1)S(1)}, bf16[256,512]{1,0:T(8,128)(2,1)S(1)}, u32[]{:S(2)}, u32[]{:S(2)}) collective-permute-start(bf16[256,512]{1,0:T(8,128)(2,1)S(1)} %add_convert_fusion.q_ref), channel_id=1, source_target_pairs={{0,2},{2,0},{1,3},{3,1},{4,6},{6,4},{5,7},{7,5},{8,10},{10,8},{9,1... | collective-permute-start | bytes 786440 | tf_op jit(solution)/shard_map/ppermute | solution.py:30
  110.1 7.4 %collective-permute-start.25 = (bf16[2,256,128]{2,1,0:T(8,128)(2,1)S(1)}, bf16[2,256,128]{2,1,0:T(8,128)(2,1)S(1)}, u32[]{:S(2)}, u32[]{:S(2)}) collective-permute-start(bf16[2,256,128]{2,1,0:T(8,128)(2,1)S(1)} %slice.228), channel_id=1, source_target_pairs={{0,2},{2,0},{1,3},{3,1},{4,6},{6,4},{5,7},{7,5},{8,10},{10,8},{9,1... | collective-permute-start | bytes 393224 | tf_op jit(solution)/shard_map/ppermute | solution.py:30
  114.6 2.9 %collective-permute-start.23 = (f32[2,2,256]{2,0,1:T(2,128)S(1)}, f32[2,2,256]{2,0,1:T(2,128)S(1)}, u32[]{:S(2)}, u32[]{:S(2)}) collective-permute-start(f32[2,2,256]{2,0,1:T(2,128)S(1)} %reshape.202), channel_id=1, source_target_pairs={{0,2},{2,0},{1,3},{3,1},{4,6},{6,4},{5,7},{7,5},{8,10},{10,8},{9,1... | collective-permute-start | bytes 12296 | tf_op jit(solution)/shard_map/ppermute | solution.py:30
  115.7 4.1 %collective-permute-start.24 = (bf16[2,256,128]{2,1,0:T(8,128)(2,1)S(1)}, bf16[2,256,128]{2,1,0:T(8,128)(2,1)S(1)}, u32[]{:S(2)}, u32[]{:S(2)}) collective-permute-start(bf16[2,256,128]{2,1,0:T(8,128)(2,1)S(1)} %slice.224), channel_id=1, source_target_pairs={{0,2},{2,0},{1,3},{3,1},{4,6},{6,4},{5,7},{7,5},{8,10},{10,8},{9,1... | collective-permute-start | bytes 393224 | tf_op jit(solution)/shard_map/ppermute | solution.py:30
  120.1 7.2 %collective-permute-start.26 = (bf16[2,256,128]{2,1,0:T(8,128)(2,1)S(1)}, bf16[2,256,128]{2,1,0:T(8,128)(2,1)S(1)}, u32[]{:S(2)}, u32[]{:S(2)}) collective-permute-start(bf16[2,256,128]{2,1,0:T(8,128)(2,1)S(1)} %get-tuple-element.78), channel_id=1, source_target_pairs={{0,1},{1,0},{2,3},{3,2},{4,5},{5,4},{6,7},{7,6},{8,9},{9,8},{10,11... | collective-permute-start | bytes 393224 | tf_op jit(solution)/shard_map/ppermute | solution.py:30
Sparse Core Ops, SparseCore 0:
  13.1 52.5 all-gather.1

commit v7 on v6

--- a/solution.py
+++ b/solution.py
@@ -234,6 +234,34 @@
         cost_estimate=pl.CostEstimate(flops=3 << 30, bytes_accessed=6 << 20, transcendentals=0),
         name="attend_last",
     )(flags, q, qs, m, acc, k3, v3)
+
+
+def pick_kernel(me, shard, row, states, out):
+    first = last = jnp.int32(0)
+    groups, per = shard.shape
+    places = [(g, n) for g in range(groups) for n in range(per)]
+    for g, n in places:
+        last = jnp.where(shard[g, n] == me[0], row[g, n], last)
+    for g, n in reversed(places):
+        first = jnp.where(shard[g, n] == me[0], row[g, n], first)
+    out[0] = states[first]
+    out[1] = states[last]
+
+
+def pick_pair(me, shard, row, states):
+    return pl.pallas_call(
+        pick_kernel,
+        grid_spec=pltpu.PrefetchScalarGridSpec(
+            num_scalar_prefetch=3,
+            grid=(1,),
+            in_specs=[pl.BlockSpec(states.shape, lambda t, a, b, c: (0, 0, 0))],
+            out_specs=pl.BlockSpec((2,) + states.shape[1:], lambda t, a, b, c: (0, 0, 0)),
+        ),
+        out_shape=jax.ShapeDtypeStruct((2,) + states.shape[1:], states.dtype),
+        compiler_params=params(24),
+        cost_estimate=pl.CostEstimate(flops=1 << 20, bytes_accessed=4 << 20, transcendentals=0),
+        name="pick_pair",
+    )(me, shard, row, states)
 
 
 def side_kernel(skip, u0, u1, u2, u3, d0, d1, d2, d3, out):
@@ -395,17 +423,7 @@
 
     kv0, shard, row = lax.optimization_barrier((jnp.stack([k, v]), nb_shard, nb_row))
 
-    place = 2 * lax.broadcasted_iota(jnp.int32, nb_shard.shape, 0) + lax.broadcasted_iota(
-        jnp.int32, nb_shard.shape, 1
-    )
-    coded = place * states.shape[0] + row
-    asked = shard == db_index
-    none = nb_shard.size * states.shape[0]
-    first = jnp.min(jnp.where(asked, coded, none)) & (states.shape[0] - 1)
-    last = jnp.max(jnp.where(asked, coded, 0)) & (states.shape[0] - 1)
-    pair = jnp.concatenate(
-        [lax.dynamic_slice_in_dim(states, i, 1, 0) for i in (first, last)], axis=0
-    )
+    pair = pick_pair(db_index.astype(jnp.int32)[None], shard, row, states)
     held_a = lax.all_gather(pair, "z", axis=0, tiled=True)
 
     kv1 = ring(kv0, "y", 1)

time: 136 us -> 137 us (level)
  other arithmetic: 5.99 us -> 2.75 us
  Pallas kernels: 24.6 us -> 27.4 us
  local copies, waits for them, and re-layouts: 11.6 us -> 13.1 us
  waiting for transfers between devices: 21.8 us -> 23.2 us
    pallas_call x0 -> x1, Pallas kernels: none -> 1.75 us  [pick_pair(): pl.pallas_call(pick_kernel, grid_spec=pltpu.PrefetchScalarGridSpec(num_sc...]
    optimization_barrier x0 -> x2, local copies, waits for them, and re-layouts: none -> 1.51 us  [local(): lax.optimization_barrier((jnp.stack([k, v]), nb_shard, nb_row))]
    unnamed x21 -> x23, local copies, waits for them, and re-layouts: 5.77 us -> 6.87 us
  transfers between devices with their start and end apart: 28 -> 28, of which waited for: 11 -> 11; matrix products, arithmetic and copies ran while one was open for 8% -> 7% of each run, Pallas kernels for 18% -> 19%
where the time goes in v7:
time: 137 us; the launch traced here: 136 us
  starting transfers between devices  42.7 us (31%)
  Pallas kernels  27.4 us (20%)
  waiting for transfers between devices  23.2 us (17%)
  between operations  14.6 us (11%)
  local copies, waits for them, and re-layouts  13.1 us (10%)
  blocking collectives  7.5 us (5%)
  matrix products  4.51 us (3%)
  other arithmetic  2.75 us (2%)
    ppermute x14, starting transfers between devices, ring(): return lax.ppermute(value, axis, [(i, (i + step) % n) for i in range(n)])  19.6 us
    ppermute x10, starting transfers between devices, swap(): return lax.ppermute(value, axis, [(0, 1), (1, 0)])  16.7 us
    ppermute x14, waiting for transfers between devices, ring(): return lax.ppermute(value, axis, [(i, (i + step) % n) for i in range(n)])  10 us
    pallas_call x1, Pallas kernels, project(): pl.pallas_call(project_kernel, grid_spec=pltpu.PrefetchScalarGridSpec(num...  8.26 us
    all_to_all x1, blocking collectives, local(): mine = lax.all_to_all(self_out.reshape(4, quarter, HD), XC, 0, 0)  7.5 us
    ppermute x1, waiting for transfers between devices, local(): lse_back = lax.ppermute(lse_sent, 'x_hi', [(0, 1)])  7.01 us
    unnamed x23, local copies, waits for them, and re-layouts  6.87 us
    ppermute x10, waiting for transfers between devices, swap(): return lax.ppermute(value, axis, [(0, 1), (1, 0)])  6.14 us
  transfers between devices with their start and end apart: 28, of which 11 were waited for; matrix products, arithmetic and copies ran while one was open for 7% of the time, Pallas kernels for 19%

profile of v7, /device:TPU:31, one launch (start us, length us, event | category | flops | bytes accessed | tf_op | source)
XLA Modules:
  0.0 135.8 jit_solution(7525502097491340377)
XLA Ops:
  7.3 1.1 pad_maximum_fusion.1.kv_ref.kv0
  8.4 0.8 copy.38.shard
  9.2 0.8 copy.39.row
  9.9 2.0 %copy-done.2 = bf16[16,128,896]{2,1,0:T(8,128)(2,1)S(1)} copy-done((bf16[16,128,896]{2,1,0:T(8,128)(2,1)S(1)}, bf16[16,128,896]{2,1,0:T(8,128)(2,1)}, u32[]{:S(2)}) %copy-start.2) | copy-done | bytes 3670040
  12.0 1.7 %pick_pair.1 = bf16[2,128,896]{2,1,0:T(8,128)(2,1)} custom-call(s32[1]{0:T(128)} %bitcast.14.me, s32[16,2]{1,0:T(8,128)S(1)} %copy.38.shard, s32[16,2]{1,0:T(8,128)S(1)} %copy.39.row, bf16[16,128,896]{2,1,0:T(8,128)(2,1)S(1)} %copy-done.2), custom_call_target="tpu_custom_call" | custom-call | flops 1048576 | bytes 4194304 | tf_op jit(solution)/shard_map/pick_pair/pallas_call | solution.py:252
  13.8 1.5 %collective-permute-start.2 = (bf16[2,1024,128]{2,1,0:T(8,128)(2,1)S(1)}, bf16[2,1024,128]{2,1,0:T(8,128)(2,1)}, u32[]{:S(2)}, u32[]{:S(2)}) collective-permute-start(bf16[2,1024,128]{2,1,0:T(8,128)(2,1)S(1)} %pad_maximum_fusion.1.kv_ref.kv0), channel_id=1, source_target_pairs={{0,96},{32,0},{64,32},{96,64},{1,97},{33,1},{65,33},{97,65},{2,98}... | collective-permute-start | bytes 1572872 | tf_op jit(solution)/shard_map/ppermute | solution.py:26
  15.3 3.7 %collective-permute-start = (bf16[1024,128]{1,0:T(8,128)(2,1)}, bf16[1024,128]{1,0:T(8,128)(2,1)}, u32[]{:S(2)}, u32[]{:S(2)}) collective-permute-start(bf16[1024,128]{1,0:T(8,128)(2,1)} %q_ref.5), channel_id=1, source_target_pairs={{128,0},{129,1},{130,2},{131,3},{132,4},{133,5},{134,6},{135,7},{1... | collective-permute-start | bytes 786440 | tf_op jit(solution)/shard_map/ppermute | solution.py:431
  19.1 1.2 slice.179.d0
  20.3 2.7 %collective-permute-start.8 = (bf16[2944,128]{1,0:T(8,128)(2,1)S(1)}, bf16[2944,128]{1,0:T(8,128)(2,1)}, u32[]{:S(2)}, u32[]{:S(2)}) collective-permute-start(bf16[2944,128]{1,0:T(8,128)(2,1)S(1)} %slice.179.d0), channel_id=1, source_target_pairs={{0,2},{2,128},{128,130},{130,0},{1,3},{3,129},{129,131},{131,1},{4... | collective-permute-start | bytes 2261000 | tf_op jit(solution)/shard_map/ppermute | solution.py:26
  23.2 2.2 %attend_own.1 = (f32[1024,128]{1,0:T(8,128)S(1)}, f32[1024,256]{1,0:T(8,128)S(1)}) custom-call(bf16[1024,128]{1,0:T(8,128)(2,1)} %q_ref.5, bf16[2,1024,128]{2,1,0:T(8,128)(2,1)S(1)} %pad_maximum_fusion.1.kv_ref.kv0), custom_call_target="tpu_custom_call" | custom-call | flops 1073741824 | bytes 3145728 | tf_op jit(solution)/shard_map/attend_own/pallas_call | solution.py:95
  25.4 1.3 collective-permute-done.1.kv1
  26.7 1.3 collective-permute-start.3
  28.0 1.0 slice_bitcast_fusion
  29.3 5.8 %attend_middle.1 = (f32[2,1024,128]{2,1,0:T(8,128)S(1)}, f32[2,1024,256]{2,1,0:T(8,128)S(1)}) custom-call(s32[8]{0:T(128)S(1)} %convert_element_type.33.flags, bf16[1024,128]{1,0:T(8,128)(2,1)} %q_ref.5, bf16[1024,128]{1,0:T(8,128)(2,1)} %collective-permute-done.qs_ref, f32[1024,128]{1,0:T(8,128)S(1)} %get-tuple-element.34.m_in, ...), custom_call_target="tpu_custom_call" | custom-call | flops 8589934592 | bytes 6291456 | tf_op jit(solution)/shard_map/attend_middle/pallas_call | solution.py:135
  35.1 1.3 collective-permute-done.4.v3
  36.4 4.0 %attend_last.1 = (f32[1024,128]{1,0:T(8,128)S(1)}, bf16[1024,128]{1,0:T(8,128)(2,1)S(1)}, f32[2,4,1,256]{3,2,1,0:T(1,128)S(1)}) custom-call(s32[8]{0:T(128)S(1)} %convert_element_type.33.flags, bf16[1024,128]{1,0:T(8,128)(2,1)} %q_ref.5, bf16[1024,128]{1,0:T(8,128)(2,1)} %collective-permute-done.qs_ref, f32[2,1024,128]{2,1,0:T(8,128)S(1)} %get-tuple-element.36.m_in, ...), custom_call_target="tpu_custom_call" | custom-call | flops 3221225472 | bytes 6291456 | tf_op jit(solution)/shard_map/attend_last/pallas_call | solution.py:206
  40.4 1.3 collective-permute-start.5
  41.7 1.3 collective-permute-start.6
  43.0 2.6 %collective-permute-start.11 = (bf16[2944,128]{1,0:T(8,128)(2,1)S(1)}, bf16[2944,128]{1,0:T(8,128)(2,1)S(1)}, u32[]{:S(2)}, u32[]{:S(2)}) collective-permute-start(bf16[2944,128]{1,0:T(8,128)(2,1)S(1)} %pad_maximum_fusion.u0.w0), channel_id=1, source_target_pairs={{0,1},{1,0},{2,3},{3,2},{4,5},{5,4},{6,7},{7,6},{8,9},{9,8},{10,11... | collective-permute-start | bytes 2261000 | tf_op jit(solution)/shard_map/ppermute | solution.py:30
  45.8 7.0 %collective-permute-done.6 = f32[4,1,256]{2,1,0:T(1,128)S(1)} collective-permute-done((f32[4,1,256]{2,1,0:T(1,128)S(1)}, f32[4,1,256]{2,1,0:T(1,128)S(1)}, u32[]{:S(2)}, u32[]{:S(2)}) %collective-permute-start.6) | collective-permute-done | bytes 4128 | tf_op jit(solution)/shard_map/ppermute | solution.py:446
  52.8 2.6 %collective-permute-start.12 = (bf16[2944,128]{1,0:T(8,128)(2,1)S(1)}, bf16[2944,128]{1,0:T(8,128)(2,1)S(1)}, u32[]{:S(2)}, u32[]{:S(2)}) collective-permute-start(bf16[2944,128]{1,0:T(8,128)(2,1)S(1)} %collective-permute-done.7.u2.w2), channel_id=1, source_target_pairs={{0,1},{1,0},{2,3},{3,2},{4,5},{5,4},{6,7},{7,6},{8,9},{9,8},{10,11... | collective-permute-start | bytes 2261000 | tf_op jit(solution)/shard_map/ppermute | solution.py:30
  55.9 7.5 %all_to_all.5 = bf16[4,256,128]{2,1,0:T(8,128)(2,1)S(1)} all-to-all(bf16[4,256,128]{2,1,0:T(8,128)(2,1)S(1)} %bitcast.173), channel_id=1, replica_groups=mesh['x_hi'=2,'y'=4,'z'=8,'x_lo'=2,'core'=2] {'x_lo','core'}, dimensions={0} | all-to-all | bytes 524288 | tf_op jit(solution)/shard_map/all_to_all | solution.py:470
  63.4 5.4 %collective-permute-start.10 = (bf16[4,256,128]{2,1,0:T(8,128)(2,1)S(1)}, bf16[4,256,128]{2,1,0:T(8,128)(2,1)S(1)}, u32[]{:S(2)}, u32[]{:S(2)}) collective-permute-start(bf16[4,256,128]{2,1,0:T(8,128)(2,1)S(1)} %all_to_all.5), channel_id=1, source_target_pairs={{0,28},{4,0},{8,4},{12,8},{16,12},{20,16},{24,20},{28,24},{1,29},{... | collective-permute-start | bytes 786440 | tf_op jit(solution)/shard_map/ppermute | solution.py:26
  68.9 2.1 %side_by_side.1 = bf16[4096,512]{1,0:T(8,128)(2,1)S(1)} custom-call(bf16[2944,128]{1,0:T(8,128)(2,1)S(1)} %pad_maximum_fusion.u0.w0, bf16[2944,128]{1,0:T(8,128)(2,1)S(1)} %collective-permute-done.11.u1.w1, bf16[2944,128]{1,0:T(8,128)(2,1)S(1)} %collective-permute-done.7.u2.w2, bf16[2944,128]{1,0:T(8,128)(2,1)S(1)} %collective-permute-done.12.u3.w3, ...), custom_call_target="tpu_custom_call" | custom-call | flops 1048576 | bytes 10485760 | tf_op jit(solution)/shard_map/side_by_side/pallas_call | solution.py:276
  71.1 2.0 %copy-done = bf16[4096,512]{1,0:T(8,128)(2,1)} copy-done((bf16[4096,512]{1,0:T(8,128)(2,1)}, bf16[4096,512]{1,0:T(8,128)(2,1)S(1)}, u32[]{:S(2)}) %copy-start) | copy-done | bytes 4194328
  73.1 0.9 collective-permute-done.10
  74.7 2.5 %collective-permute-done.9 = bf16[4,256,128]{2,1,0:T(8,128)(2,1)} collective-permute-done((bf16[4,256,128]{2,1,0:T(8,128)(2,1)S(1)}, bf16[4,256,128]{2,1,0:T(8,128)(2,1)}, u32[]{:S(2)}, u32[]{:S(2)}) %collective-permute-start.9) | collective-permute-done | bytes 262176 | tf_op jit(solution)/shard_map/ppermute | solution.py:26
  77.2 1.8 %collective-permute-start.19 = (bf16[16,128,896]{2,1,0:T(8,128)(2,1)}, bf16[16,128,896]{2,1,0:T(8,128)(2,1)}, u32[]{:S(2)}, u32[]{:S(2)}) collective-permute-start(bf16[16,128,896]{2,1,0:T(8,128)(2,1)} %all-gather.2.cloned.1.call-done.a_ref), channel_id=1, source_target_pairs={{0,1},{1,0},{2,3},{3,2},{4,5},{5,4},{6,7},{7,6},{8,9},{9,8},{10,11... | collective-permute-start | bytes 11010056 | tf_op jit(solution)/shard_map/ppermute | solution.py:30
  79.7 2.7 %collective-permute-start.17 = (bf16[4,256,128]{2,1,0:T(8,128)(2,1)}, bf16[4,256,128]{2,1,0:T(8,128)(2,1)S(1)}, u32[]{:S(2)}, u32[]{:S(2)}) collective-permute-start(bf16[4,256,128]{2,1,0:T(8,128)(2,1)} %copy-done.7), channel_id=1, source_target_pairs={{0,28},{4,0},{8,4},{12,8},{16,12},{20,16},{24,20},{28,24},{1,29},{... | collective-permute-start | bytes 786440 | tf_op jit(solution)/shard_map/ppermute | solution.py:26
  82.4 1.1 slice_bitcast_fusion.21
  83.5 1.3 fusion.8
  84.8 1.3 convolution_add_fusion.5
  86.2 2.9 %collective-permute-done.15 = bf16[4,256,128]{2,1,0:T(8,128)(2,1)S(1)} collective-permute-done((bf16[4,256,128]{2,1,0:T(8,128)(2,1)}, bf16[4,256,128]{2,1,0:T(8,128)(2,1)S(1)}, u32[]{:S(2)}, u32[]{:S(2)}) %collective-permute-start.15) | collective-permute-done | bytes 262176 | tf_op jit(solution)/shard_map/ppermute | solution.py:26
  89.1 2.7 %collective-permute-start.18 = (bf16[4,256,128]{2,1,0:T(8,128)(2,1)S(1)}, bf16[4,256,128]{2,1,0:T(8,128)(2,1)S(1)}, u32[]{:S(2)}, u32[]{:S(2)}) collective-permute-start(bf16[4,256,128]{2,1,0:T(8,128)(2,1)S(1)} %collective-permute-done.17), channel_id=1, source_target_pairs={{0,28},{4,0},{8,4},{12,8},{16,12},{20,16},{24,20},{28,24},{1,29},{... | collective-permute-start | bytes 786440 | tf_op jit(solution)/shard_map/ppermute | solution.py:26
  92.2 2.0 %copy-done.5 = bf16[16,128,896]{2,1,0:T(8,128)(2,1)S(1)} copy-done((bf16[16,128,896]{2,1,0:T(8,128)(2,1)S(1)}, bf16[16,128,896]{2,1,0:T(8,128)(2,1)}, u32[]{:S(2)}) %copy-start.5) | copy-done | bytes 3670040
  94.2 8.3 %project.1 = (bf16[8,512,256]{2,1,0:T(8,128)(2,1)S(1)}, bf16[8,256,512]{2,1,0:T(8,128)(2,1)S(1)}) custom-call(s32[16]{0:T(128)S(1)} %add_bitcast_fusion.info, bf16[16,128,896]{2,1,0:T(8,128)(2,1)S(1)} %copy-done.5, bf16[16,128,896]{2,1,0:T(8,128)(2,1)} %collective-permute-done.19.b_ref, bf16[2944,128]{1,0:T(8,128)(2,1)S(1)} %pad_maximum_fusion.u0.w0, ...), custom_call_target="tpu_custom_call" | custom-call | flops 4294967296 | bytes 12582912 | tf_op jit(solution)/shard_map/project/pallas_call | solution.py:326
  102.7 2.7 %collective-permute-start.21 = (bf16[2,256,128]{2,1,0:T(8,128)(2,1)S(1)}, bf16[2,256,128]{2,1,0:T(8,128)(2,1)S(1)}, u32[]{:S(2)}, u32[]{:S(2)}) collective-permute-start(bf16[2,256,128]{2,1,0:T(8,128)(2,1)S(1)} %slice.182), channel_id=1, source_target_pairs={{0,28},{4,0},{8,4},{12,8},{16,12},{20,16},{24,20},{28,24},{1,29},{... | collective-permute-start | bytes 393224 | tf_op jit(solution)/shard_map/ppermute | solution.py:26
  106.6 1.1 collective-permute-done.20
  108.1 1.2 collective-permute-start.22
  109.3 1.7 %cross.2 = (bf16[4,256,128]{2,1,0:T(8,128)(2,1)S(1)}, f32[4,8,64]{2,1,0:T(8,128)S(1)}) custom-call(s32[8]{0:T(128)S(1)} %bitcast.172, bf16[256,512]{1,0:T(8,128)(2,1)S(1)} %add_convert_fusion.q_ref, bf16[8,512,256]{2,1,0:T(8,128)(2,1)S(1)} %get-tuple-element.58.k_ref, bf16[8,256,512]{2,1,0:T(8,128)(2,1)S(1)} %get-tuple-element.59.v_ref), custom_call_target="tpu_custom_call" | custom-call | flops 2147483648 | bytes 3145728 | tf_op jit(solution)/shard_map/cross/pallas_call | solution.py:382
  111.7 2.0 %collective-permute-done.22 = bf16[256,512]{1,0:T(8,128)(2,1)S(1)} collective-permute-done((bf16[256,512]{1,0:T(8,128)(2,1)S(1)}, bf16[256,512]{1,0:T(8,128)(2,1)S(1)}, u32[]{:S(2)}, u32[]{:S(2)}) %collective-permute-start.22) | collective-permute-done | bytes 262176 | tf_op jit(solution)/shard_map/ppermute | solution.py:30
  113.7 1.7 %cross.3 = (bf16[4,256,128]{2,1,0:T(8,128)(2,1)S(1)}, f32[4,8,64]{2,1,0:T(8,128)S(1)}) custom-call(s32[8]{0:T(128)S(1)} %bitcast.171, bf16[256,512]{1,0:T(8,128)(2,1)S(1)} %pad_maximum_fusion.2.q_ref, bf16[8,512,256]{2,1,0:T(8,128)(2,1)S(1)} %get-tuple-element.58.k_ref, bf16[8,256,512]{2,1,0:T(8,128)(2,1)S(1)} %get-tuple-element.59.v_ref), custom_call_target="tpu_custom_call" | custom-call | flops 2147483648 | bytes 3145728 | tf_op jit(solution)/shard_map/cross/pallas_call | solution.py:382
  115.5 0.9 collective-permute-start.23
  117.2 1.2 collective-permute-done.23
  118.7 2.0 %collective-permute-done.24 = bf16[2,256,128]{2,1,0:T(8,128)(2,1)S(1)} collective-permute-done((bf16[2,256,128]{2,1,0:T(8,128)(2,1)S(1)}, bf16[2,256,128]{2,1,0:T(8,128)(2,1)S(1)}, u32[]{:S(2)}, u32[]{:S(2)}) %collective-permute-start.24) | collective-permute-done | bytes 131104 | tf_op jit(solution)/shard_map/ppermute | solution.py:30
  121.0 6.2 %collective-permute-start.26 = (bf16[2,256,128]{2,1,0:T(8,128)(2,1)S(1)}, bf16[2,256,128]{2,1,0:T(8,128)(2,1)S(1)}, u32[]{:S(2)}, u32[]{:S(2)}) collective-permute-start(bf16[2,256,128]{2,1,0:T(8,128)(2,1)S(1)} %get-tuple-element.74), channel_id=1, source_target_pairs={{0,1},{1,0},{2,3},{3,2},{4,5},{5,4},{6,7},{7,6},{8,9},{9,8},{10,11... | collective-permute-start | bytes 393224 | tf_op jit(solution)/shard_map/ppermute | solution.py:30
  127.2 1.0 collective-permute-done.26
  128.3 0.7 copy.45
  (102 shorter events, 7.2 us)
Async XLA Ops:
  7.2 11.8 %slice-start = ((bf16[4096,128]{1,0:T(8,128)(2,1)}), bf16[1152,128]{1,0:T(8,128)(2,1)S(1)}, s32[]{:S(2)}) async-start(bf16[4096,128]{1,0:T(8,128)(2,1)} %param.17), calls=%async_computation.2 | async-start | bytes 589824 | tf_op jit(solution)/shard_map/slice | solution.py:439
  7.2 11.8 %copy-start.9 = (bf16[896,128]{1,0:T(8,128)(2,1)S(1)}, bf16[896,128]{1,0:T(8,128)(2,1)}, u32[]{:S(2)}) copy-start(bf16[896,128]{1,0:T(8,128)(2,1)} %param.15) | copy-start | bytes 688132
  7.2 11.8 %copy-start.8 = (bf16[896,128]{1,0:T(8,128)(2,1)S(1)}, bf16[896,128]{1,0:T(8,128)(2,1)}, u32[]{:S(2)}) copy-start(bf16[896,128]{1,0:T(8,128)(2,1)} %param.16) | copy-start | bytes 688132
  7.2 70.0 %all-gather.2.cloned.1.call-start = ((), (), s32[]{:S(2)}) async-start(), calls=%async_computation.1 | async-start | bytes 4128768 | tf_op jit(solution)/shard_map/all_gather | solution.py:427
  9.9 2.0 %copy-start.2 = (bf16[16,128,896]{2,1,0:T(8,128)(2,1)S(1)}, bf16[16,128,896]{2,1,0:T(8,128)(2,1)}, u32[]{:S(2)}) copy-start(bf16[16,128,896]{2,1,0:T(8,128)(2,1)} %states.1) | copy-start | bytes 11010052
  13.7 13.0 %collective-permute-start.1 = (bf16[2,1024,128]{2,1,0:T(8,128)(2,1)S(1)}, bf16[2,1024,128]{2,1,0:T(8,128)(2,1)S(1)}, u32[]{:S(2)}, u32[]{:S(2)}) collective-permute-start(bf16[2,1024,128]{2,1,0:T(8,128)(2,1)S(1)} %pad_maximum_fusion.1.kv_ref.kv0), channel_id=1, source_target_pairs={{0,32},{32,64},{64,96},{96,0},{1,33},{33,65},{65,97},{97,1},{2,34}... | collective-permute-start | bytes 1572872 | tf_op jit(solution)/shard_map/ppermute | solution.py:26
  13.8 14.2 %collective-permute-start.2 = (bf16[2,1024,128]{2,1,0:T(8,128)(2,1)S(1)}, bf16[2,1024,128]{2,1,0:T(8,128)(2,1)}, u32[]{:S(2)}, u32[]{:S(2)}) collective-permute-start(bf16[2,1024,128]{2,1,0:T(8,128)(2,1)S(1)} %pad_maximum_fusion.1.kv_ref.kv0), channel_id=1, source_target_pairs={{0,96},{32,0},{64,32},{96,64},{1,97},{33,1},{65,33},{97,65},{2,98}... | collective-permute-start | bytes 1572872 | tf_op jit(solution)/shard_map/ppermute | solution.py:26
  15.3 14.1 %collective-permute-start = (bf16[1024,128]{1,0:T(8,128)(2,1)}, bf16[1024,128]{1,0:T(8,128)(2,1)}, u32[]{:S(2)}, u32[]{:S(2)}) collective-permute-start(bf16[1024,128]{1,0:T(8,128)(2,1)} %q_ref.5), channel_id=1, source_target_pairs={{128,0},{129,1},{130,2},{131,3},{132,4},{133,5},{134,6},{135,7},{1... | collective-permute-start | bytes 786440 | tf_op jit(solution)/shard_map/ppermute | solution.py:431
  19.1 26.6 %collective-permute-start.7 = (bf16[2944,128]{1,0:T(8,128)(2,1)S(1)}, bf16[2944,128]{1,0:T(8,128)(2,1)S(1)}, u32[]{:S(2)}, u32[]{:S(2)}) collective-permute-start(bf16[2944,128]{1,0:T(8,128)(2,1)S(1)} %pad_maximum_fusion.u0.w0), channel_id=1, source_target_pairs={{0,130},{2,0},{128,2},{130,128},{1,131},{3,1},{129,3},{131,129},{4... | collective-permute-start | bytes 2261000 | tf_op jit(solution)/shard_map/ppermute | solution.py:26
  20.3 25.5 %collective-permute-start.8 = (bf16[2944,128]{1,0:T(8,128)(2,1)S(1)}, bf16[2944,128]{1,0:T(8,128)(2,1)}, u32[]{:S(2)}, u32[]{:S(2)}) collective-permute-start(bf16[2944,128]{1,0:T(8,128)(2,1)S(1)} %slice.179.d0), channel_id=1, source_target_pairs={{0,2},{2,128},{128,130},{130,0},{1,3},{3,129},{129,131},{131,1},{4... | collective-permute-start | bytes 2261000 | tf_op jit(solution)/shard_map/ppermute | solution.py:26
  26.7 8.4 %collective-permute-start.3 = (bf16[1024,128]{1,0:T(8,128)(2,1)S(1)}, bf16[1024,128]{1,0:T(8,128)(2,1)S(1)}, u32[]{:S(2)}, u32[]{:S(2)}) collective-permute-start(bf16[1024,128]{1,0:T(8,128)(2,1)S(1)} %slice_bitcast_fusion.1), channel_id=1, source_target_pairs={{0,32},{32,64},{64,96},{96,0},{1,33},{33,65},{65,97},{97,1},{2,34}... | collective-permute-start | bytes 786440 | tf_op jit(solution)/shard_map/ppermute | solution.py:26
  29.0 7.4 %collective-permute-start.4 = (bf16[1024,128]{1,0:T(8,128)(2,1)S(1)}, bf16[1024,128]{1,0:T(8,128)(2,1)S(1)}, u32[]{:S(2)}, u32[]{:S(2)}) collective-permute-start(bf16[1024,128]{1,0:T(8,128)(2,1)S(1)} %slice_bitcast_fusion), channel_id=1, source_target_pairs={{0,96},{32,0},{64,32},{96,64},{1,97},{33,1},{65,33},{97,65},{2,98}... | collective-permute-start | bytes 786440 | tf_op jit(solution)/shard_map/ppermute | solution.py:26
  40.4 12.4 %collective-permute-start.5 = (bf16[1024,128]{1,0:T(8,128)(2,1)S(1)}, bf16[1024,128]{1,0:T(8,128)(2,1)S(1)}, u32[]{:S(2)}, u32[]{:S(2)}) collective-permute-start(bf16[1024,128]{1,0:T(8,128)(2,1)S(1)} %get-tuple-element.40), channel_id=1, source_target_pairs={{0,128},{1,129},{2,130},{3,131},{4,132},{5,133},{6,134},{7,135},{8... | collective-permute-start | bytes 786440 | tf_op jit(solution)/shard_map/ppermute | solution.py:445
  41.7 11.1 %collective-permute-start.6 = (f32[4,1,256]{2,1,0:T(1,128)S(1)}, f32[4,1,256]{2,1,0:T(1,128)S(1)}, u32[]{:S(2)}, u32[]{:S(2)}) collective-permute-start(f32[4,1,256]{2,1,0:T(1,128)S(1)} %get-tuple-element.112), channel_id=1, source_target_pairs={{0,128},{1,129},{2,130},{3,131},{4,132},{5,133},{6,134},{7,135},{8... | collective-permute-start | bytes 12296 | tf_op jit(solution)/shard_map/ppermute | solution.py:446
  43.0 25.8 %collective-permute-start.11 = (bf16[2944,128]{1,0:T(8,128)(2,1)S(1)}, bf16[2944,128]{1,0:T(8,128)(2,1)S(1)}, u32[]{:S(2)}, u32[]{:S(2)}) collective-permute-start(bf16[2944,128]{1,0:T(8,128)(2,1)S(1)} %pad_maximum_fusion.u0.w0), channel_id=1, source_target_pairs={{0,1},{1,0},{2,3},{3,2},{4,5},{5,4},{6,7},{7,6},{8,9},{9,8},{10,11... | collective-permute-start | bytes 2261000 | tf_op jit(solution)/shard_map/ppermute | solution.py:30
  45.7 23.2 %collective-permute-start.13 = (bf16[2944,128]{1,0:T(8,128)(2,1)S(1)}, bf16[2944,128]{1,0:T(8,128)(2,1)S(1)}, u32[]{:S(2)}, u32[]{:S(2)}) collective-permute-start(bf16[2944,128]{1,0:T(8,128)(2,1)S(1)} %slice.179.d0), channel_id=1, source_target_pairs={{0,1},{1,0},{2,3},{3,2},{4,5},{5,4},{6,7},{7,6},{8,9},{9,8},{10,11... | collective-permute-start | bytes 2261000 | tf_op jit(solution)/shard_map/ppermute | solution.py:30
  52.8 16.1 %collective-permute-start.12 = (bf16[2944,128]{1,0:T(8,128)(2,1)S(1)}, bf16[2944,128]{1,0:T(8,128)(2,1)S(1)}, u32[]{:S(2)}, u32[]{:S(2)}) collective-permute-start(bf16[2944,128]{1,0:T(8,128)(2,1)S(1)} %collective-permute-done.7.u2.w2), channel_id=1, source_target_pairs={{0,1},{1,0},{2,3},{3,2},{4,5},{5,4},{6,7},{7,6},{8,9},{9,8},{10,11... | collective-permute-start | bytes 2261000 | tf_op jit(solution)/shard_map/ppermute | solution.py:30
  55.4 13.5 %collective-permute-start.14 = (bf16[2944,128]{1,0:T(8,128)(2,1)}, bf16[2944,128]{1,0:T(8,128)(2,1)S(1)}, u32[]{:S(2)}, u32[]{:S(2)}) collective-permute-start(bf16[2944,128]{1,0:T(8,128)(2,1)} %collective-permute-done.8.d2), channel_id=1, source_target_pairs={{0,1},{1,0},{2,3},{3,2},{4,5},{5,4},{6,7},{7,6},{8,9},{9,8},{10,11... | collective-permute-start | bytes 2261000 | tf_op jit(solution)/shard_map/ppermute | solution.py:30
  55.9 15.1 %copy-start.6 = (bf16[1024,128]{1,0:T(8,128)(2,1)}, bf16[1024,128]{1,0:T(8,128)(2,1)S(1)}, u32[]{:S(2)}) copy-start(bf16[1024,128]{1,0:T(8,128)(2,1)S(1)} %divide_convert_fusion) | copy-start | bytes 786436
  63.4 15.5 %copy-start.10 = (s32[16,2]{0,1:T(2,128)S(1)}, s32[16,2]{0,1:T(2,128)}, u32[]{:S(2)}) copy-start(s32[16,2]{0,1:T(2,128)} %param.13) | copy-start | bytes 388
  63.4 10.5 %collective-permute-start.10 = (bf16[4,256,128]{2,1,0:T(8,128)(2,1)S(1)}, bf16[4,256,128]{2,1,0:T(8,128)(2,1)S(1)}, u32[]{:S(2)}, u32[]{:S(2)}) collective-permute-start(bf16[4,256,128]{2,1,0:T(8,128)(2,1)S(1)} %all_to_all.5), channel_id=1, source_target_pairs={{0,28},{4,0},{8,4},{12,8},{16,12},{20,16},{24,20},{28,24},{1,29},{... | collective-permute-start | bytes 786440 | tf_op jit(solution)/shard_map/ppermute | solution.py:26
  68.9 8.3 %collective-permute-start.9 = (bf16[4,256,128]{2,1,0:T(8,128)(2,1)S(1)}, bf16[4,256,128]{2,1,0:T(8,128)(2,1)}, u32[]{:S(2)}, u32[]{:S(2)}) collective-permute-start(bf16[4,256,128]{2,1,0:T(8,128)(2,1)S(1)} %all_to_all.5), channel_id=1, source_target_pairs={{0,4},{4,8},{8,12},{12,16},{16,20},{20,24},{24,28},{28,0},{1,5},{5... | collective-permute-start | bytes 786440 | tf_op jit(solution)/shard_map/ppermute | solution.py:26
  68.9 2.1 %copy-start.3 = (bf16[2944,128]{1,0:T(8,128)(2,1)}, bf16[2944,128]{1,0:T(8,128)(2,1)S(1)}, u32[]{:S(2)}) copy-start(bf16[2944,128]{1,0:T(8,128)(2,1)S(1)} %collective-permute-done.12.u3.w3) | copy-start | bytes 2260996
  71.1 2.0 %copy-start = (bf16[4096,512]{1,0:T(8,128)(2,1)}, bf16[4096,512]{1,0:T(8,128)(2,1)S(1)}, u32[]{:S(2)}) copy-start(bf16[4096,512]{1,0:T(8,128)(2,1)S(1)} %side_by_side.1) | copy-start | bytes 12582916
  74.0 0.7 copy-start.7
  74.7 17.5 %copy-start.4 = (bf16[2944,128]{1,0:T(8,128)(2,1)S(1)}, bf16[2944,128]{1,0:T(8,128)(2,1)}, u32[]{:S(2)}) copy-start(bf16[2944,128]{1,0:T(8,128)(2,1)} %copy-done.3) | copy-start | bytes 2260996
  77.2 15.0 %collective-permute-start.19 = (bf16[16,128,896]{2,1,0:T(8,128)(2,1)}, bf16[16,128,896]{2,1,0:T(8,128)(2,1)}, u32[]{:S(2)}, u32[]{:S(2)}) collective-permute-start(bf16[16,128,896]{2,1,0:T(8,128)(2,1)} %all-gather.2.cloned.1.call-done.a_ref), channel_id=1, source_target_pairs={{0,1},{1,0},{2,3},{3,2},{4,5},{5,4},{6,7},{7,6},{8,9},{9,8},{10,11... | collective-permute-start | bytes 11010056 | tf_op jit(solution)/shard_map/ppermute | solution.py:30
  79.5 12.3 %copy-start.1 = (bf16[4096,512]{1,0:T(8,128)(2,1)S(1)}, bf16[4096,512]{1,0:T(8,128)(2,1)}, u32[]{:S(2)}) copy-start(bf16[4096,512]{1,0:T(8,128)(2,1)} %copy-done) | copy-start | bytes 12582916
  79.6 9.4 %collective-permute-start.15 = (bf16[4,256,128]{2,1,0:T(8,128)(2,1)}, bf16[4,256,128]{2,1,0:T(8,128)(2,1)S(1)}, u32[]{:S(2)}, u32[]{:S(2)}) collective-permute-start(bf16[4,256,128]{2,1,0:T(8,128)(2,1)} %collective-permute-done.9), channel_id=1, source_target_pairs={{0,4},{4,8},{8,12},{12,16},{16,20},{20,24},{24,28},{28,0},{1,5},{5... | collective-permute-start | bytes 786440 | tf_op jit(solution)/shard_map/ppermute | solution.py:26
  79.7 9.4 %collective-permute-start.17 = (bf16[4,256,128]{2,1,0:T(8,128)(2,1)}, bf16[4,256,128]{2,1,0:T(8,128)(2,1)S(1)}, u32[]{:S(2)}, u32[]{:S(2)}) collective-permute-start(bf16[4,256,128]{2,1,0:T(8,128)(2,1)} %copy-done.7), channel_id=1, source_target_pairs={{0,28},{4,0},{8,4},{12,8},{16,12},{20,16},{24,20},{28,24},{1,29},{... | collective-permute-start | bytes 786440 | tf_op jit(solution)/shard_map/ppermute | solution.py:26
  89.1 13.4 %collective-permute-start.16 = (bf16[4,256,128]{2,1,0:T(8,128)(2,1)S(1)}, bf16[4,256,128]{2,1,0:T(8,128)(2,1)S(1)}, u32[]{:S(2)}, u32[]{:S(2)}) collective-permute-start(bf16[4,256,128]{2,1,0:T(8,128)(2,1)S(1)} %collective-permute-done.15), channel_id=1, source_target_pairs={{0,4},{4,8},{8,12},{12,16},{16,20},{20,24},{24,28},{28,0},{1,5},{5... | collective-permute-start | bytes 786440 | tf_op jit(solution)/shard_map/ppermute | solution.py:26
  89.1 13.4 %collective-permute-start.18 = (bf16[4,256,128]{2,1,0:T(8,128)(2,1)S(1)}, bf16[4,256,128]{2,1,0:T(8,128)(2,1)S(1)}, u32[]{:S(2)}, u32[]{:S(2)}) collective-permute-start(bf16[4,256,128]{2,1,0:T(8,128)(2,1)S(1)} %collective-permute-done.17), channel_id=1, source_target_pairs={{0,28},{4,0},{8,4},{12,8},{16,12},{20,16},{24,20},{28,24},{1,29},{... | collective-permute-start | bytes 786440 | tf_op jit(solution)/shard_map/ppermute | solution.py:26
  92.1 2.0 %copy-start.5 = (bf16[16,128,896]{2,1,0:T(8,128)(2,1)S(1)}, bf16[16,128,896]{2,1,0:T(8,128)(2,1)}, u32[]{:S(2)}) copy-start(bf16[16,128,896]{2,1,0:T(8,128)(2,1)} %all-gather.2.cloned.1.call-done.a_ref) | copy-start | bytes 11010052
  102.6 5.1 %collective-permute-start.20 = (bf16[2,256,128]{2,1,0:T(8,128)(2,1)S(1)}, bf16[2,256,128]{2,1,0:T(8,128)(2,1)S(1)}, u32[]{:S(2)}, u32[]{:S(2)}) collective-permute-start(bf16[2,256,128]{2,1,0:T(8,128)(2,1)S(1)} %slice.181), channel_id=1, source_target_pairs={{0,4},{4,8},{8,12},{12,16},{16,20},{20,24},{24,28},{28,0},{1,5},{5... | collective-permute-start | bytes 393224 | tf_op jit(solution)/shard_map/ppermute | solution.py:26
  102.7 5.0 %collective-permute-start.21 = (bf16[2,256,128]{2,1,0:T(8,128)(2,1)S(1)}, bf16[2,256,128]{2,1,0:T(8,128)(2,1)S(1)}, u32[]{:S(2)}, u32[]{:S(2)}) collective-permute-start(bf16[2,256,128]{2,1,0:T(8,128)(2,1)S(1)} %slice.182), channel_id=1, source_target_pairs={{0,28},{4,0},{8,4},{12,8},{16,12},{20,16},{24,20},{28,24},{1,29},{... | collective-permute-start | bytes 393224 | tf_op jit(solution)/shard_map/ppermute | solution.py:26
  108.1 5.5 %collective-permute-start.22 = (bf16[256,512]{1,0:T(8,128)(2,1)S(1)}, bf16[256,512]{1,0:T(8,128)(2,1)S(1)}, u32[]{:S(2)}, u32[]{:S(2)}) collective-permute-start(bf16[256,512]{1,0:T(8,128)(2,1)S(1)} %add_convert_fusion.q_ref), channel_id=1, source_target_pairs={{0,2},{2,0},{1,3},{3,1},{4,6},{6,4},{5,7},{7,5},{8,10},{10,8},{9,1... | collective-permute-start | bytes 786440 | tf_op jit(solution)/shard_map/ppermute | solution.py:30
  111.0 7.4 %collective-permute-start.25 = (bf16[2,256,128]{2,1,0:T(8,128)(2,1)S(1)}, bf16[2,256,128]{2,1,0:T(8,128)(2,1)S(1)}, u32[]{:S(2)}, u32[]{:S(2)}) collective-permute-start(bf16[2,256,128]{2,1,0:T(8,128)(2,1)S(1)} %slice.228), channel_id=1, source_target_pairs={{0,2},{2,0},{1,3},{3,1},{4,6},{6,4},{5,7},{7,5},{8,10},{10,8},{9,1... | collective-permute-start | bytes 393224 | tf_op jit(solution)/shard_map/ppermute | solution.py:30
  115.5 2.9 %collective-permute-start.23 = (f32[2,2,256]{2,0,1:T(2,128)S(1)}, f32[2,2,256]{2,0,1:T(2,128)S(1)}, u32[]{:S(2)}, u32[]{:S(2)}) collective-permute-start(f32[2,2,256]{2,0,1:T(2,128)S(1)} %reshape.202), channel_id=1, source_target_pairs={{0,2},{2,0},{1,3},{3,1},{4,6},{6,4},{5,7},{7,5},{8,10},{10,8},{9,1... | collective-permute-start | bytes 12296 | tf_op jit(solution)/shard_map/ppermute | solution.py:30
  116.6 4.1 %collective-permute-start.24 = (bf16[2,256,128]{2,1,0:T(8,128)(2,1)S(1)}, bf16[2,256,128]{2,1,0:T(8,128)(2,1)S(1)}, u32[]{:S(2)}, u32[]{:S(2)}) collective-permute-start(bf16[2,256,128]{2,1,0:T(8,128)(2,1)S(1)} %slice.224), channel_id=1, source_target_pairs={{0,2},{2,0},{1,3},{3,1},{4,6},{6,4},{5,7},{7,5},{8,10},{10,8},{9,1... | collective-permute-start | bytes 393224 | tf_op jit(solution)/shard_map/ppermute | solution.py:30
  121.0 7.2 %collective-permute-start.26 = (bf16[2,256,128]{2,1,0:T(8,128)(2,1)S(1)}, bf16[2,256,128]{2,1,0:T(8,128)(2,1)S(1)}, u32[]{:S(2)}, u32[]{:S(2)}) collective-permute-start(bf16[2,256,128]{2,1,0:T(8,128)(2,1)S(1)} %get-tuple-element.74), channel_id=1, source_target_pairs={{0,1},{1,0},{2,3},{3,2},{4,5},{5,4},{6,7},{7,6},{8,9},{9,8},{10,11... | collective-permute-start | bytes 393224 | tf_op jit(solution)/shard_map/ppermute | solution.py:30
Sparse Core Ops, SparseCore 0:
  13.8 52.5 all-gather.1

commit v8 on v6

--- a/solution.py
+++ b/solution.py
@@ -393,7 +393,10 @@
     late = lax.axis_index("x_hi") == 1
     db_index = lax.axis_index(DB)
 
-    kv0, shard, row = lax.optimization_barrier((jnp.stack([k, v]), nb_shard, nb_row))
+    kv0 = jnp.stack([k, v])
+    qs = lax.ppermute(q, "x_hi", [(1, 0)])
+    kv1 = ring(kv0, "y", 1)
+    kv1, shard, row = lax.optimization_barrier((kv1, nb_shard, nb_row))
 
     place = 2 * lax.broadcasted_iota(jnp.int32, nb_shard.shape, 0) + lax.broadcasted_iota(
         jnp.int32, nb_shard.shape, 1
@@ -408,9 +411,7 @@
     )
     held_a = lax.all_gather(pair, "z", axis=0, tiled=True)
 
-    kv1 = ring(kv0, "y", 1)
     kv2 = ring(kv0, "y", -1)
-    qs = lax.ppermute(q, "x_hi", [(1, 0)])
     k3 = ring(kv1[0], "y", 1)
     v3 = ring(kv2[1], "y", -1)
     flags = jnp.stack([y < 0, y >= 1, y >= 3, y >= 2] + [~late] * 4).astype(jnp.int32)
@@ -452,10 +453,11 @@
     mine = lax.all_to_all(self_out.reshape(4, quarter, HD), XC, 0, 0)
     f1 = ring(mine, "z", 1)
     b1 = ring(mine, "z", -1)
-    f1, b1, held_a, wq4 = lax.optimization_barrier((f1, b1, held_a, wq4))
-    held_b = swap(held_a, "core")
+    f1, b1, wq4 = lax.optimization_barrier((f1, b1, wq4))
     f2 = ring(f1, "z", 1)
     b2 = ring(b1, "z", -1)
+    f2, b2, held_a = lax.optimization_barrier((f2, b2, held_a))
+    held_b = swap(held_a, "core")
     f3 = ring(f2, "z", 1)
     b3 = ring(b2, "z", -1)
     keys, values = project(info, held_a, held_b, ups)

time: 136 us -> 152 us (1.12)
  waiting for transfers between devices: 21.8 us -> 36.3 us
    ppermute x14, waiting for transfers between devices: 8.72 us -> 24.3 us  [ring(): return lax.ppermute(value, axis, [(i, (i + step) % n) for i in range(n)])]
    ppermute x1, waiting for transfers between devices: 6.92 us -> 5.12 us  [local(): lse_back = lax.ppermute(lse_sent, 'x_hi', [(0, 1)])]
    unnamed x21 -> x25, local copies, waits for them, and re-layouts: 5.77 us -> 5.07 us
  transfers between devices with their start and end apart: 28 -> 28, of which waited for: 11 -> 11; matrix products, arithmetic and copies ran while one was open for 8% -> 8% of each run, Pallas kernels for 18% -> 16%
where the time goes in v8:
time: 152 us; the launch traced here: 151 us
  starting transfers between devices  44.1 us (29%)
  waiting for transfers between devices  36.3 us (24%)
  Pallas kernels  24.7 us (16%)
  between operations  16 us (11%)
  local copies, waits for them, and re-layouts  12 us (8%)
  blocking collectives  7.5 us (5%)
  other arithmetic  6 us (4%)
  matrix products  4.67 us (3%)
    ppermute x14, waiting for transfers between devices, ring(): return lax.ppermute(value, axis, [(i, (i + step) % n) for i in range(n)])  24.3 us
    ppermute x14, starting transfers between devices, ring(): return lax.ppermute(value, axis, [(i, (i + step) % n) for i in range(n)])  19.5 us
    ppermute x10, starting transfers between devices, swap(): return lax.ppermute(value, axis, [(0, 1), (1, 0)])  18.3 us
    pallas_call x1, Pallas kernels, project(): pl.pallas_call(project_kernel, grid_spec=pltpu.PrefetchScalarGridSpec(num...  8.26 us
    all_to_all x1, blocking collectives, local(): mine = lax.all_to_all(self_out.reshape(4, quarter, HD), XC, 0, 0)  7.5 us
    ppermute x10, waiting for transfers between devices, swap(): return lax.ppermute(value, axis, [(0, 1), (1, 0)])  6.77 us
    pallas_call x1, Pallas kernels, attend_middle(): pl.pallas_call(middle_kernel, grid_spec=pltpu.PrefetchScalarGridSpec(num_...  5.77 us
    ppermute x1, waiting for transfers between devices, local(): lse_back = lax.ppermute(lse_sent, 'x_hi', [(0, 1)])  5.12 us
  transfers between devices with their start and end apart: 28, of which 11 were waited for; matrix products, arithmetic and copies ran while one was open for 8% of the time, Pallas kernels for 16%

profile of v8, /device:TPU:31, one launch (start us, length us, event | category | flops | bytes accessed | tf_op | source)
XLA Modules:
  0.0 151.2 jit_solution(17486930385463048592)
XLA Ops:
  7.2 1.1 pad_maximum_fusion.1.kv_ref.kv0
  8.5 12.8 %collective-permute-done.1.kv1 = bf16[2,1024,128]{2,1,0:T(8,128)(2,1)S(1)} collective-permute-done((bf16[2,1024,128]{2,1,0:T(8,128)(2,1)S(1)}, bf16[2,1024,128]{2,1,0:T(8,128)(2,1)S(1)}, u32[]{:S(2)}, u32[]{:S(2)}) %collective-permute-start.1) | collective-permute-done | bytes 524320 | tf_op jit(solution)/shard_map/ppermute | solution.py:26
  21.2 1.3 select_reduce_fusion.1
  23.8 1.1 constant_dynamic-slice_fusion.2
  26.4 3.7 %collective-permute-start = (bf16[1024,128]{1,0:T(8,128)(2,1)}, bf16[1024,128]{1,0:T(8,128)(2,1)}, u32[]{:S(2)}, u32[]{:S(2)}) collective-permute-start(bf16[1024,128]{1,0:T(8,128)(2,1)} %q_ref.5), channel_id=1, source_target_pairs={{128,0},{129,1},{130,2},{131,3},{132,4},{133,5},{134,6},{135,7},{1... | collective-permute-start | bytes 786440 | tf_op jit(solution)/shard_map/ppermute | solution.py:397
  30.1 1.1 pad_maximum_fusion.u0.w0
  31.3 1.2 slice.179.d0
  32.5 2.7 %collective-permute-start.8 = (bf16[2944,128]{1,0:T(8,128)(2,1)S(1)}, bf16[2944,128]{1,0:T(8,128)(2,1)}, u32[]{:S(2)}, u32[]{:S(2)}) collective-permute-start(bf16[2944,128]{1,0:T(8,128)(2,1)S(1)} %slice.179.d0), channel_id=1, source_target_pairs={{0,2},{2,128},{128,130},{130,0},{1,3},{3,129},{129,131},{131,1},{4... | collective-permute-start | bytes 2261000 | tf_op jit(solution)/shard_map/ppermute | solution.py:26
  35.3 0.9 copy-done.5
  36.3 1.3 attend_own.1
  37.6 2.3 %collective-permute-start.3 = (bf16[1024,128]{1,0:T(8,128)(2,1)S(1)}, bf16[1024,128]{1,0:T(8,128)(2,1)S(1)}, u32[]{:S(2)}, u32[]{:S(2)}) collective-permute-start(bf16[1024,128]{1,0:T(8,128)(2,1)S(1)} %slice_bitcast_fusion.1), channel_id=1, source_target_pairs={{0,32},{32,64},{64,96},{96,0},{1,33},{33,65},{65,97},{97,1},{2,34}... | collective-permute-start | bytes 786440 | tf_op jit(solution)/shard_map/ppermute | solution.py:26
  39.9 1.0 slice_bitcast_fusion
  41.0 5.8 %attend_middle.1 = (f32[2,1024,128]{2,1,0:T(8,128)S(1)}, f32[2,1024,256]{2,1,0:T(8,128)S(1)}) custom-call(s32[8]{0:T(128)S(1)} %convert_element_type.33.flags, bf16[1024,128]{1,0:T(8,128)(2,1)S(1)} %copy-done.6, bf16[1024,128]{1,0:T(8,128)(2,1)} %collective-permute-done.qs_ref, f32[1024,128]{1,0:T(8,128)S(1)} %get-tuple-element.35.m_in, ...), custom_call_target="tpu_custom_call" | custom-call | flops 8589934592 | bytes 6291456 | tf_op jit(solution)/shard_map/attend_middle/pallas_call | solution.py:135
  46.7 1.0 collective-permute-done.4.v3
  47.8 3.9 %attend_last.1 = (f32[1024,128]{1,0:T(8,128)S(1)}, bf16[1024,128]{1,0:T(8,128)(2,1)S(1)}, f32[2,4,1,256]{3,2,1,0:T(1,128)S(1)}) custom-call(s32[8]{0:T(128)S(1)} %convert_element_type.33.flags, bf16[1024,128]{1,0:T(8,128)(2,1)S(1)} %copy-done.6, bf16[1024,128]{1,0:T(8,128)(2,1)} %collective-permute-done.qs_ref, f32[2,1024,128]{2,1,0:T(8,128)S(1)} %get-tuple-element.38.m_in, ...), custom_call_target="tpu_custom_call" | custom-call | flops 3221225472 | bytes 6291456 | tf_op jit(solution)/shard_map/attend_last/pallas_call | solution.py:206
  51.7 1.3 collective-permute-start.5
  53.0 1.3 collective-permute-start.6
  54.3 3.8 %collective-permute-start.11 = (bf16[2944,128]{1,0:T(8,128)(2,1)S(1)}, bf16[2944,128]{1,0:T(8,128)(2,1)S(1)}, u32[]{:S(2)}, u32[]{:S(2)}) collective-permute-start(bf16[2944,128]{1,0:T(8,128)(2,1)S(1)} %pad_maximum_fusion.u0.w0), channel_id=1, source_target_pairs={{0,1},{1,0},{2,3},{3,2},{4,5},{5,4},{6,7},{7,6},{8,9},{9,8},{10,11... | collective-permute-start | bytes 2261000 | tf_op jit(solution)/shard_map/ppermute | solution.py:30
  58.2 5.1 %collective-permute-done.6 = f32[4,1,256]{2,1,0:T(1,128)S(1)} collective-permute-done((f32[4,1,256]{2,1,0:T(1,128)S(1)}, f32[4,1,256]{2,1,0:T(1,128)S(1)}, u32[]{:S(2)}, u32[]{:S(2)}) %collective-permute-start.6) | collective-permute-done | bytes 4128 | tf_op jit(solution)/shard_map/ppermute | solution.py:429
  63.3 3.0 %collective-permute-start.12 = (bf16[2944,128]{1,0:T(8,128)(2,1)S(1)}, bf16[2944,128]{1,0:T(8,128)(2,1)S(1)}, u32[]{:S(2)}, u32[]{:S(2)}) collective-permute-start(bf16[2944,128]{1,0:T(8,128)(2,1)S(1)} %collective-permute-done.7.u2.w2), channel_id=1, source_target_pairs={{0,1},{1,0},{2,3},{3,2},{4,5},{5,4},{6,7},{7,6},{8,9},{9,8},{10,11... | collective-permute-start | bytes 2261000 | tf_op jit(solution)/shard_map/ppermute | solution.py:30
  66.9 7.5 %all_to_all.5 = bf16[4,256,128]{2,1,0:T(8,128)(2,1)S(1)} all-to-all(bf16[4,256,128]{2,1,0:T(8,128)(2,1)S(1)} %bitcast.172), channel_id=1, replica_groups=mesh['x_hi'=2,'y'=4,'z'=8,'x_lo'=2,'core'=2] {'x_lo','core'}, dimensions={0} | all-to-all | bytes 524288 | tf_op jit(solution)/shard_map/all_to_all | solution.py:453
  74.4 5.5 %collective-permute-start.10 = (bf16[4,256,128]{2,1,0:T(8,128)(2,1)S(1)}, bf16[4,256,128]{2,1,0:T(8,128)(2,1)S(1)}, u32[]{:S(2)}, u32[]{:S(2)}) collective-permute-start(bf16[4,256,128]{2,1,0:T(8,128)(2,1)S(1)} %all_to_all.5), channel_id=1, source_target_pairs={{0,28},{4,0},{8,4},{12,8},{16,12},{20,16},{24,20},{28,24},{1,29},{... | collective-permute-start | bytes 786440 | tf_op jit(solution)/shard_map/ppermute | solution.py:26
  79.9 2.1 %side_by_side.1 = bf16[4096,512]{1,0:T(8,128)(2,1)S(1)} custom-call(bf16[2944,128]{1,0:T(8,128)(2,1)S(1)} %pad_maximum_fusion.u0.w0, bf16[2944,128]{1,0:T(8,128)(2,1)S(1)} %collective-permute-done.11.u1.w1, bf16[2944,128]{1,0:T(8,128)(2,1)S(1)} %collective-permute-done.7.u2.w2, bf16[2944,128]{1,0:T(8,128)(2,1)S(1)} %collective-permute-done.12.u3.w3, ...), custom_call_target="tpu_custom_call" | custom-call | flops 1048576 | bytes 10485760 | tf_op jit(solution)/shard_map/side_by_side/pallas_call | solution.py:248
  82.1 2.0 %copy-done = bf16[4096,512]{1,0:T(8,128)(2,1)} copy-done((bf16[4096,512]{1,0:T(8,128)(2,1)}, bf16[4096,512]{1,0:T(8,128)(2,1)S(1)}, u32[]{:S(2)}) %copy-start) | copy-done | bytes 4194328
  84.1 1.0 collective-permute-done.10
  85.1 3.1 %collective-permute-done.9 = bf16[4,256,128]{2,1,0:T(8,128)(2,1)S(1)} collective-permute-done((bf16[4,256,128]{2,1,0:T(8,128)(2,1)S(1)}, bf16[4,256,128]{2,1,0:T(8,128)(2,1)S(1)}, u32[]{:S(2)}, u32[]{:S(2)}) %collective-permute-start.9) | collective-permute-done | bytes 262176 | tf_op jit(solution)/shard_map/ppermute | solution.py:26
  88.2 2.7 %collective-permute-start.16 = (bf16[4,256,128]{2,1,0:T(8,128)(2,1)S(1)}, bf16[4,256,128]{2,1,0:T(8,128)(2,1)S(1)}, u32[]{:S(2)}, u32[]{:S(2)}) collective-permute-start(bf16[4,256,128]{2,1,0:T(8,128)(2,1)S(1)} %collective-permute-done.10), channel_id=1, source_target_pairs={{0,28},{4,0},{8,4},{12,8},{16,12},{20,16},{24,20},{28,24},{1,29},{... | collective-permute-start | bytes 786440 | tf_op jit(solution)/shard_map/ppermute | solution.py:26
  90.9 4.7 %collective-permute-done.15 = bf16[4,256,128]{2,1,0:T(8,128)(2,1)S(1)} collective-permute-done((bf16[4,256,128]{2,1,0:T(8,128)(2,1)S(1)}, bf16[4,256,128]{2,1,0:T(8,128)(2,1)S(1)}, u32[]{:S(2)}, u32[]{:S(2)}) %collective-permute-start.15) | collective-permute-done | bytes 262176 | tf_op jit(solution)/shard_map/ppermute | solution.py:26
  95.6 2.6 %collective-permute-start.19 = (bf16[16,128,896]{2,1,0:T(8,128)(2,1)}, bf16[16,128,896]{2,1,0:T(8,128)(2,1)}, u32[]{:S(2)}, u32[]{:S(2)}) collective-permute-start(bf16[16,128,896]{2,1,0:T(8,128)(2,1)} %all-gather.2.cloned.1.call-done.a_ref), channel_id=1, source_target_pairs={{0,1},{1,0},{2,3},{3,2},{4,5},{5,4},{6,7},{7,6},{8,9},{9,8},{10,11... | collective-permute-start | bytes 11010056 | tf_op jit(solution)/shard_map/ppermute | solution.py:30
  98.9 1.1 slice_bitcast_fusion.5
  100.0 1.5 fusion.8
  101.5 1.1 slice_bitcast_fusion.13
  102.6 1.3 convolution_add_fusion.5
  104.1 2.7 %collective-permute-start.18 = (bf16[4,256,128]{2,1,0:T(8,128)(2,1)S(1)}, bf16[4,256,128]{2,1,0:T(8,128)(2,1)S(1)}, u32[]{:S(2)}, u32[]{:S(2)}) collective-permute-start(bf16[4,256,128]{2,1,0:T(8,128)(2,1)S(1)} %collective-permute-done.16), channel_id=1, source_target_pairs={{0,28},{4,0},{8,4},{12,8},{16,12},{20,16},{24,20},{28,24},{1,29},{... | collective-permute-start | bytes 786440 | tf_op jit(solution)/shard_map/ppermute | solution.py:26
  107.1 2.0 %copy-done.4 = bf16[16,128,896]{2,1,0:T(8,128)(2,1)S(1)} copy-done((bf16[16,128,896]{2,1,0:T(8,128)(2,1)S(1)}, bf16[16,128,896]{2,1,0:T(8,128)(2,1)}, u32[]{:S(2)}) %copy-start.4) | copy-done | bytes 3670040
  109.2 8.3 %project.1 = (bf16[8,512,256]{2,1,0:T(8,128)(2,1)S(1)}, bf16[8,256,512]{2,1,0:T(8,128)(2,1)S(1)}) custom-call(s32[16]{0:T(128)S(1)} %add_bitcast_fusion.info, bf16[16,128,896]{2,1,0:T(8,128)(2,1)S(1)} %copy-done.4, bf16[16,128,896]{2,1,0:T(8,128)(2,1)} %collective-permute-done.19.b_ref, bf16[2944,128]{1,0:T(8,128)(2,1)S(1)} %pad_maximum_fusion.u0.w0, ...), custom_call_target="tpu_custom_call" | custom-call | flops 4294967296 | bytes 12582912 | tf_op jit(solution)/shard_map/project/pallas_call | solution.py:298
  117.6 2.7 %collective-permute-start.21 = (bf16[2,256,128]{2,1,0:T(8,128)(2,1)S(1)}, bf16[2,256,128]{2,1,0:T(8,128)(2,1)S(1)}, u32[]{:S(2)}, u32[]{:S(2)}) collective-permute-start(bf16[2,256,128]{2,1,0:T(8,128)(2,1)S(1)} %slice.182), channel_id=1, source_target_pairs={{0,28},{4,0},{8,4},{12,8},{16,12},{20,16},{24,20},{28,24},{1,29},{... | collective-permute-start | bytes 393224 | tf_op jit(solution)/shard_map/ppermute | solution.py:26
  121.6 1.7 %collective-permute-done.20 = bf16[2,256,128]{2,1,0:T(8,128)(2,1)S(1)} collective-permute-done((bf16[2,256,128]{2,1,0:T(8,128)(2,1)S(1)}, bf16[2,256,128]{2,1,0:T(8,128)(2,1)S(1)}, u32[]{:S(2)}, u32[]{:S(2)}) %collective-permute-start.20) | collective-permute-done | bytes 131104 | tf_op jit(solution)/shard_map/ppermute | solution.py:26
  123.7 1.0 collective-permute-start.22
  124.7 1.7 %cross.2 = (bf16[4,256,128]{2,1,0:T(8,128)(2,1)S(1)}, f32[4,8,64]{2,1,0:T(8,128)S(1)}) custom-call(s32[8]{0:T(128)S(1)} %bitcast.171, bf16[256,512]{1,0:T(8,128)(2,1)S(1)} %add_convert_fusion.q_ref, bf16[8,512,256]{2,1,0:T(8,128)(2,1)S(1)} %get-tuple-element.62.k_ref, bf16[8,256,512]{2,1,0:T(8,128)(2,1)S(1)} %get-tuple-element.63.v_ref), custom_call_target="tpu_custom_call" | custom-call | flops 2147483648 | bytes 3145728 | tf_op jit(solution)/shard_map/cross/pallas_call | solution.py:354
  126.4 0.9 collective-permute-start.25
  127.3 3.1 %collective-permute-done.22 = bf16[256,512]{1,0:T(8,128)(2,1)S(1)} collective-permute-done((bf16[256,512]{1,0:T(8,128)(2,1)S(1)}, bf16[256,512]{1,0:T(8,128)(2,1)S(1)}, u32[]{:S(2)}, u32[]{:S(2)}) %collective-permute-start.22) | collective-permute-done | bytes 262176 | tf_op jit(solution)/shard_map/ppermute | solution.py:30
  130.5 1.7 %cross.3 = (bf16[4,256,128]{2,1,0:T(8,128)(2,1)S(1)}, f32[4,8,64]{2,1,0:T(8,128)S(1)}) custom-call(s32[8]{0:T(128)S(1)} %bitcast.170, bf16[256,512]{1,0:T(8,128)(2,1)S(1)} %pad_maximum_fusion.3.q_ref, bf16[8,512,256]{2,1,0:T(8,128)(2,1)S(1)} %get-tuple-element.62.k_ref, bf16[8,256,512]{2,1,0:T(8,128)(2,1)S(1)} %get-tuple-element.63.v_ref), custom_call_target="tpu_custom_call" | custom-call | flops 2147483648 | bytes 3145728 | tf_op jit(solution)/shard_map/cross/pallas_call | solution.py:354
  133.1 0.9 collective-permute-start.24
  134.0 1.2 collective-permute-done.23
  135.5 1.5 %collective-permute-done.24 = bf16[2,256,128]{2,1,0:T(8,128)(2,1)S(1)} collective-permute-done((bf16[2,256,128]{2,1,0:T(8,128)(2,1)S(1)}, bf16[2,256,128]{2,1,0:T(8,128)(2,1)S(1)}, u32[]{:S(2)}, u32[]{:S(2)}) %collective-permute-start.24) | collective-permute-done | bytes 131104 | tf_op jit(solution)/shard_map/ppermute | solution.py:30
  137.3 5.3 %collective-permute-start.26 = (bf16[2,256,128]{2,1,0:T(8,128)(2,1)S(1)}, bf16[2,256,128]{2,1,0:T(8,128)(2,1)S(1)}, u32[]{:S(2)}, u32[]{:S(2)}) collective-permute-start(bf16[2,256,128]{2,1,0:T(8,128)(2,1)S(1)} %get-tuple-element.82), channel_id=1, source_target_pairs={{0,1},{1,0},{2,3},{3,2},{4,5},{5,4},{6,7},{7,6},{8,9},{9,8},{10,11... | collective-permute-start | bytes 393224 | tf_op jit(solution)/shard_map/ppermute | solution.py:30
  142.6 1.0 collective-permute-done.26
  (104 shorter events, 7.7 us)
Async XLA Ops:
  7.2 23.0 %slice-start = ((bf16[4096,128]{1,0:T(8,128)(2,1)}), bf16[1152,128]{1,0:T(8,128)(2,1)S(1)}, s32[]{:S(2)}) async-start(bf16[4096,128]{1,0:T(8,128)(2,1)} %param.17), calls=%async_computation.2 | async-start | bytes 589824 | tf_op jit(solution)/shard_map/slice | solution.py:422
  7.2 88.4 %all-gather.2.cloned.1.call-start = ((), (), s32[]{:S(2)}) async-start(), calls=%async_computation.1 | async-start | bytes 4128768 | tf_op jit(solution)/shard_map/all_gather | solution.py:412
  8.3 12.9 %collective-permute-start.1 = (bf16[2,1024,128]{2,1,0:T(8,128)(2,1)S(1)}, bf16[2,1024,128]{2,1,0:T(8,128)(2,1)S(1)}, u32[]{:S(2)}, u32[]{:S(2)}) collective-permute-start(bf16[2,1024,128]{2,1,0:T(8,128)(2,1)S(1)} %pad_maximum_fusion.1.kv_ref.kv0), channel_id=1, source_target_pairs={{0,32},{32,64},{64,96},{96,0},{1,33},{33,65},{65,97},{97,1},{2,34}... | collective-permute-start | bytes 1572872 | tf_op jit(solution)/shard_map/ppermute | solution.py:26
  25.8 14.0 %collective-permute-start.2 = (bf16[2,1024,128]{2,1,0:T(8,128)(2,1)S(1)}, bf16[2,1024,128]{2,1,0:T(8,128)(2,1)}, u32[]{:S(2)}, u32[]{:S(2)}) collective-permute-start(bf16[2,1024,128]{2,1,0:T(8,128)(2,1)S(1)} %pad_maximum_fusion.1.kv_ref.kv0), channel_id=1, source_target_pairs={{0,96},{32,0},{64,32},{96,64},{1,97},{33,1},{65,33},{97,65},{2,98}... | collective-permute-start | bytes 1572872 | tf_op jit(solution)/shard_map/ppermute | solution.py:26
  26.4 14.6 %collective-permute-start = (bf16[1024,128]{1,0:T(8,128)(2,1)}, bf16[1024,128]{1,0:T(8,128)(2,1)}, u32[]{:S(2)}, u32[]{:S(2)}) collective-permute-start(bf16[1024,128]{1,0:T(8,128)(2,1)} %q_ref.5), channel_id=1, source_target_pairs={{128,0},{129,1},{130,2},{131,3},{132,4},{133,5},{134,6},{135,7},{1... | collective-permute-start | bytes 786440 | tf_op jit(solution)/shard_map/ppermute | solution.py:397
  31.2 26.9 %collective-permute-start.7 = (bf16[2944,128]{1,0:T(8,128)(2,1)S(1)}, bf16[2944,128]{1,0:T(8,128)(2,1)S(1)}, u32[]{:S(2)}, u32[]{:S(2)}) collective-permute-start(bf16[2944,128]{1,0:T(8,128)(2,1)S(1)} %pad_maximum_fusion.u0.w0), channel_id=1, source_target_pairs={{0,130},{2,0},{128,2},{130,128},{1,131},{3,1},{129,3},{131,129},{4... | collective-permute-start | bytes 2261000 | tf_op jit(solution)/shard_map/ppermute | solution.py:26
  32.5 25.7 %collective-permute-start.8 = (bf16[2944,128]{1,0:T(8,128)(2,1)S(1)}, bf16[2944,128]{1,0:T(8,128)(2,1)}, u32[]{:S(2)}, u32[]{:S(2)}) collective-permute-start(bf16[2944,128]{1,0:T(8,128)(2,1)S(1)} %slice.179.d0), channel_id=1, source_target_pairs={{0,2},{2,128},{128,130},{130,0},{1,3},{3,129},{129,131},{131,1},{4... | collective-permute-start | bytes 2261000 | tf_op jit(solution)/shard_map/ppermute | solution.py:26
  35.3 1.0 copy-start.5
  36.3 4.7 %copy-start.6 = (bf16[1024,128]{1,0:T(8,128)(2,1)S(1)}, bf16[1024,128]{1,0:T(8,128)(2,1)}, u32[]{:S(2)}) copy-start(bf16[1024,128]{1,0:T(8,128)(2,1)} %q_ref.5) | copy-start | bytes 786436
  37.6 9.2 %collective-permute-start.3 = (bf16[1024,128]{1,0:T(8,128)(2,1)S(1)}, bf16[1024,128]{1,0:T(8,128)(2,1)S(1)}, u32[]{:S(2)}, u32[]{:S(2)}) collective-permute-start(bf16[1024,128]{1,0:T(8,128)(2,1)S(1)} %slice_bitcast_fusion.1), channel_id=1, source_target_pairs={{0,32},{32,64},{64,96},{96,0},{1,33},{33,65},{65,97},{97,1},{2,34}... | collective-permute-start | bytes 786440 | tf_op jit(solution)/shard_map/ppermute | solution.py:26
  40.8 6.9 %collective-permute-start.4 = (bf16[1024,128]{1,0:T(8,128)(2,1)S(1)}, bf16[1024,128]{1,0:T(8,128)(2,1)S(1)}, u32[]{:S(2)}, u32[]{:S(2)}) collective-permute-start(bf16[1024,128]{1,0:T(8,128)(2,1)S(1)} %slice_bitcast_fusion), channel_id=1, source_target_pairs={{0,96},{32,0},{64,32},{96,64},{1,97},{33,1},{65,33},{97,65},{2,98}... | collective-permute-start | bytes 786440 | tf_op jit(solution)/shard_map/ppermute | solution.py:26
  51.7 11.6 %collective-permute-start.5 = (bf16[1024,128]{1,0:T(8,128)(2,1)S(1)}, bf16[1024,128]{1,0:T(8,128)(2,1)S(1)}, u32[]{:S(2)}, u32[]{:S(2)}) collective-permute-start(bf16[1024,128]{1,0:T(8,128)(2,1)S(1)} %get-tuple-element.42), channel_id=1, source_target_pairs={{0,128},{1,129},{2,130},{3,131},{4,132},{5,133},{6,134},{7,135},{8... | collective-permute-start | bytes 786440 | tf_op jit(solution)/shard_map/ppermute | solution.py:428
  53.0 10.3 %collective-permute-start.6 = (f32[4,1,256]{2,1,0:T(1,128)S(1)}, f32[4,1,256]{2,1,0:T(1,128)S(1)}, u32[]{:S(2)}, u32[]{:S(2)}) collective-permute-start(f32[4,1,256]{2,1,0:T(1,128)S(1)} %get-tuple-element.120), channel_id=1, source_target_pairs={{0,128},{1,129},{2,130},{3,131},{4,132},{5,133},{6,134},{7,135},{8... | collective-permute-start | bytes 12296 | tf_op jit(solution)/shard_map/ppermute | solution.py:429
  54.3 25.6 %collective-permute-start.11 = (bf16[2944,128]{1,0:T(8,128)(2,1)S(1)}, bf16[2944,128]{1,0:T(8,128)(2,1)S(1)}, u32[]{:S(2)}, u32[]{:S(2)}) collective-permute-start(bf16[2944,128]{1,0:T(8,128)(2,1)S(1)} %pad_maximum_fusion.u0.w0), channel_id=1, source_target_pairs={{0,1},{1,0},{2,3},{3,2},{4,5},{5,4},{6,7},{7,6},{8,9},{9,8},{10,11... | collective-permute-start | bytes 2261000 | tf_op jit(solution)/shard_map/ppermute | solution.py:30
  58.1 21.8 %collective-permute-start.13 = (bf16[2944,128]{1,0:T(8,128)(2,1)S(1)}, bf16[2944,128]{1,0:T(8,128)(2,1)S(1)}, u32[]{:S(2)}, u32[]{:S(2)}) collective-permute-start(bf16[2944,128]{1,0:T(8,128)(2,1)S(1)} %slice.179.d0), channel_id=1, source_target_pairs={{0,1},{1,0},{2,3},{3,2},{4,5},{5,4},{6,7},{7,6},{8,9},{9,8},{10,11... | collective-permute-start | bytes 2261000 | tf_op jit(solution)/shard_map/ppermute | solution.py:30
  63.3 16.6 %collective-permute-start.12 = (bf16[2944,128]{1,0:T(8,128)(2,1)S(1)}, bf16[2944,128]{1,0:T(8,128)(2,1)S(1)}, u32[]{:S(2)}, u32[]{:S(2)}) collective-permute-start(bf16[2944,128]{1,0:T(8,128)(2,1)S(1)} %collective-permute-done.7.u2.w2), channel_id=1, source_target_pairs={{0,1},{1,0},{2,3},{3,2},{4,5},{5,4},{6,7},{7,6},{8,9},{9,8},{10,11... | collective-permute-start | bytes 2261000 | tf_op jit(solution)/shard_map/ppermute | solution.py:30
  66.4 13.6 %collective-permute-start.14 = (bf16[2944,128]{1,0:T(8,128)(2,1)}, bf16[2944,128]{1,0:T(8,128)(2,1)S(1)}, u32[]{:S(2)}, u32[]{:S(2)}) collective-permute-start(bf16[2944,128]{1,0:T(8,128)(2,1)} %collective-permute-done.8.d2), channel_id=1, source_target_pairs={{0,1},{1,0},{2,3},{3,2},{4,5},{5,4},{6,7},{7,6},{8,9},{9,8},{10,11... | collective-permute-start | bytes 2261000 | tf_op jit(solution)/shard_map/ppermute | solution.py:30
  66.9 15.2 %copy-start.8 = (bf16[1024,128]{1,0:T(8,128)(2,1)}, bf16[1024,128]{1,0:T(8,128)(2,1)S(1)}, u32[]{:S(2)}) copy-start(bf16[1024,128]{1,0:T(8,128)(2,1)S(1)} %divide_convert_fusion) | copy-start | bytes 786436
  74.4 7.7 %copy-start.7 = (bf16[4,256,128]{2,1,0:T(8,128)(2,1)}, bf16[4,256,128]{2,1,0:T(8,128)(2,1)S(1)}, u32[]{:S(2)}) copy-start(bf16[4,256,128]{2,1,0:T(8,128)(2,1)S(1)} %all_to_all.5) | copy-start | bytes 786436
  74.4 23.9 %copy-start.11 = (s32[16,2]{0,1:T(2,128)S(1)}, s32[16,2]{0,1:T(2,128)}, u32[]{:S(2)}) copy-start(s32[16,2]{0,1:T(2,128)} %param.13) | copy-start | bytes 388
  74.4 10.7 %collective-permute-start.10 = (bf16[4,256,128]{2,1,0:T(8,128)(2,1)S(1)}, bf16[4,256,128]{2,1,0:T(8,128)(2,1)S(1)}, u32[]{:S(2)}, u32[]{:S(2)}) collective-permute-start(bf16[4,256,128]{2,1,0:T(8,128)(2,1)S(1)} %all_to_all.5), channel_id=1, source_target_pairs={{0,28},{4,0},{8,4},{12,8},{16,12},{20,16},{24,20},{28,24},{1,29},{... | collective-permute-start | bytes 786440 | tf_op jit(solution)/shard_map/ppermute | solution.py:26
  79.9 8.3 %collective-permute-start.9 = (bf16[4,256,128]{2,1,0:T(8,128)(2,1)S(1)}, bf16[4,256,128]{2,1,0:T(8,128)(2,1)S(1)}, u32[]{:S(2)}, u32[]{:S(2)}) collective-permute-start(bf16[4,256,128]{2,1,0:T(8,128)(2,1)S(1)} %all_to_all.5), channel_id=1, source_target_pairs={{0,4},{4,8},{8,12},{12,16},{16,20},{20,24},{24,28},{28,0},{1,5},{5... | collective-permute-start | bytes 786440 | tf_op jit(solution)/shard_map/ppermute | solution.py:26
  79.9 2.2 %copy-start.2 = (bf16[2944,128]{1,0:T(8,128)(2,1)}, bf16[2944,128]{1,0:T(8,128)(2,1)S(1)}, u32[]{:S(2)}) copy-start(bf16[2944,128]{1,0:T(8,128)(2,1)S(1)} %collective-permute-done.12.u3.w3) | copy-start | bytes 2260996
  82.1 2.0 %copy-start = (bf16[4096,512]{1,0:T(8,128)(2,1)}, bf16[4096,512]{1,0:T(8,128)(2,1)S(1)}, u32[]{:S(2)}) copy-start(bf16[4096,512]{1,0:T(8,128)(2,1)S(1)} %side_by_side.1) | copy-start | bytes 12582916
  85.1 10.5 %copy-start.9 = (bf16[4,256,128]{2,1,0:T(8,128)(2,1)}, bf16[4,256,128]{2,1,0:T(8,128)(2,1)S(1)}, u32[]{:S(2)}) copy-start(bf16[4,256,128]{2,1,0:T(8,128)(2,1)S(1)} %collective-permute-done.10) | copy-start | bytes 786436
  85.1 22.0 %copy-start.3 = (bf16[2944,128]{1,0:T(8,128)(2,1)S(1)}, bf16[2944,128]{1,0:T(8,128)(2,1)}, u32[]{:S(2)}) copy-start(bf16[2944,128]{1,0:T(8,128)(2,1)} %copy-done.2) | copy-start | bytes 2260996
  88.2 7.4 %copy-start.10 = (bf16[4,256,128]{2,1,0:T(8,128)(2,1)}, bf16[4,256,128]{2,1,0:T(8,128)(2,1)S(1)}, u32[]{:S(2)}) copy-start(bf16[4,256,128]{2,1,0:T(8,128)(2,1)S(1)} %collective-permute-done.9) | copy-start | bytes 786436
  88.2 7.4 %collective-permute-start.15 = (bf16[4,256,128]{2,1,0:T(8,128)(2,1)S(1)}, bf16[4,256,128]{2,1,0:T(8,128)(2,1)S(1)}, u32[]{:S(2)}, u32[]{:S(2)}) collective-permute-start(bf16[4,256,128]{2,1,0:T(8,128)(2,1)S(1)} %collective-permute-done.9), channel_id=1, source_target_pairs={{0,4},{4,8},{8,12},{12,16},{16,20},{20,24},{24,28},{28,0},{1,5},{5... | collective-permute-start | bytes 786440 | tf_op jit(solution)/shard_map/ppermute | solution.py:26
  88.2 7.4 %collective-permute-start.16 = (bf16[4,256,128]{2,1,0:T(8,128)(2,1)S(1)}, bf16[4,256,128]{2,1,0:T(8,128)(2,1)S(1)}, u32[]{:S(2)}, u32[]{:S(2)}) collective-permute-start(bf16[4,256,128]{2,1,0:T(8,128)(2,1)S(1)} %collective-permute-done.10), channel_id=1, source_target_pairs={{0,28},{4,0},{8,4},{12,8},{16,12},{20,16},{24,20},{28,24},{1,29},{... | collective-permute-start | bytes 786440 | tf_op jit(solution)/shard_map/ppermute | solution.py:26
  95.6 11.5 %collective-permute-start.19 = (bf16[16,128,896]{2,1,0:T(8,128)(2,1)}, bf16[16,128,896]{2,1,0:T(8,128)(2,1)}, u32[]{:S(2)}, u32[]{:S(2)}) collective-permute-start(bf16[16,128,896]{2,1,0:T(8,128)(2,1)} %all-gather.2.cloned.1.call-done.a_ref), channel_id=1, source_target_pairs={{0,1},{1,0},{2,3},{3,2},{4,5},{5,4},{6,7},{7,6},{8,9},{9,8},{10,11... | collective-permute-start | bytes 11010056 | tf_op jit(solution)/shard_map/ppermute | solution.py:30
  98.8 8.0 %copy-start.1 = (bf16[4096,512]{1,0:T(8,128)(2,1)S(1)}, bf16[4096,512]{1,0:T(8,128)(2,1)}, u32[]{:S(2)}) copy-start(bf16[4096,512]{1,0:T(8,128)(2,1)} %copy-done) | copy-start | bytes 12582916
  104.0 13.4 %collective-permute-start.17 = (bf16[4,256,128]{2,1,0:T(8,128)(2,1)S(1)}, bf16[4,256,128]{2,1,0:T(8,128)(2,1)S(1)}, u32[]{:S(2)}, u32[]{:S(2)}) collective-permute-start(bf16[4,256,128]{2,1,0:T(8,128)(2,1)S(1)} %collective-permute-done.15), channel_id=1, source_target_pairs={{0,4},{4,8},{8,12},{12,16},{16,20},{20,24},{24,28},{28,0},{1,5},{5... | collective-permute-start | bytes 786440 | tf_op jit(solution)/shard_map/ppermute | solution.py:26
  104.1 13.4 %collective-permute-start.18 = (bf16[4,256,128]{2,1,0:T(8,128)(2,1)S(1)}, bf16[4,256,128]{2,1,0:T(8,128)(2,1)S(1)}, u32[]{:S(2)}, u32[]{:S(2)}) collective-permute-start(bf16[4,256,128]{2,1,0:T(8,128)(2,1)S(1)} %collective-permute-done.16), channel_id=1, source_target_pairs={{0,28},{4,0},{8,4},{12,8},{16,12},{20,16},{24,20},{28,24},{1,29},{... | collective-permute-start | bytes 786440 | tf_op jit(solution)/shard_map/ppermute | solution.py:26
  107.1 2.0 %copy-start.4 = (bf16[16,128,896]{2,1,0:T(8,128)(2,1)S(1)}, bf16[16,128,896]{2,1,0:T(8,128)(2,1)}, u32[]{:S(2)}) copy-start(bf16[16,128,896]{2,1,0:T(8,128)(2,1)} %all-gather.2.cloned.1.call-done.a_ref) | copy-start | bytes 11010052
  117.5 5.8 %collective-permute-start.20 = (bf16[2,256,128]{2,1,0:T(8,128)(2,1)S(1)}, bf16[2,256,128]{2,1,0:T(8,128)(2,1)S(1)}, u32[]{:S(2)}, u32[]{:S(2)}) collective-permute-start(bf16[2,256,128]{2,1,0:T(8,128)(2,1)S(1)} %slice.181), channel_id=1, source_target_pairs={{0,4},{4,8},{8,12},{12,16},{16,20},{20,24},{24,28},{28,0},{1,5},{5... | collective-permute-start | bytes 393224 | tf_op jit(solution)/shard_map/ppermute | solution.py:26
  117.6 5.7 %collective-permute-start.21 = (bf16[2,256,128]{2,1,0:T(8,128)(2,1)S(1)}, bf16[2,256,128]{2,1,0:T(8,128)(2,1)S(1)}, u32[]{:S(2)}, u32[]{:S(2)}) collective-permute-start(bf16[2,256,128]{2,1,0:T(8,128)(2,1)S(1)} %slice.182), channel_id=1, source_target_pairs={{0,28},{4,0},{8,4},{12,8},{16,12},{20,16},{24,20},{28,24},{1,29},{... | collective-permute-start | bytes 393224 | tf_op jit(solution)/shard_map/ppermute | solution.py:26
  123.7 6.7 %collective-permute-start.22 = (bf16[256,512]{1,0:T(8,128)(2,1)S(1)}, bf16[256,512]{1,0:T(8,128)(2,1)S(1)}, u32[]{:S(2)}, u32[]{:S(2)}) collective-permute-start(bf16[256,512]{1,0:T(8,128)(2,1)S(1)} %add_convert_fusion.q_ref), channel_id=1, source_target_pairs={{0,2},{2,0},{1,3},{3,1},{4,6},{6,4},{5,7},{7,5},{8,10},{10,8},{9,1... | collective-permute-start | bytes 786440 | tf_op jit(solution)/shard_map/ppermute | solution.py:30
  126.4 8.8 %collective-permute-start.25 = (bf16[2,256,128]{2,1,0:T(8,128)(2,1)S(1)}, bf16[2,256,128]{2,1,0:T(8,128)(2,1)S(1)}, u32[]{:S(2)}, u32[]{:S(2)}) collective-permute-start(bf16[2,256,128]{2,1,0:T(8,128)(2,1)S(1)} %slice.228), channel_id=1, source_target_pairs={{0,2},{2,0},{1,3},{3,1},{4,6},{6,4},{5,7},{7,5},{8,10},{10,8},{9,1... | collective-permute-start | bytes 393224 | tf_op jit(solution)/shard_map/ppermute | solution.py:30
  132.3 2.9 %collective-permute-start.23 = (f32[2,2,256]{2,0,1:T(2,128)S(1)}, f32[2,2,256]{2,0,1:T(2,128)S(1)}, u32[]{:S(2)}, u32[]{:S(2)}) collective-permute-start(f32[2,2,256]{2,0,1:T(2,128)S(1)} %reshape.202), channel_id=1, source_target_pairs={{0,2},{2,0},{1,3},{3,1},{4,6},{6,4},{5,7},{7,5},{8,10},{10,8},{9,1... | collective-permute-start | bytes 12296 | tf_op jit(solution)/shard_map/ppermute | solution.py:30
  133.1 3.9 %collective-permute-start.24 = (bf16[2,256,128]{2,1,0:T(8,128)(2,1)S(1)}, bf16[2,256,128]{2,1,0:T(8,128)(2,1)S(1)}, u32[]{:S(2)}, u32[]{:S(2)}) collective-permute-start(bf16[2,256,128]{2,1,0:T(8,128)(2,1)S(1)} %slice.224), channel_id=1, source_target_pairs={{0,2},{2,0},{1,3},{3,1},{4,6},{6,4},{5,7},{7,5},{8,10},{10,8},{9,1... | collective-permute-start | bytes 393224 | tf_op jit(solution)/shard_map/ppermute | solution.py:30
  137.3 6.3 %collective-permute-start.26 = (bf16[2,256,128]{2,1,0:T(8,128)(2,1)S(1)}, bf16[2,256,128]{2,1,0:T(8,128)(2,1)S(1)}, u32[]{:S(2)}, u32[]{:S(2)}) collective-permute-start(bf16[2,256,128]{2,1,0:T(8,128)(2,1)S(1)} %get-tuple-element.82), channel_id=1, source_target_pairs={{0,1},{1,0},{2,3},{3,2},{4,5},{5,4},{6,7},{7,6},{8,9},{9,8},{10,11... | collective-permute-start | bytes 393224 | tf_op jit(solution)/shard_map/ppermute | solution.py:30
Sparse Core Ops, SparseCore 0:
  26.0 53.3 all-gather.1
